TPU v7x, 32 devices: a whole 2x2x4 slice. The times are simulated.
32 devices in a mesh: sub: 2 (over core), brick: 16 (over z, y, x).
Axes of the slice: x: 2, y: 2, z: 4, core: 2. Of those that a mesh axis runs over, the one named last changes fastest.
Arguments:
- increments: float32 [4, 128, 256, 512], P('sub', None, 'brick'), may hold values from -6 to 6
- courant_x: float32 [4, 128, 256, 512], P('sub', None, 'brick'), may hold values from -0.5 to 0.5
- courant_y: float32 [4, 128, 256, 512], P('sub', None, 'brick'), may hold values from -0.5 to 0.5
- spectrum: float32 [256, 512], replicated, may hold values from 0.05 to 2
- vertical: float32 [128, 128], replicated, may hold values from -0.5 to 0.5
Outputs:
- covaried: float32 [4, 128, 256, 512], P('sub', None, 'brick')
All inputs are finite; a program needn't handle non-finite values.
Results may differ from a plain program's by a relative error of at most 0.00007.
Values sent between devices are 32-bit elements; how exact they have to be, the bound alone decides.
No kernel may reach another device: no remote copies, remote signals or barrier semaphores. Data moves between devices by JAX's collectives and lax.ppermute only.
A program may use at most 192 MiB of HBM per device.

v0:
```python
import jax
import jax.numpy as jnp
from jax import lax
from jax.sharding import PartitionSpec as P

STEPS = 4


diffusion = 0.2


def extended_2(value, sides, width):
    for axis, dim in sides:
        count, length = (lax.axis_size(axis), value.shape[dim])
        up = [(i, (i + 1) % count) for i in range(count - 1)]
        down = [(j, i) for i, j in up]
        last = lax.slice_in_dim(value, length - width, length, axis=dim)
        initial = lax.slice_in_dim(value, 0, width, axis=dim)
        before = lax.ppermute(last, axis, up)
        after = lax.ppermute(initial, axis, down)
        value = jnp.concatenate([before, value, after], axis=dim)
    return value


def shifted(value, axis, by):
    count = lax.axis_size(axis)
    pairs = [(i, i + by) for i in range(count) if 0 <= i + by < count]
    return lax.ppermute(value, axis, pairs)


def dct_table(count):
    freq = jnp.arange(count, dtype=jnp.float32)[:, None]
    cells = jnp.arange(count, dtype=jnp.float32)[None, :]
    table = jnp.cos(jnp.pi * (cells + 0.5) * freq / count) * jnp.sqrt(jnp.float32(2.0) / count)
    first = jnp.where(jnp.arange(count)[:, None] == 0, jnp.sqrt(jnp.float32(0.5)), jnp.float32(1.0))
    return table * first


def advance(extended, courant_x, courant_y):
    center = extended[..., 1:-1, :]
    north = extended[..., 2:, :]
    south = extended[..., :-2, :]
    widths = [(0, 0)] * (center.ndim - 1) + [(1, 1)]
    padded = jnp.pad(center, widths)
    east = padded[..., 2:]
    west = padded[..., :-2]
    return (
        center
        - 0.5 * courant_x * (north - south)
        - 0.5 * courant_y * (east - west)
        + diffusion * (north + south + east + west - 4.0 * center)
    )


def on_device(increments, courant_x, courant_y, spectrum, vertical):
    high = lax.Precision.HIGHEST
    rows = increments.shape[2]
    total_rows = rows * lax.axis_size("brick")
    state = increments
    for number in range(STEPS):
        extended = extended_2(state, (("brick", 2),), 1)
        state = advance(extended, courant_x, courant_y)
    prior = shifted(state[-1], "sub", 1)
    previous = jnp.concatenate([prior[None], state[:-1]], axis=0)
    jumps = increments - previous
    row_table = dct_table(total_rows)
    col_table = dct_table(increments.shape[3])
    forward_y = jnp.einsum("slxy,jy->sljx", jumps, col_table, precision=high)
    block = lax.all_to_all(forward_y, "brick", split_axis=2, concat_axis=3, tiled=True)
    width = block.shape[2]
    own = lax.dynamic_slice_in_dim(spectrum, lax.axis_index("brick") * width, width, 1)
    forward = jnp.einsum("kx,sljx->sljk", row_table, block, precision=high)
    scaled = forward * own.T
    back = jnp.einsum("kx,sljk->sljx", row_table, scaled, precision=high)
    partial_value = lax.all_to_all(back, "brick", split_axis=3, concat_axis=2, tiled=True)
    horizontal = jnp.einsum("sljx,jy->slxy", partial_value, col_table, precision=high)
    return jnp.einsum("ml,slxy->smxy", vertical, horizontal, precision=high)


def solution(mesh):
    in_specs = (
        P("sub", None, "brick", None),
        P("sub", None, "brick", None),
        P("sub", None, "brick", None),
        P(),
        P(),
    )
    out_specs = P("sub", None, "brick", None)
    return jax.shard_map(
        on_device, mesh=mesh, in_specs=in_specs, out_specs=out_specs, check_vma=False
    )
```

profile of v0, /device:TPU:0, one launch (start us, length us, event | category | flops | bytes accessed | tf_op | source)
XLA Modules:
  0.0 743.4 jit_solution(17310429168226254493)
XLA Ops:
  0.0 0.0 copy-start
  0.0 0.0 copy-start.1
  0.0 0.0 copy-start.2
  0.0 11.8 %copy.43 = f32[2,128,16,512]{3,1,2,0:T(8,128)} copy(f32[2,128,16,512]{3,2,1,0:T(8,128)} %param.5) | data formatting | bytes 16777216 | tf_op args[0]
  11.8 1.3 fusion.37
  13.1 1.3 collective-permute-start
  14.4 5.5 collective-permute-start.1
  19.9 10.8 %collective-permute-done = f32[2,128,1,512]{3,1,2,0:T(8,128)S(1)} collective-permute-done((f32[2,128,1,512]{3,1,2,0:T(8,128)S(1)}, f32[2,128,1,512]{3,1,2,0:T(8,128)S(1)}, u32[]{:S(2)}, u32[]{:S(2)}) %collective-permute-start) | collective-permute-done | bytes 524320 | tf_op jit(solution)/shard_map/ppermute | solution.py:20
  30.7 11.5 %collective-permute-done.1 = f32[2,128,1,512]{3,1,2,0:T(8,128)S(1)} collective-permute-done((f32[2,128,1,512]{3,1,2,0:T(8,128)S(1)}, f32[2,128,1,512]{3,1,2,0:T(8,128)S(1)}, u32[]{:S(2)}, u32[]{:S(2)}) %collective-permute-start.1) | collective-permute-done | bytes 524320 | tf_op jit(solution)/shard_map/ppermute | solution.py:19
  42.2 0.0 copy-done.1
  42.2 0.0 copy-done.2
  42.2 21.9 %multiply_add_fusion.3 = f32[2,128,16,512]{3,1,2,0:T(8,128)} fusion(f32[2,128,16,512]{3,1,2,0:T(8,128)} %copy.43, f32[2,128,1,512]{3,1,2,0:T(8,128)S(1)} %collective-permute-done, f32[2,128,1,512]{3,1,2,0:T(8,128)S(1)} %collective-permute-done.1, f32[2,128,16,512]{3,2,1,0:T(8,128)S(1)} %copy-done.1, f32[2,128,16,512]{3,2,1,0:T(8,128)S(1)} %copy-done.2), kind=kLoop, calls=%fused_computation.29 | loop fusion | flops 35651584 | bytes 34603008 | tf_op jit(solution)/shard_map/add | solution.py:48
  64.2 1.3 fusion.36
  65.4 1.3 collective-permute-start.2
  66.7 5.5 collective-permute-start.3
  72.2 10.3 %collective-permute-done.2 = f32[2,128,1,512]{3,1,2,0:T(8,128)S(1)} collective-permute-done((f32[2,128,1,512]{3,1,2,0:T(8,128)S(1)}, f32[2,128,1,512]{3,1,2,0:T(8,128)S(1)}, u32[]{:S(2)}, u32[]{:S(2)}) %collective-permute-start.2) | collective-permute-done | bytes 524320 | tf_op jit(solution)/shard_map/ppermute | solution.py:20
  82.6 8.7 %collective-permute-done.3 = f32[2,128,1,512]{3,1,2,0:T(8,128)S(1)} collective-permute-done((f32[2,128,1,512]{3,1,2,0:T(8,128)S(1)}, f32[2,128,1,512]{3,1,2,0:T(8,128)S(1)}, u32[]{:S(2)}, u32[]{:S(2)}) %collective-permute-start.3) | collective-permute-done | bytes 524320 | tf_op jit(solution)/shard_map/ppermute | solution.py:19
  91.3 21.9 %multiply_add_fusion.2 = f32[2,128,16,512]{3,1,2,0:T(8,128)} fusion(f32[2,128,16,512]{3,1,2,0:T(8,128)} %multiply_add_fusion.3, f32[2,128,1,512]{3,1,2,0:T(8,128)S(1)} %collective-permute-done.2, f32[2,128,1,512]{3,1,2,0:T(8,128)S(1)} %collective-permute-done.3, f32[2,128,16,512]{3,2,1,0:T(8,128)S(1)} %copy-done.1, f32[2,128,16,512]{3,2,1,0:T(8,128)S(1)} %copy-done.2), kind=kLoop, calls=%fused_computation.28 | loop fusion | flops 35651584 | bytes 34603008 | tf_op jit(solution)/shard_map/add | solution.py:48
  113.2 1.3 fusion.35
  114.5 1.3 collective-permute-start.4
  115.8 5.0 collective-permute-start.5
  120.8 10.8 %collective-permute-done.4 = f32[2,128,1,512]{3,1,2,0:T(8,128)S(1)} collective-permute-done((f32[2,128,1,512]{3,1,2,0:T(8,128)S(1)}, f32[2,128,1,512]{3,1,2,0:T(8,128)S(1)}, u32[]{:S(2)}, u32[]{:S(2)}) %collective-permute-start.4) | collective-permute-done | bytes 524320 | tf_op jit(solution)/shard_map/ppermute | solution.py:20
  131.6 11.8 %collective-permute-done.5 = f32[2,128,1,512]{3,1,2,0:T(8,128)S(1)} collective-permute-done((f32[2,128,1,512]{3,1,2,0:T(8,128)S(1)}, f32[2,128,1,512]{3,1,2,0:T(8,128)S(1)}, u32[]{:S(2)}, u32[]{:S(2)}) %collective-permute-start.5) | collective-permute-done | bytes 524320 | tf_op jit(solution)/shard_map/ppermute | solution.py:19
  143.4 21.9 %multiply_add_fusion.1 = f32[2,128,16,512]{3,1,2,0:T(8,128)} fusion(f32[2,128,16,512]{3,1,2,0:T(8,128)} %multiply_add_fusion.2, f32[2,128,1,512]{3,1,2,0:T(8,128)S(1)} %collective-permute-done.4, f32[2,128,1,512]{3,1,2,0:T(8,128)S(1)} %collective-permute-done.5, f32[2,128,16,512]{3,2,1,0:T(8,128)S(1)} %copy-done.1, f32[2,128,16,512]{3,2,1,0:T(8,128)S(1)} %copy-done.2), kind=kLoop, calls=%fused_computation.27 | loop fusion | flops 35651584 | bytes 34603008 | tf_op jit(solution)/shard_map/add | solution.py:48
  165.3 1.3 fusion.34
  166.6 1.3 collective-permute-start.6
  167.9 5.0 collective-permute-start.7
  172.9 10.8 %collective-permute-done.6 = f32[2,128,1,512]{3,1,2,0:T(8,128)S(1)} collective-permute-done((f32[2,128,1,512]{3,1,2,0:T(8,128)S(1)}, f32[2,128,1,512]{3,1,2,0:T(8,128)S(1)}, u32[]{:S(2)}, u32[]{:S(2)}) %collective-permute-start.6) | collective-permute-done | bytes 524320 | tf_op jit(solution)/shard_map/ppermute | solution.py:20
  183.7 8.8 %collective-permute-done.7 = f32[2,128,1,512]{3,1,2,0:T(8,128)S(1)} collective-permute-done((f32[2,128,1,512]{3,1,2,0:T(8,128)S(1)}, f32[2,128,1,512]{3,1,2,0:T(8,128)S(1)}, u32[]{:S(2)}, u32[]{:S(2)}) %collective-permute-start.7) | collective-permute-done | bytes 524320 | tf_op jit(solution)/shard_map/ppermute | solution.py:19
  192.6 21.9 %multiply_add_fusion = f32[2,128,16,512]{3,1,2,0:T(8,128)} fusion(f32[2,128,16,512]{3,1,2,0:T(8,128)} %multiply_add_fusion.1, f32[2,128,1,512]{3,1,2,0:T(8,128)S(1)} %collective-permute-done.6, f32[2,128,1,512]{3,1,2,0:T(8,128)S(1)} %collective-permute-done.7, f32[2,128,16,512]{3,2,1,0:T(8,128)S(1)} %copy-done.1, f32[2,128,16,512]{3,2,1,0:T(8,128)S(1)} %copy-done.2), kind=kLoop, calls=%fused_computation.26 | loop fusion | flops 35651584 | bytes 34603008 | tf_op jit(solution)/shard_map/add | solution.py:48
  214.4 4.5 slice_bitcast_fusion
  218.9 2.2 collective-permute-start.8
  221.1 6.5 collective-permute-done.8
  227.6 30.0 %fusion.8 = f32[2,128,512,16]{1,2,3,0:T(8,128)S(1)} fusion(f32[1,128,16,512]{3,1,2,0:T(8,128)S(1)} %get-tuple-element.6, f32[1,128,16,512]{3,1,2,0:T(8,128)S(1)} %bitcast.41, f32[512]{0:T(512)S(1)} %get-tuple-element.15, f32[512]{0:T(512)S(1)} %get-tuple-element.16, f32[2,128,16,512]{3,2,1,0:T(8,128)} %param.5), kind=kOutput, calls=%fused_computation.33 | convolution fusion | flops 12889882624 | bytes 25169920 | tf_op jit(solution)/shard_map/slxy,jy->sljx/dot_general | solution.py:68
  257.6 8.3 %copy.44 = f32[2,128,512,16]{1,3,0,2:T(8,128)} copy(f32[2,128,512,16]{1,2,3,0:T(8,128)S(1)} %fusion.8) | data formatting | bytes 16777216 | tf_op jit(solution)/shard_map/slxy,jy->sljx/transpose | solution.py:68
  265.9 7.3 all-to-all-start
  273.2 0.0 copy-done
  273.2 0.1 dynamic-slice_bitcast_fusion
  273.3 0.1 copy.48
  273.4 159.1 %all-to-all-done = f32[2,128,512,16]{1,3,0,2:T(8,128)} async-done(((f32[2,128,512,16]{1,3,0,2:T(8,128)}), f32[2,128,512,16]{1,3,0,2:T(8,128)}, u32[]{:S(2)}, u32[]{:S(2)}) %all-to-all-start) | async-done | bytes 8388640 | tf_op jit(solution)/shard_map/all_to_all | solution.py:69
  432.5 4.4 copy.46
  436.9 15.0 %fusion.18 = f32[2,128,32,256]{3,1,2,0:T(8,128)S(1)} fusion(f32[2,128,32,256]{1,3,2,0:T(8,128)S(1)} %bitcast.39, f32[256]{0:T(256)S(1)} %get-tuple-element.17, f32[256]{0:T(256)S(1)} %get-tuple-element.18), kind=kOutput, calls=%fused_computation.44 | convolution fusion | flops 6442647552 | bytes 16779264 | tf_op jit(solution)/shard_map/kx,sljx->sljk/dot_general | solution.py:72
  451.9 10.8 %fusion.5 = f32[2,128,32,256]{3,1,2,0:T(8,128)} fusion(f32[2,128,32,256]{3,1,2,0:T(8,128)S(1)} %fusion.18, f32[32,256]{1,0:T(8,128)S(1)} %copy.48, f32[256]{0:T(256)S(1)} %get-tuple-element.17, f32[256]{0:T(256)S(1)} %get-tuple-element.18), kind=kOutput, calls=%fused_computation.24 | convolution fusion | flops 6444744704 | bytes 16812032 | tf_op jit(solution)/shard_map/kx,sljk->sljx/dot_general | solution.py:74
  462.7 10.3 %copy.49 = f32[2,128,32,256]{1,2,0,3:T(8,128)} copy(f32[2,128,32,256]{3,1,2,0:T(8,128)} %fusion.5) | data formatting | bytes 16777216 | tf_op jit(solution)/shard_map/kx,sljk->sljx/dot_general | solution.py:74
  473.0 221.1 %all_to_all.36 = f32[2,128,32,256]{1,2,0,3:T(8,128)S(1)} all-to-all(f32[2,128,32,256]{1,2,0,3:T(8,128)} %copy.49), channel_id=1, replica_groups=mesh['sub'=2,'brick'=16] {'brick'}, dimensions={3} | all-to-all | bytes 16777216 | tf_op jit(solution)/shard_map/all_to_all | solution.py:75
  694.0 7.6 %copy.51 = f32[2,128,16,32,16]{1,4,3,2,0:T(8,128)S(1)} copy(f32[2,128,16,32,16]{1,3,0,4,2:T(8,128)S(1)} %bitcast.40) | data formatting | bytes 16777216 | tf_op jit(solution)/shard_map/all_to_all | solution.py:75
  701.6 0.0 copy-start.3
  701.6 22.5 %fusion.3 = f32[2,128,16,512]{1,3,2,0:T(8,128)S(1)} fusion(f32[2,128,512,16]{1,3,2,0:T(8,128)S(1)} %bitcast.38, f32[512]{0:T(512)S(1)} %get-tuple-element.15, f32[512]{0:T(512)S(1)} %get-tuple-element.16), kind=kOutput, calls=%fused_computation.20 | convolution fusion | flops 12885688320 | bytes 16781312 | tf_op jit(solution)/shard_map/sljx,jy->slxy/dot_general | solution.py:76
  724.1 0.0 copy-done.3
  724.1 8.8 %convolution_bitcast_fusion = f32[2,128,16,512]{1,3,2,0:T(8,128)} fusion(f32[2,128,16,512]{1,3,2,0:T(8,128)S(1)} %fusion.3, f32[128,128]{1,0:T(8,128)S(1)} %copy-done.3), kind=kOutput, calls=%fused_computation.32 | convolution fusion | flops 3221225472 | bytes 16842752 | tf_op jit(solution)/shard_map/ml,slxy->smxy/dot_general | solution.py:77
  733.0 10.3 %copy.54 = f32[2,128,16,512]{3,2,1,0:T(8,128)} copy(f32[2,128,16,512]{1,3,2,0:T(8,128)} %convolution_bitcast_fusion) | data formatting | bytes 16777216 | tf_op jit(solution)/shard_map/ml,slxy->smxy/transpose | solution.py:77
  (2 shorter events, 0.0 us)
Async XLA Ops:
  0.0 273.2 %copy-start = (f32[256,512]{1,0:T(8,128)S(1)}, f32[256,512]{1,0:T(8,128)}, u32[]{:S(2)}) copy-start(f32[256,512]{1,0:T(8,128)} %param.8) | copy-start | bytes 1572868
  0.0 42.2 %copy-start.1 = (f32[2,128,16,512]{3,2,1,0:T(8,128)S(1)}, f32[2,128,16,512]{3,2,1,0:T(8,128)}, u32[]{:S(2)}) copy-start(f32[2,128,16,512]{3,2,1,0:T(8,128)} %param.6) | copy-start | bytes 25165828
  0.0 42.2 %copy-start.2 = (f32[2,128,16,512]{3,2,1,0:T(8,128)S(1)}, f32[2,128,16,512]{3,2,1,0:T(8,128)}, u32[]{:S(2)}) copy-start(f32[2,128,16,512]{3,2,1,0:T(8,128)} %param.7) | copy-start | bytes 25165828
  13.1 17.6 %collective-permute-start = (f32[2,128,1,512]{3,1,2,0:T(8,128)S(1)}, f32[2,128,1,512]{3,1,2,0:T(8,128)S(1)}, u32[]{:S(2)}, u32[]{:S(2)}) collective-permute-start(f32[2,128,1,512]{3,1,2,0:T(8,128)S(1)} %get-tuple-element.14), channel_id=1, source_target_pairs={{1,0},{2,1},{3,2},{4,3},{5,4},{6,5},{7,6},{8,7},{9,8},{10,9},{11,1... | collective-permute-start | bytes 1572872 | tf_op jit(solution)/shard_map/ppermute | solution.py:20
  14.4 27.8 %collective-permute-start.1 = (f32[2,128,1,512]{3,1,2,0:T(8,128)S(1)}, f32[2,128,1,512]{3,1,2,0:T(8,128)S(1)}, u32[]{:S(2)}, u32[]{:S(2)}) collective-permute-start(f32[2,128,1,512]{3,1,2,0:T(8,128)S(1)} %get-tuple-element.13), channel_id=1, source_target_pairs={{0,1},{1,2},{2,3},{3,4},{4,5},{5,6},{6,7},{7,8},{8,9},{9,10},{10,1... | collective-permute-start | bytes 1572872 | tf_op jit(solution)/shard_map/ppermute | solution.py:19
  65.4 17.2 %collective-permute-start.2 = (f32[2,128,1,512]{3,1,2,0:T(8,128)S(1)}, f32[2,128,1,512]{3,1,2,0:T(8,128)S(1)}, u32[]{:S(2)}, u32[]{:S(2)}) collective-permute-start(f32[2,128,1,512]{3,1,2,0:T(8,128)S(1)} %get-tuple-element.12), channel_id=1, source_target_pairs={{1,0},{2,1},{3,2},{4,3},{5,4},{6,5},{7,6},{8,7},{9,8},{10,9},{11,1... | collective-permute-start | bytes 1572872 | tf_op jit(solution)/shard_map/ppermute | solution.py:20
  66.7 24.6 %collective-permute-start.3 = (f32[2,128,1,512]{3,1,2,0:T(8,128)S(1)}, f32[2,128,1,512]{3,1,2,0:T(8,128)S(1)}, u32[]{:S(2)}, u32[]{:S(2)}) collective-permute-start(f32[2,128,1,512]{3,1,2,0:T(8,128)S(1)} %get-tuple-element.11), channel_id=1, source_target_pairs={{0,1},{1,2},{2,3},{3,4},{4,5},{5,6},{6,7},{7,8},{8,9},{9,10},{10,1... | collective-permute-start | bytes 1572872 | tf_op jit(solution)/shard_map/ppermute | solution.py:19
  114.5 17.2 %collective-permute-start.4 = (f32[2,128,1,512]{3,1,2,0:T(8,128)S(1)}, f32[2,128,1,512]{3,1,2,0:T(8,128)S(1)}, u32[]{:S(2)}, u32[]{:S(2)}) collective-permute-start(f32[2,128,1,512]{3,1,2,0:T(8,128)S(1)} %get-tuple-element.10), channel_id=1, source_target_pairs={{1,0},{2,1},{3,2},{4,3},{5,4},{6,5},{7,6},{8,7},{9,8},{10,9},{11,1... | collective-permute-start | bytes 1572872 | tf_op jit(solution)/shard_map/ppermute | solution.py:20
  115.8 27.6 %collective-permute-start.5 = (f32[2,128,1,512]{3,1,2,0:T(8,128)S(1)}, f32[2,128,1,512]{3,1,2,0:T(8,128)S(1)}, u32[]{:S(2)}, u32[]{:S(2)}) collective-permute-start(f32[2,128,1,512]{3,1,2,0:T(8,128)S(1)} %get-tuple-element.9), channel_id=1, source_target_pairs={{0,1},{1,2},{2,3},{3,4},{4,5},{5,6},{6,7},{7,8},{8,9},{9,10},{10,1... | collective-permute-start | bytes 1572872 | tf_op jit(solution)/shard_map/ppermute | solution.py:19
  166.6 17.2 %collective-permute-start.6 = (f32[2,128,1,512]{3,1,2,0:T(8,128)S(1)}, f32[2,128,1,512]{3,1,2,0:T(8,128)S(1)}, u32[]{:S(2)}, u32[]{:S(2)}) collective-permute-start(f32[2,128,1,512]{3,1,2,0:T(8,128)S(1)} %get-tuple-element.8), channel_id=1, source_target_pairs={{1,0},{2,1},{3,2},{4,3},{5,4},{6,5},{7,6},{8,7},{9,8},{10,9},{11,1... | collective-permute-start | bytes 1572872 | tf_op jit(solution)/shard_map/ppermute | solution.py:20
  167.9 24.7 %collective-permute-start.7 = (f32[2,128,1,512]{3,1,2,0:T(8,128)S(1)}, f32[2,128,1,512]{3,1,2,0:T(8,128)S(1)}, u32[]{:S(2)}, u32[]{:S(2)}) collective-permute-start(f32[2,128,1,512]{3,1,2,0:T(8,128)S(1)} %get-tuple-element.7), channel_id=1, source_target_pairs={{0,1},{1,2},{2,3},{3,4},{4,5},{5,6},{6,7},{7,8},{8,9},{9,10},{10,1... | collective-permute-start | bytes 1572872 | tf_op jit(solution)/shard_map/ppermute | solution.py:19
  218.9 8.7 %collective-permute-start.8 = (f32[128,16,512]{2,0,1:T(8,128)S(1)}, f32[128,16,512]{2,0,1:T(8,128)S(1)}, u32[]{:S(2)}, u32[]{:S(2)}) collective-permute-start(f32[128,16,512]{2,0,1:T(8,128)S(1)} %get-tuple-element.5), channel_id=1, source_target_pairs={{0,16},{1,17},{2,18},{3,19},{4,20},{5,21},{6,22},{7,23},{8,24},{9,... | collective-permute-start | bytes 12582920 | tf_op jit(solution)/shard_map/ppermute | solution.py:28
  265.9 166.6 %all-to-all-start = ((f32[2,128,512,16]{1,3,0,2:T(8,128)}), f32[2,128,512,16]{1,3,0,2:T(8,128)}, u32[]{:S(2)}, u32[]{:S(2)}) async-start(f32[2,128,512,16]{1,3,0,2:T(8,128)} %copy.44), calls=%async_computation | async-start | bytes 16777216 | tf_op jit(solution)/shard_map/all_to_all | solution.py:69
  701.6 22.5 %copy-start.3 = (f32[128,128]{1,0:T(8,128)S(1)}, f32[128,128]{1,0:T(8,128)}, u32[]{:S(2)}) copy-start(f32[128,128]{1,0:T(8,128)} %param.9) | copy-start | bytes 196612
where the time goes:
time: 751 us; the launch traced here: 743 us
  waiting for transfers between devices  249 us (33%)
  blocking collectives  221 us (29%)
  other arithmetic  87.7 us (12%)
  matrix products  87.2 us (12%)
  local copies, waits for them, and re-layouts  62.2 us (8%)
  starting transfers between devices  35.8 us (5%)
    all_to_all x1, blocking collectives, on_device(): lax.all_to_all(back, 'brick', split_axis=3, concat_axis=2, tiled=True)  221 us
    all_to_all x1, waiting for transfers between devices, on_device(): lax.all_to_all(forward_y, 'brick', split_axis=2, concat_axis=3, tiled=True)  159 us
    add x4, other arithmetic, advance(): center - 0.5 * courant_x * (north - south) - 0.5 * courant_y * (east - west)  87.6 us
    ppermute x4, waiting for transfers between devices, extended_2(): after = lax.ppermute(initial, axis, down)  42.7 us
    ppermute x4, waiting for transfers between devices, extended_2(): before = lax.ppermute(last, axis, up)  40.8 us
    dot_general x1, matrix products, on_device(): forward_y = jnp.einsum('slxy,jy->sljx', jumps, col_table, precision=high)  30 us
    dot_general x1, matrix products, on_device(): jnp.einsum('sljx,jy->slxy', partial_value, col_table, precision=high)  22.5 us
    ppermute x4, starting transfers between devices, extended_2(): before = lax.ppermute(last, axis, up)  21.1 us
  transfers between devices with their start and end apart: 10, of which 10 were waited for; matrix products, arithmetic and copies ran while one was open for 0% of the time, Pallas kernels for 0%

commit v1 on v0

v1 whole, which is shorter than its diff:
```python
import functools

import jax
import jax.numpy as jnp
from jax import lax
from jax.experimental import pallas as pl
from jax.experimental.pallas import tpu as pltpu
from jax.sharding import PartitionSpec as P

STEPS = 4
LANES = 128
DIFFUSION = 0.2
CUTS_LAST = (4, 8)
CUTS_FIRST = (8,)


def dct_table(count):
    freq = jnp.arange(count, dtype=jnp.float32)[:, None]
    cells = jnp.arange(count, dtype=jnp.float32)[None, :]
    table = jnp.cos(jnp.pi * (cells + 0.5) * freq / count) * jnp.sqrt(jnp.float32(2.0) / count)
    first = jnp.where(jnp.arange(count)[:, None] == 0, jnp.sqrt(jnp.float32(0.5)), jnp.float32(1.0))
    return table * first


def halves(table):
    high = lax.reduce_precision(table, 8, 7)
    return high.astype(jnp.bfloat16), (table - high).astype(jnp.bfloat16)


def split(value):
    high = value.astype(jnp.bfloat16)
    return high, (value - high.astype(jnp.float32)).astype(jnp.bfloat16)


def dot3(left, right):
    dot = functools.partial(jnp.dot, preferred_element_type=jnp.float32)
    return dot(left[0], right[0]) + (dot(left[0], right[1]) + dot(left[1], right[0]))


def stepped(center, north, south, half_x, half_y):
    cols = center.shape[1]
    lane = lax.broadcasted_iota(jnp.int32, center.shape, 1)
    east = jnp.where(lane == cols - 1, 0.0, pltpu.roll(center, cols - 1, 1))
    west = jnp.where(lane == 0, 0.0, pltpu.roll(center, 1, 1))
    total = (north + south) + (east + west) + center
    return DIFFUSION * total - half_x * (north - south) - half_y * (east - west)


def tangent_kernel(rows, parts, first, last, *refs):
    refs = list(refs)

    def take(count):
        taken = refs[:count]
        del refs[:count]
        return taken

    (inside,) = take(1)
    state = take(parts) if first else take(1)[0]
    cx, cy = take(parts), take(parts)
    before, after = take(2)
    far_before, far_after = (before, after) if first else take(2)
    target = take(parts) if last == "jump" else None
    (out,) = take(1)
    old, mid, hx, hy, flat = refs
    at = lambda i: slice(i * LANES, (i + 1) * LANES)

    def gather(pieces, x):
        return jnp.concatenate([p[pl.ds(x, 8, stride=rows), :] for p in pieces], axis=1)

    for x in range(rows):
        old[x + 2] = gather(state, x) if first else state[x]
        hx[x + 1] = 0.5 * gather(cx, x)
        hy[x + 1] = 0.5 * gather(cy, x)
    for h in range(2):
        old[h] = before[h]
        old[rows + 2 + h] = after[h]
    hx[0], hy[0] = 0.5 * far_before[2], 0.5 * far_before[3]
    hx[rows + 1], hy[rows + 1] = 0.5 * far_after[2], 0.5 * far_after[3]
    for x in range(rows + 2):
        new = stepped(old[x + 1], old[x + 2], old[x], hx[x], hy[x])
        if x == 0:
            new = new * inside[0]
        if x == rows + 1:
            new = new * inside[1]
        mid[x] = new
    for x in range(rows):
        new = stepped(mid[x + 1], mid[x + 2], mid[x], hx[x + 1], hy[x + 1])
        if not last:
            out[x] = new
        else:
            for i in range(parts):
                flat[i, pl.ds(x, 8, stride=rows), :] = new[:, at(i)]
    if last:
        for i in range(parts):
            out[:, at(i)] = target[i][...] - flat[i] if target else flat[i]


def mid_kernel(block_ref, spectrum_ref, rh, rl, rth, rtl, ch, cl, cth, ctl, out_ref):
    count, _, rows, cols = block_ref.shape
    field = block_ref[...].reshape(count * rows, cols)
    along_y = dot3(split(field), (cth[...], ctl[...]))
    full = dot3((rh[...], rl[...]), split(along_y)) * spectrum_ref[...]
    back = dot3((rth[...], rtl[...]), split(full))
    out_ref[...] = dot3(split(back), (ch[...], cl[...])).reshape(count, 1, rows, cols)


def mix_kernel(rows, field_ref, vh_ref, vl_ref, *refs):
    out_ref = refs[-1]
    levels = vh_ref.shape[1]
    factor = (vh_ref[...], vl_ref[...])
    for x in range(rows):
        field = field_ref[pl.ds(x, levels, stride=rows), :]
        out_ref[pl.ds(x, levels, stride=rows), :] = dot3(factor, split(field))


def params(**more):
    return pltpu.CompilerParams(vmem_limit_bytes=56 << 20, **more)


def on_device(increments, courant_x, courant_y, spectrum, vertical):
    subs, levels, rows, cols = increments.shape
    bricks, groups = lax.axis_size("brick"), lax.axis_size("sub")
    brick = lax.axis_index("brick")
    f32 = jnp.float32

    def neighbour(value, by, part_of_end):
        pairs = []
        for g in range(groups - 1 if part_of_end else groups):
            pairs += [(g * bricks + i, g * bricks + i + by) for i in range(bricks) if 0 <= i + by < bricks]
        return lax.ppermute(value, ("sub", "brick"), pairs)

    def next_sub(value):
        return lax.ppermute(value, "sub", [(i, i + 1) for i in range(groups - 1)])

    row_table, col_table = dct_table(rows * bricks), dct_table(cols)
    tables = (*halves(row_table), *halves(row_table.T), *halves(col_table), *halves(col_table.T))

    def cost(values, passes):
        return pl.CostEstimate(flops=20 * values * passes, bytes_accessed=16 * values * passes, transcendentals=0)

    def chunk_of(cuts):
        ends = [max(1, round(c * (levels // bricks) / 8)) * bricks for c in cuts]
        return [(a, b) for a, b in zip([0] + ends[:-1], ends) if b > a]

    parts = cols // LANES
    flat_all = [a.reshape(-1, cols) for a in (increments, courant_x, courant_y)]
    inside = jnp.stack([jnp.where(brick > 0, 1.0, 0.0), jnp.where(brick < bricks - 1, 1.0, 0.0)]).astype(f32)

    def pieces(array, sub, start):
        specs = [
            pl.BlockSpec((8 * rows, LANES), lambda i, j=j: ((sub * levels + start) // 8 + i, j)) for j in range(parts)
        ]
        return [array] * parts, specs

    def first_halo(sub, start, stop):
        inc, cx, cy = (a[sub, start:stop] for a in (increments, courant_x, courant_y))
        last = sub == subs - 1
        low = jnp.stack([inc[:, rows - 2], inc[:, rows - 1], cx[:, rows - 1], cy[:, rows - 1]])
        high = jnp.stack([inc[:, 0], inc[:, 1], cx[:, 0], cy[:, 0]])
        return neighbour(low, 1, last), neighbour(high, -1, last)

    def tangent(number, sub, start, stop, state, halo, far, target):
        span = stop - start
        first = number == 0
        last = None if first else ("end" if target is None else "jump")
        slab = pl.BlockSpec((rows, 8, cols), lambda i: (0, i, 0))
        inputs, specs = [inside], [pl.BlockSpec(memory_space=pltpu.SMEM)]

        def add(more, with_specs):
            inputs.extend(more)
            specs.extend(with_specs)

        if first:
            add(*pieces(flat_all[0], sub, start))
        else:
            add([state], [slab])
        add(*pieces(flat_all[1], sub, start))
        add(*pieces(flat_all[2], sub, start))
        for pair in (halo,) if first else (halo, far):
            add(pair, [pl.BlockSpec((pair[0].shape[0], 8, cols), lambda i: (0, i, 0))] * 2)
        if last == "jump":
            add(*pieces(flat_all[0], target, start))
        if first:
            out, out_spec = (rows, span, cols), slab
        else:
            out, out_spec = (span * rows, cols), pl.BlockSpec((8 * rows, cols), lambda i: (i, 0))
        return pl.pallas_call(
            functools.partial(tangent_kernel, rows, parts, first, last),
            grid=(span // 8,),
            in_specs=specs,
            out_specs=out_spec,
            out_shape=jax.ShapeDtypeStruct(out, f32),
            scratch_shapes=[
                pltpu.VMEM((rows + 4, 8, cols), f32),
                pltpu.VMEM((rows + 2, 8, cols), f32),
                pltpu.VMEM((rows + 2, 8, cols), f32),
                pltpu.VMEM((rows + 2, 8, cols), f32),
                pltpu.VMEM((parts, 8 * rows, LANES), f32),
            ],
            compiler_params=params(),
            cost_estimate=cost(span * rows * cols, 2),
            name="tangent",
        )(*inputs)

    def advance(sub, target, start, stop):
        far = first_halo(sub, start, stop)
        state = tangent(0, sub, start, stop, None, far, far, None)
        last = sub == subs - 1
        halo = neighbour(state[rows - 2 :], 1, last), neighbour(state[:2], -1, last)
        return tangent(1, sub, start, stop, state, halo, far, target).reshape(stop - start, rows, cols)

    def spread(value):
        return lax.all_to_all(value, "brick", split_axis=0, concat_axis=0, tiled=True)

    def middle(block, done, offset, total):
        share = block.shape[0] // bricks
        block = block.reshape(bricks, share, rows, cols)
        fixed = [pl.BlockSpec(t.shape, lambda i: (0, 0), pipeline_mode=pl.Buffered(1)) for t in (spectrum, *tables)]
        piece = pl.BlockSpec((bricks, 1, rows, cols), lambda i: (0, i, 0, 0))
        flops = 12 * share * bricks * rows * cols * (cols + bricks * rows)
        inputs = [block, spectrum, *tables]
        specs = [piece] + fixed
        kernel, alias = mid_kernel, {}
        if done is not None:
            alias = {len(inputs): 0}
            inputs.append(done)
            specs.append(pl.BlockSpec(memory_space=pl.ANY))
            kernel = lambda *refs: mid_kernel(*refs[:-2], refs[-1])
        return pl.pallas_call(
            kernel,
            grid=(share,),
            in_specs=specs,
            out_specs=pl.BlockSpec((bricks, 1, rows, cols), lambda i: (0, i + offset, 0, 0)),
            out_shape=jax.ShapeDtypeStruct((bricks, total, rows, cols), f32),
            input_output_aliases=alias,
            compiler_params=params(),
            cost_estimate=pl.CostEstimate(flops=flops, bytes_accessed=8 * block.size, transcendentals=0),
            name="middle",
        )(*inputs)

    def mix(field, sub, factor, old):
        field = field.reshape(levels * rows, cols)
        inputs = [field, *factor]
        whole = pl.BlockSpec((levels, levels), lambda i: (0, 0))
        specs = [pl.BlockSpec((levels * rows, LANES), lambda i: (0, i)), whole, whole]
        kernel, alias = functools.partial(mix_kernel, rows), {}
        if old is not None:
            inputs.append(old)
            specs.append(pl.BlockSpec(memory_space=pl.ANY))
            alias = {3: 0}
        return pl.pallas_call(
            kernel,
            grid=(parts,),
            in_specs=specs,
            out_specs=pl.BlockSpec((levels * rows, LANES), lambda i: (sub, i)),
            out_shape=jax.ShapeDtypeStruct((subs * levels * rows, cols), f32),
            input_output_aliases=alias,
            compiler_params=params(),
            cost_estimate=pl.CostEstimate(
                flops=6 * levels * levels * rows * cols, bytes_accessed=8 * levels * rows * cols, transcendentals=0
            ),
            name="mix",
        )(*inputs)

    out = None
    work = []
    for target in range(subs - 1, 0, -1):
        cuts = chunk_of(CUTS_LAST if target == subs - 1 else CUTS_FIRST)
        work.append((target, [(a, b, advance(target - 1, target, a, b)) for a, b in cuts]))
    ends = [(a, b, advance(subs - 1, None, a, b)) for a, b in chunk_of(CUTS_FIRST)]
    work.append((0, [(a, b, increments[0, a:b] - next_sub(e)) for a, b, e in ends]))
    received = [(sub, [(a, b, spread(jump)) for a, b, jump in group]) for sub, group in work]
    returned = []
    for sub, group in received:
        done, offset, columns = None, 0, []
        for a, b, block in group:
            share = (b - a) // bricks
            done = middle(block, done, offset, levels // bricks)
            offset += share
            columns.append(vertical[:, a:b].reshape(levels, bricks, share))
        factor = jnp.concatenate(columns, axis=2).reshape(levels, levels)
        returned.append((sub, halves(factor), spread(done)))
    for sub, factor, part in returned:
        out = mix(part, sub, factor, out)
    return out.reshape(increments.shape)


def solution(mesh):
    spec = P("sub", None, "brick", None)
    return jax.shard_map(
        on_device, mesh=mesh, in_specs=(spec, spec, spec, P(), P()), out_specs=spec, check_vma=False
    )
```

time: 751 us -> 570 us (0.76)
  blocking collectives: 221 us -> 0 us
  Pallas kernels: 0 us -> 116 us
  matrix products: 87.2 us -> 0 us
  starting transfers between devices: 35.8 us -> 117 us
  other arithmetic: 87.7 us -> 21.7 us
  local copies, waits for them, and re-layouts: 62.2 us -> 41.9 us
  waiting for transfers between devices: 249 us -> 262 us
    all_to_all x1 -> x0, blocking collectives: 221 us -> none  [on_device(): lax.all_to_all(back, 'brick', split_axis=3, concat_axis=2, tiled=True)]
    pallas_call x0 -> x11, Pallas kernels: none -> 116 us  [the longest x6 66.1 us: tangent(): pl.pallas_call(functools.partial(tangent_kernel, rows, parts, first, last...]
    add x4 -> x0, other arithmetic: 87.6 us -> none  [advance(): center - 0.5 * courant_x * (north - south) - 0.5 * courant_y * (east - west)]
    dot_general x5 -> x0, matrix products: 87.2 us -> none  [the longest x1 30 us: on_device(): forward_y = jnp.einsum('slxy,jy->sljx', jumps, col_table, precision=high)]
    all_to_all x1 -> x5, starting transfers between devices: 7.29 us -> 78.8 us  [spread(): lax.all_to_all(value, 'brick', split_axis=0, concat_axis=0, tiled=True)]
    transpose x4 -> x0, local copies, waits for them, and re-layouts: 18.7 us -> none  [the longest x1 10.3 us: on_device(): return jnp.einsum('ml,slxy->smxy', vertical, horizontal, precision=high)]
    all_to_all x1 -> x5, waiting for transfers between devices: 159 us -> 174 us  [spread(): lax.all_to_all(value, 'brick', split_axis=0, concat_axis=0, tiled=True)]
    convert_element_type x0 -> x4, other arithmetic: none -> 12.2 us  [halves(): return (high.astype(jnp.bfloat16), (table - high).astype(jnp.bfloat16))]
  transfers between devices with their start and end apart: 10 -> 18, of which waited for: 10 -> 14; matrix products, arithmetic and copies ran while one was open for 0% -> 7% of each run, Pallas kernels for 0% -> 17%
where the time goes in v1:
time: 570 us; the launch traced here: 559 us
  waiting for transfers between devices  262 us (46%)
  starting transfers between devices  117 us (21%)
  Pallas kernels  116 us (20%)
  local copies, waits for them, and re-layouts  41.9 us (7%)
  other arithmetic  21.7 us (4%)
    all_to_all x5, waiting for transfers between devices, spread(): lax.all_to_all(value, 'brick', split_axis=0, concat_axis=0, tiled=True)  174 us
    ppermute x12, waiting for transfers between devices, neighbour(): return lax.ppermute(value, ('sub', 'brick'), pairs)  87.5 us
    all_to_all x5, starting transfers between devices, spread(): lax.all_to_all(value, 'brick', split_axis=0, concat_axis=0, tiled=True)  78.8 us
    pallas_call x6, Pallas kernels, tangent(): pl.pallas_call(functools.partial(tangent_kernel, rows, parts, first, last...  66.1 us
    pallas_call x3, Pallas kernels, middle(): pl.pallas_call(kernel, grid=(share,), in_specs=specs, out_specs=pl.BlockS...  37.3 us
    ppermute x12, starting transfers between devices, neighbour(): return lax.ppermute(value, ('sub', 'brick'), pairs)  34.9 us
    unnamed x45, local copies, waits for them, and re-layouts  15.2 us
    pallas_call x2, Pallas kernels, mix(): pl.pallas_call(kernel, grid=(parts,), in_specs=specs, out_specs=pl.BlockS...  12.9 us
  transfers between devices with their start and end apart: 18, of which 14 were waited for; matrix products, arithmetic and copies ran while one was open for 7% of the time, Pallas kernels for 17%

profile of v1, /device:TPU:0, one launch (start us, length us, event | category | flops | bytes accessed | tf_op | source)
XLA Modules:
  0.0 559.3 jit_solution(13218649004649522853)
XLA Ops:
  0.0 2.8 fusion.8
  2.9 3.7 copy_bitcast_fusion.4
  7.5 3.8 copy_bitcast_fusion.3
  12.2 2.4 copy_bitcast_fusion.5
  14.7 0.8 pad_maximum_fusion.4
  15.5 4.9 collective-permute-start.9
  20.4 0.9 pad_maximum_fusion.5
  21.3 1.3 collective-permute-start.10
  23.2 19.9 %collective-permute-done.9.refs_13_.refs_12_ = f32[4,64,512]{2,1,0:T(8,128)S(1)} collective-permute-done((f32[4,64,512]{2,1,0:T(8,128)}, f32[4,64,512]{2,1,0:T(8,128)S(1)}, u32[]{:S(2)}, u32[]{:S(2)}) %collective-permute-start.9) | collective-permute-done | bytes 524320 | tf_op jit(solution)/shard_map/ppermute | solution.py:130
  43.1 1.8 collective-permute-done.10.refs_14_.refs_13_
  45.8 8.4 %tangent.10.refs_1_ = f32[16,64,512]{2,1,0:T(8,128)} custom-call(f32[2]{0:T(128)} %pad_maximum_fusion.6.refs_0_, f32[4096,512]{1,0:T(8,128)} %bitcast.139, f32[4096,512]{1,0:T(8,128)} %bitcast.140, f32[4096,512]{1,0:T(8,128)} %bitcast.141, f32[4096,512]{1,0:T(8,128)} %bitcast.142, f32[4096,512]{1,0:T(8,128)} %bitcast.89, f32[4096,512]{1,0:T(8,128)} %bitcast.90, ...), custom_call_target="tpu_custom_call" | custom-call | flops 20971520 | bytes 16777216 | tf_op jit(solution)/shard_map/tangent/pallas_call | solution.py:187
  54.2 1.1 fusion.11
  55.2 1.3 collective-permute-start.12
  56.5 4.6 collective-permute-start.11
  61.1 4.8 collective-permute-done.12.refs_11_
  65.9 2.8 collective-permute-done.11.refs_10_
  69.5 9.0 %tangent.11 = f32[1024,512]{1,0:T(8,128)} custom-call(f32[2]{0:T(128)} %pad_maximum_fusion.6.refs_0_, f32[16,64,512]{2,1,0:T(8,128)} %tangent.10.refs_1_, f32[4096,512]{1,0:T(8,128)} %bitcast.93, f32[4096,512]{1,0:T(8,128)} %bitcast.94, f32[4096,512]{1,0:T(8,128)} %bitcast.95, f32[4096,512]{1,0:T(8,128)} %bitcast.96, f32[4096,512]{1,0:T(8,128)} %bitcast.117, ...), custom_call_target="tpu_custom_call" | custom-call | flops 20971520 | bytes 16777216 | tf_op jit(solution)/shard_map/tangent/pallas_call | solution.py:187
  78.5 8.8 %all-to-all-start.3 = ((f32[64,16,512]{2,1,0:T(8,128)}), f32[64,16,512]{2,1,0:T(8,128)}, u32[]{:S(2)}, u32[]{:S(2)}) async-start(f32[64,16,512]{2,1,0:T(8,128)} %bitcast.163), calls=%async_computation.3 | async-start | bytes 4194304 | tf_op jit(solution)/shard_map/all_to_all | solution.py:213
  87.3 2.8 slice.130
  90.1 2.8 slice.132
  94.6 2.4 copy.51
  97.0 2.4 copy.50
  99.4 2.4 copy.52
  102.1 3.8 collective-permute-start
  106.0 1.3 collective-permute-start.1
  107.3 1.0 slice_bitcast_fusion.17
  108.4 46.4 %collective-permute-done.refs_13_.refs_12_ = f32[4,128,512]{2,1,0:T(8,128)S(1)} collective-permute-done((f32[4,128,512]{2,1,0:T(8,128)S(1)}, f32[4,128,512]{2,1,0:T(8,128)S(1)}, u32[]{:S(2)}, u32[]{:S(2)}) %collective-permute-start) | collective-permute-done | bytes 1048608 | tf_op jit(solution)/shard_map/ppermute | solution.py:130
  154.8 1.9 collective-permute-done.1.refs_14_.refs_13_
  156.7 1.0 copy-done.1
  157.7 15.4 %tangent.6.refs_1_ = f32[16,128,512]{2,1,0:T(8,128)} custom-call(f32[2]{0:T(128)} %pad_maximum_fusion.6.refs_0_, f32[4096,512]{1,0:T(8,128)} %bitcast.148, f32[4096,512]{1,0:T(8,128)} %bitcast.147, f32[4096,512]{1,0:T(8,128)} %bitcast.149, f32[4096,512]{1,0:T(8,128)} %bitcast.150, f32[4096,512]{1,0:T(8,128)} %bitcast.99, f32[4096,512]{1,0:T(8,128)} %bitcast.98, ...), custom_call_target="tpu_custom_call" | custom-call | flops 41943040 | bytes 33554432 | tf_op jit(solution)/shard_map/tangent/pallas_call | solution.py:187
  173.1 1.3 fusion.10
  174.4 1.3 collective-permute-start.3
  175.7 4.6 collective-permute-start.2
  180.3 1.0 slice_bitcast_fusion.16
  181.3 4.3 collective-permute-start.5
  185.7 1.3 collective-permute-start.6
  187.0 4.8 collective-permute-done.2.refs_10_
  192.5 15.9 %tangent.7 = f32[2048,512]{1,0:T(8,128)} custom-call(f32[2]{0:T(128)} %pad_maximum_fusion.6.refs_0_, f32[16,128,512]{2,1,0:T(8,128)} %tangent.6.refs_1_, f32[4096,512]{1,0:T(8,128)} %bitcast.101, f32[4096,512]{1,0:T(8,128)} %bitcast.102, f32[4096,512]{1,0:T(8,128)} %bitcast.103, f32[4096,512]{1,0:T(8,128)} %bitcast.104, f32[4096,512]{1,0:T(8,128)} %bitcast.125, ...), custom_call_target="tpu_custom_call" | custom-call | flops 41943040 | bytes 33554432 | tf_op jit(solution)/shard_map/tangent/pallas_call | solution.py:187
  208.4 3.4 collective-permute-start.4
  211.8 0.8 collective-permute-done.5.refs_13_.refs_12_
  214.3 8.4 %tangent.8.refs_1_ = f32[16,64,512]{2,1,0:T(8,128)} custom-call(f32[2]{0:T(128)} %pad_maximum_fusion.6.refs_0_, f32[4096,512]{1,0:T(8,128)} %bitcast.151, f32[4096,512]{1,0:T(8,128)} %bitcast.152, f32[4096,512]{1,0:T(8,128)} %bitcast.153, f32[4096,512]{1,0:T(8,128)} %bitcast.154, f32[4096,512]{1,0:T(8,128)} %bitcast.105, f32[4096,512]{1,0:T(8,128)} %bitcast.106, ...), custom_call_target="tpu_custom_call" | custom-call | flops 20971520 | bytes 16777216 | tf_op jit(solution)/shard_map/tangent/pallas_call | solution.py:187
  222.6 1.1 fusion.12
  223.7 1.3 collective-permute-start.8
  225.0 5.0 collective-permute-start.7
  230.0 2.4 collective-permute-done.8.refs_11_
  232.4 1.8 collective-permute-done.7.refs_10_
  234.9 9.0 %tangent.9 = f32[1024,512]{1,0:T(8,128)} custom-call(f32[2]{0:T(128)} %pad_maximum_fusion.6.refs_0_, f32[16,64,512]{2,1,0:T(8,128)} %tangent.8.refs_1_, f32[4096,512]{1,0:T(8,128)} %bitcast.109, f32[4096,512]{1,0:T(8,128)} %bitcast.110, f32[4096,512]{1,0:T(8,128)} %bitcast.111, f32[4096,512]{1,0:T(8,128)} %bitcast.112, f32[4096,512]{1,0:T(8,128)} %bitcast.133, ...), custom_call_target="tpu_custom_call" | custom-call | flops 20971520 | bytes 16777216 | tf_op jit(solution)/shard_map/tangent/pallas_call | solution.py:187
  243.9 15.8 %all-to-all-start.2 = ((f32[64,16,512]{2,1,0:T(8,128)}), f32[64,16,512]{2,1,0:T(8,128)S(1)}, u32[]{:S(2)}, u32[]{:S(2)}) async-start(f32[64,16,512]{2,1,0:T(8,128)} %bitcast.164), calls=%async_computation.2 | async-start | bytes 4194304 | tf_op jit(solution)/shard_map/all_to_all | solution.py:213
  259.8 7.0 %bitcast_subtract_fusion = f32[128,16,512]{2,1,0:T(8,128)} fusion(f32[128,16,512]{2,1,0:T(8,128)} %collective-permute-done.4, f32[2,128,16,512]{3,2,1,0:T(8,128)} %param.5), kind=kLoop, calls=%fused_computation.3 | loop fusion | flops 1048576 | bytes 12582912 | tf_op jit(solution)/shard_map/sub | solution.py:271
  266.7 30.3 %all-to-all-done.2 = f32[64,16,512]{2,1,0:T(8,128)S(1)} async-done(((f32[64,16,512]{2,1,0:T(8,128)}), f32[64,16,512]{2,1,0:T(8,128)S(1)}, u32[]{:S(2)}, u32[]{:S(2)}) %all-to-all-start.2) | async-done | bytes 2097184 | tf_op jit(solution)/shard_map/all_to_all | solution.py:213
  297.0 1.3 copy-done.6
  298.4 15.7 %all-to-all-start = ((f32[128,16,512]{2,1,0:T(8,128)}), f32[128,16,512]{2,1,0:T(8,128)}, u32[]{:S(2)}, u32[]{:S(2)}) async-start(f32[128,16,512]{2,1,0:T(8,128)} %bitcast_subtract_fusion), calls=%async_computation | async-start | bytes 8388608 | tf_op jit(solution)/shard_map/all_to_all | solution.py:213
  314.1 2.7 fusion.3
  316.8 8.2 %fusion.1 = (bf16[512,512]{1,0:T(8,128)(2,1)}, bf16[512,512]{1,0:T(8,128)(2,1)}, bf16[512,512]{1,0:T(8,128)(2,1)}, bf16[512,512]{1,0:T(8,128)(2,1)}) fusion(f32[512]{0:T(512)S(1)} %get-tuple-element.59, f32[512]{0:T(512)S(1)} %get-tuple-element.60), kind=kLoop, calls=%fused_computation.15 | loop fusion | flops 3670016 | bytes 2101248 | tf_op jit(solution)/shard_map/convert_element_type | solution.py:27
  325.0 10.1 %middle.4.refs_10_ = f32[16,8,16,512]{3,2,1,0:T(8,128)} custom-call(f32[16,4,16,512]{3,2,1,0:T(8,128)} %bitcast.45.block_ref, f32[256,512]{1,0:T(8,128)} %refs_1_.1, bf16[256,256]{1,0:T(8,128)(2,1)} %get-tuple-element.54.rh.refs_2_, bf16[256,256]{1,0:T(8,128)(2,1)} %get-tuple-element.52.rl.refs_3_, bf16[256,256]{1,0:T(8,128)(2,1)} %get-tuple-element.53.rth.refs_4_, ...), custom_call_target="tpu_custom_call" | custom-call | flops 4831838208 | bytes 4194304 | tf_op jit(solution)/shard_map/middle/pallas_call | solution.py:229
  335.0 10.1 %middle.5 = f32[16,8,16,512]{3,2,1,0:T(8,128)} custom-call(f32[16,4,16,512]{3,2,1,0:T(8,128)} %bitcast.169, f32[256,512]{1,0:T(8,128)} %refs_1_.1, bf16[256,256]{1,0:T(8,128)(2,1)} %get-tuple-element.54.rh.refs_2_, bf16[256,256]{1,0:T(8,128)(2,1)} %get-tuple-element.52.rl.refs_3_, ...), custom_call_target="tpu_custom_call", output_to_operand_aliasing={{}: (10, {})} | custom-call | flops 4831838208 | bytes 4194304 | tf_op jit(solution)/shard_map/middle/pallas_call | solution.py:229
  345.1 47.4 %all-to-all-done = f32[128,16,512]{2,1,0:T(8,128)} async-done(((f32[128,16,512]{2,1,0:T(8,128)}), f32[128,16,512]{2,1,0:T(8,128)}, u32[]{:S(2)}, u32[]{:S(2)}) %all-to-all-start) | async-done | bytes 4194336 | tf_op jit(solution)/shard_map/all_to_all | solution.py:213
  392.5 19.0 %all-to-all-start.4 = ((f32[16,8,16,512]{3,2,1,0:T(8,128)}), f32[16,8,16,512]{3,2,1,0:T(8,128)}, u32[]{:S(2)}, u32[]{:S(2)}) async-start(f32[16,8,16,512]{3,2,1,0:T(8,128)} %middle.5), calls=%async_computation.4 | async-start | bytes 8388608 | tf_op jit(solution)/shard_map/all_to_all | solution.py:213
  411.5 17.2 %middle.3 = f32[16,8,16,512]{3,2,1,0:T(8,128)} custom-call(f32[16,8,16,512]{3,2,1,0:T(8,128)} %bitcast.18.block_ref, f32[256,512]{1,0:T(8,128)} %refs_1_.1, bf16[256,256]{1,0:T(8,128)(2,1)} %get-tuple-element.54.rh.refs_2_, bf16[256,256]{1,0:T(8,128)(2,1)} %get-tuple-element.52.rl.refs_3_, bf16[256,256]{1,0:T(8,128)(2,1)} %get-tuple-element.53.rth.refs_4_, ...), custom_call_target="tpu_custom_call" | custom-call | flops 9663676416 | bytes 8388608 | tf_op jit(solution)/shard_map/middle/pallas_call | solution.py:229
  428.8 61.2 %all-to-all-done.4 = f32[16,8,16,512]{3,2,1,0:T(8,128)} async-done(((f32[16,8,16,512]{3,2,1,0:T(8,128)}), f32[16,8,16,512]{3,2,1,0:T(8,128)}, u32[]{:S(2)}, u32[]{:S(2)}) %all-to-all-start.4) | async-done | bytes 4194336 | tf_op jit(solution)/shard_map/all_to_all | solution.py:213
  490.0 19.5 %all-to-all-start.1 = ((f32[16,8,16,512]{3,2,1,0:T(8,128)}), f32[16,8,16,512]{3,2,1,0:T(8,128)}, u32[]{:S(2)}, u32[]{:S(2)}) async-start(f32[16,8,16,512]{3,2,1,0:T(8,128)} %middle.3), calls=%async_computation.1 | async-start | bytes 8388608 | tf_op jit(solution)/shard_map/all_to_all | solution.py:213
  511.2 6.5 %mix.2.refs_0_ = f32[4096,512]{1,0:T(8,128)} custom-call(f32[2048,512]{1,0:T(8,128)} %bitcast.46.field_ref, bf16[128,128]{1,0:T(8,128)(2,1)} %get-tuple-element.42.vh_ref, bf16[128,128]{1,0:T(8,128)(2,1)} %get-tuple-element.41.vl_ref), custom_call_target="tpu_custom_call" | custom-call | flops 805306368 | bytes 8388608 | tf_op jit(solution)/shard_map/mix/pallas_call | solution.py:251
  517.6 35.3 %all-to-all-done.1 = f32[16,8,16,512]{3,2,1,0:T(8,128)} async-done(((f32[16,8,16,512]{3,2,1,0:T(8,128)}), f32[16,8,16,512]{3,2,1,0:T(8,128)}, u32[]{:S(2)}, u32[]{:S(2)}) %all-to-all-start.1) | async-done | bytes 4194336 | tf_op jit(solution)/shard_map/all_to_all | solution.py:213
  552.9 6.5 %mix.3 = f32[4096,512]{1,0:T(8,128)} custom-call(f32[2048,512]{1,0:T(8,128)} %bitcast.19.field_ref, bf16[128,128]{1,0:T(8,128)(2,1)} %get-tuple-element.46.vh_ref, bf16[128,128]{1,0:T(8,128)(2,1)} %get-tuple-element.45.vl_ref, f32[4096,512]{1,0:T(8,128)} %mix.2.refs_0_), custom_call_target="tpu_custom_call", output_to_operand_aliasing={{}: (3, {})} | custom-call | flops 805306368 | bytes 8388608 | tf_op jit(solution)/shard_map/mix/pallas_call | solution.py:251
  (68 shorter events, 10.7 us)
Async XLA Ops:
  0.0 6.6 %slice-start = ((s8[8388608]{0:T(1024)(128)(4,1)}), s8[4194304]{0:T(1024)(128)(4,1)S(1)}, s32[]{:S(2)}) async-start(s8[8388608]{0:T(1024)(128)(4,1)} %bitcast.137), calls=%async_computation.5 | async-start | bytes 8388608
  2.9 3.8 slice-start.1
  6.7 4.7 slice-start.2
  7.5 3.8 slice-start.3
  15.5 27.6 %collective-permute-start.9 = (f32[4,64,512]{2,1,0:T(8,128)}, f32[4,64,512]{2,1,0:T(8,128)S(1)}, u32[]{:S(2)}, u32[]{:S(2)}) collective-permute-start(f32[4,64,512]{2,1,0:T(8,128)} %pad_maximum_fusion.4), channel_id=1, source_target_pairs={{0,1},{1,2},{2,3},{3,4},{4,5},{5,6},{6,7},{7,8},{8,9},{9,10},{10,1... | collective-permute-start | bytes 1572872 | tf_op jit(solution)/shard_map/ppermute | solution.py:130
  21.3 23.7 %collective-permute-start.10 = (f32[4,64,512]{2,1,0:T(8,128)}, f32[4,64,512]{2,1,0:T(8,128)S(1)}, u32[]{:S(2)}, u32[]{:S(2)}) collective-permute-start(f32[4,64,512]{2,1,0:T(8,128)} %pad_maximum_fusion.5), channel_id=1, source_target_pairs={{1,0},{2,1},{3,2},{4,3},{5,4},{6,5},{7,6},{8,7},{9,8},{10,9},{11,1... | collective-permute-start | bytes 1572872 | tf_op jit(solution)/shard_map/ppermute | solution.py:130
  43.1 1.8 copy-start.2
  44.9 0.8 copy-start.4
  55.2 10.7 %collective-permute-start.12 = (f32[2,64,512]{2,1,0:T(8,128)S(1)}, f32[2,64,512]{2,1,0:T(8,128)S(1)}, u32[]{:S(2)}, u32[]{:S(2)}) collective-permute-start(f32[2,64,512]{2,1,0:T(8,128)S(1)} %get-tuple-element.21), channel_id=1, source_target_pairs={{1,0},{2,1},{3,2},{4,3},{5,4},{6,5},{7,6},{8,7},{9,8},{10,9},{11,1... | collective-permute-start | bytes 786440 | tf_op jit(solution)/shard_map/ppermute | solution.py:130
  56.5 12.2 %collective-permute-start.11 = (f32[2,64,512]{2,1,0:T(8,128)S(1)}, f32[2,64,512]{2,1,0:T(8,128)S(1)}, u32[]{:S(2)}, u32[]{:S(2)}) collective-permute-start(f32[2,64,512]{2,1,0:T(8,128)S(1)} %get-tuple-element.22), channel_id=1, source_target_pairs={{0,1},{1,2},{2,3},{3,4},{4,5},{5,6},{6,7},{7,8},{8,9},{9,10},{10,1... | collective-permute-start | bytes 786440 | tf_op jit(solution)/shard_map/ppermute | solution.py:130
  65.9 2.9 copy-start.11
  68.8 0.7 copy-start.13
  78.5 165.4 %all-to-all-start.3 = ((f32[64,16,512]{2,1,0:T(8,128)}), f32[64,16,512]{2,1,0:T(8,128)}, u32[]{:S(2)}, u32[]{:S(2)}) async-start(f32[64,16,512]{2,1,0:T(8,128)} %bitcast.163), calls=%async_computation.3 | async-start | bytes 4194304 | tf_op jit(solution)/shard_map/all_to_all | solution.py:213
  87.3 5.7 %slice-start.4 = ((s8[8388608]{0:T(1024)(128)(4,1)}), s8[4194304]{0:T(1024)(128)(4,1)S(1)}, s32[]{:S(2)}) async-start(s8[8388608]{0:T(1024)(128)(4,1)} %bitcast.161), calls=%async_computation.9 | async-start | bytes 8388608
  90.1 3.6 slice-start.5
  102.1 52.6 %collective-permute-start = (f32[4,128,512]{2,1,0:T(8,128)S(1)}, f32[4,128,512]{2,1,0:T(8,128)S(1)}, u32[]{:S(2)}, u32[]{:S(2)}) collective-permute-start(f32[4,128,512]{2,1,0:T(8,128)S(1)} %pad_maximum_fusion), channel_id=1, source_target_pairs={{0,1},{1,2},{2,3},{3,4},{4,5},{5,6},{6,7},{7,8},{8,9},{9,10},{10,1... | collective-permute-start | bytes 3145736 | tf_op jit(solution)/shard_map/ppermute | solution.py:130
  106.0 50.6 %collective-permute-start.1 = (f32[4,128,512]{2,1,0:T(8,128)S(1)}, f32[4,128,512]{2,1,0:T(8,128)S(1)}, u32[]{:S(2)}, u32[]{:S(2)}) collective-permute-start(f32[4,128,512]{2,1,0:T(8,128)S(1)} %pad_maximum_fusion.1), channel_id=1, source_target_pairs={{1,0},{2,1},{3,2},{4,3},{5,4},{6,5},{7,6},{8,7},{9,8},{10,9},{11,1... | collective-permute-start | bytes 3145736 | tf_op jit(solution)/shard_map/ppermute | solution.py:130
  154.8 1.9 copy-start
  156.7 1.0 copy-start.1
  174.4 12.6 %collective-permute-start.3 = (f32[2,128,512]{2,1,0:T(8,128)S(1)}, f32[2,128,512]{2,1,0:T(8,128)S(1)}, u32[]{:S(2)}, u32[]{:S(2)}) collective-permute-start(f32[2,128,512]{2,1,0:T(8,128)S(1)} %get-tuple-element.11), channel_id=1, source_target_pairs={{1,0},{2,1},{3,2},{4,3},{5,4},{6,5},{7,6},{8,7},{9,8},{10,9},{11,1... | collective-permute-start | bytes 1572872 | tf_op jit(solution)/shard_map/ppermute | solution.py:130
  175.7 16.1 %collective-permute-start.2 = (f32[2,128,512]{2,1,0:T(8,128)S(1)}, f32[2,128,512]{2,1,0:T(8,128)S(1)}, u32[]{:S(2)}, u32[]{:S(2)}) collective-permute-start(f32[2,128,512]{2,1,0:T(8,128)S(1)} %get-tuple-element.12), channel_id=1, source_target_pairs={{0,1},{1,2},{2,3},{3,4},{4,5},{5,6},{6,7},{7,8},{8,9},{9,10},{10,1... | collective-permute-start | bytes 1572872 | tf_op jit(solution)/shard_map/ppermute | solution.py:130
  181.3 31.4 %collective-permute-start.5 = (f32[4,64,512]{2,1,0:T(8,128)S(1)}, f32[4,64,512]{2,1,0:T(8,128)S(1)}, u32[]{:S(2)}, u32[]{:S(2)}) collective-permute-start(f32[4,64,512]{2,1,0:T(8,128)S(1)} %pad_maximum_fusion.2), channel_id=1, source_target_pairs={{0,1},{1,2},{2,3},{3,4},{4,5},{5,6},{6,7},{7,8},{8,9},{9,10},{10,1... | collective-permute-start | bytes 1572872 | tf_op jit(solution)/shard_map/ppermute | solution.py:130
  185.7 27.0 %collective-permute-start.6 = (f32[4,64,512]{2,1,0:T(8,128)S(1)}, f32[4,64,512]{2,1,0:T(8,128)S(1)}, u32[]{:S(2)}, u32[]{:S(2)}) collective-permute-start(f32[4,64,512]{2,1,0:T(8,128)S(1)} %pad_maximum_fusion.3), channel_id=1, source_target_pairs={{1,0},{2,1},{3,2},{4,3},{5,4},{6,5},{7,6},{8,7},{9,8},{10,9},{11,1... | collective-permute-start | bytes 1572872 | tf_op jit(solution)/shard_map/ppermute | solution.py:130
  187.0 4.8 copy-start.8
  191.7 0.8 copy-start.9
  208.4 51.3 %collective-permute-start.4 = (f32[128,16,512]{2,1,0:T(8,128)}, f32[128,16,512]{2,1,0:T(8,128)}, u32[]{:S(2)}, u32[]{:S(2)}) collective-permute-start(f32[128,16,512]{2,1,0:T(8,128)} %bitcast.168), channel_id=1, source_target_pairs={{0,16},{1,17},{2,18},{3,19},{4,20},{5,21},{6,22},{7,23},{8,24},{9,... | collective-permute-start | bytes 12582920 | tf_op jit(solution)/shard_map/ppermute | solution.py:133
  212.6 0.8 copy-start.3
  213.4 0.8 copy-start.5
  223.7 8.7 %collective-permute-start.8 = (f32[2,64,512]{2,1,0:T(8,128)S(1)}, f32[2,64,512]{2,1,0:T(8,128)S(1)}, u32[]{:S(2)}, u32[]{:S(2)}) collective-permute-start(f32[2,64,512]{2,1,0:T(8,128)S(1)} %get-tuple-element.31), channel_id=1, source_target_pairs={{1,0},{2,1},{3,2},{4,3},{5,4},{6,5},{7,6},{8,7},{9,8},{10,9},{11,1... | collective-permute-start | bytes 786440 | tf_op jit(solution)/shard_map/ppermute | solution.py:130
  225.0 9.2 %collective-permute-start.7 = (f32[2,64,512]{2,1,0:T(8,128)S(1)}, f32[2,64,512]{2,1,0:T(8,128)S(1)}, u32[]{:S(2)}, u32[]{:S(2)}) collective-permute-start(f32[2,64,512]{2,1,0:T(8,128)S(1)} %get-tuple-element.32), channel_id=1, source_target_pairs={{0,1},{1,2},{2,3},{3,4},{4,5},{5,6},{6,7},{7,8},{8,9},{9,10},{10,1... | collective-permute-start | bytes 786440 | tf_op jit(solution)/shard_map/ppermute | solution.py:130
  232.4 1.8 copy-start.10
  234.2 0.7 copy-start.12
  243.9 53.1 %all-to-all-start.2 = ((f32[64,16,512]{2,1,0:T(8,128)}), f32[64,16,512]{2,1,0:T(8,128)S(1)}, u32[]{:S(2)}, u32[]{:S(2)}) async-start(f32[64,16,512]{2,1,0:T(8,128)} %bitcast.164), calls=%async_computation.2 | async-start | bytes 4194304 | tf_op jit(solution)/shard_map/all_to_all | solution.py:213
  297.0 1.3 copy-start.6
  298.4 94.1 %all-to-all-start = ((f32[128,16,512]{2,1,0:T(8,128)}), f32[128,16,512]{2,1,0:T(8,128)}, u32[]{:S(2)}, u32[]{:S(2)}) async-start(f32[128,16,512]{2,1,0:T(8,128)} %bitcast_subtract_fusion), calls=%async_computation | async-start | bytes 8388608 | tf_op jit(solution)/shard_map/all_to_all | solution.py:213
  392.5 97.5 %all-to-all-start.4 = ((f32[16,8,16,512]{3,2,1,0:T(8,128)}), f32[16,8,16,512]{3,2,1,0:T(8,128)}, u32[]{:S(2)}, u32[]{:S(2)}) async-start(f32[16,8,16,512]{3,2,1,0:T(8,128)} %middle.5), calls=%async_computation.4 | async-start | bytes 8388608 | tf_op jit(solution)/shard_map/all_to_all | solution.py:213
  428.8 80.7 %copy-start.7 = (f32[128,128]{1,0:T(8,128)S(1)}, f32[128,128]{1,0:T(8,128)}, u32[]{:S(2)}) copy-start(f32[128,128]{1,0:T(8,128)} %param.9) | copy-start | bytes 196612
  490.0 62.9 %all-to-all-start.1 = ((f32[16,8,16,512]{3,2,1,0:T(8,128)}), f32[16,8,16,512]{3,2,1,0:T(8,128)}, u32[]{:S(2)}, u32[]{:S(2)}) async-start(f32[16,8,16,512]{3,2,1,0:T(8,128)} %middle.3), calls=%async_computation.1 | async-start | bytes 8388608 | tf_op jit(solution)/shard_map/all_to_all | solution.py:213

commit v2 on v1

--- a/solution.py
+++ b/solution.py
@@ -7,7 +7,7 @@
 from jax.experimental.pallas import tpu as pltpu
 from jax.sharding import PartitionSpec as P
 
-STEPS = 4
+
 LANES = 128
 DIFFUSION = 0.2
 CUTS_LAST = (4, 8)
@@ -46,6 +46,13 @@
     return DIFFUSION * total - half_x * (north - south) - half_y * (east - west)
 
 
+def edge_kernel(inc_b, cx_b, cy_b, inc_t, cx_t, cy_t, low, high):
+    low[0], low[1] = inc_b[:, 6, :], inc_b[:, 7, :]
+    low[2], low[3] = cx_b[:, 7, :], cy_b[:, 7, :]
+    high[0], high[1] = inc_t[:, 0, :], inc_t[:, 1, :]
+    high[2], high[3] = cx_t[:, 0, :], cy_t[:, 0, :]
+
+
 def tangent_kernel(rows, parts, first, last, *refs):
     refs = list(refs)
 
@@ -61,6 +68,7 @@
     far_before, far_after = (before, after) if first else take(2)
     target = take(parts) if last == "jump" else None
     (out,) = take(1)
+    low, high = (None, None) if last else take(2)
     old, mid, hx, hy, flat = refs
     at = lambda i: slice(i * LANES, (i + 1) * LANES)
 
@@ -87,6 +95,10 @@
         new = stepped(mid[x + 1], mid[x + 2], mid[x], hx[x + 1], hy[x + 1])
         if not last:
             out[x] = new
+            if x < 2:
+                high[x] = new
+            if x >= rows - 2:
+                low[x - rows + 2] = new
         else:
             for i in range(parts):
                 flat[i, pl.ds(x, 8, stride=rows), :] = new[:, at(i)]
@@ -117,6 +129,19 @@
     return pltpu.CompilerParams(vmem_limit_bytes=56 << 20, **more)
 
 
+def chunk_of(cuts, levels, bricks):
+    ends = [max(1, round(c * (levels // bricks) / 8)) * bricks for c in cuts]
+    return [(a, b) for a, b in zip([0] + ends[:-1], ends) if b > a]
+
+
+def jobs_of(subs, levels, bricks):
+    jobs = []
+    for target in range(subs - 1, 0, -1):
+        cuts = CUTS_LAST if target == subs - 1 else CUTS_FIRST
+        jobs += [(f"s{target}l{a}", target - 1, target, a, b) for a, b in chunk_of(cuts, levels, bricks)]
+    return jobs + [(f"s0l{a}", subs - 1, None, a, b) for a, b in chunk_of(CUTS_FIRST, levels, bricks)]
+
+
 def on_device(increments, courant_x, courant_y, spectrum, vertical):
     subs, levels, rows, cols = increments.shape
     bricks, groups = lax.axis_size("brick"), lax.axis_size("sub")
@@ -138,10 +163,6 @@
     def cost(values, passes):
         return pl.CostEstimate(flops=20 * values * passes, bytes_accessed=16 * values * passes, transcendentals=0)
 
-    def chunk_of(cuts):
-        ends = [max(1, round(c * (levels // bricks) / 8)) * bricks for c in cuts]
-        return [(a, b) for a, b in zip([0] + ends[:-1], ends) if b > a]
-
     parts = cols // LANES
     flat_all = [a.reshape(-1, cols) for a in (increments, courant_x, courant_y)]
     inside = jnp.stack([jnp.where(brick > 0, 1.0, 0.0), jnp.where(brick < bricks - 1, 1.0, 0.0)]).astype(f32)
@@ -152,12 +173,20 @@
         ]
         return [array] * parts, specs
 
-    def first_halo(sub, start, stop):
-        inc, cx, cy = (a[sub, start:stop] for a in (increments, courant_x, courant_y))
-        last = sub == subs - 1
-        low = jnp.stack([inc[:, rows - 2], inc[:, rows - 1], cx[:, rows - 1], cy[:, rows - 1]])
-        high = jnp.stack([inc[:, 0], inc[:, 1], cx[:, 0], cy[:, 0]])
-        return neighbour(low, 1, last), neighbour(high, -1, last)
+    def edges(sub, start, stop):
+        size = 16
+        block = lambda at: pl.BlockSpec((size, 8, cols), lambda i: ((sub * levels + start) // size + i, at, 0))
+        arrays = [a.reshape(-1, rows, cols) for a in (increments, courant_x, courant_y)]
+        return pl.pallas_call(
+            edge_kernel,
+            grid=((stop - start) // size,),
+            in_specs=[block(rows // 8 - 1)] * 3 + [block(0)] * 3,
+            out_specs=[pl.BlockSpec((4, size, cols), lambda i: (0, i, 0))] * 2,
+            out_shape=[jax.ShapeDtypeStruct((4, stop - start, cols), f32)] * 2,
+            compiler_params=params(),
+            cost_estimate=pl.CostEstimate(flops=0, bytes_accessed=200 * (stop - start) * cols, transcendentals=0),
+            name="edge",
+        )(*arrays, *arrays)
 
     def tangent(number, sub, start, stop, state, halo, far, target):
         span = stop - start
@@ -181,15 +210,16 @@
         if last == "jump":
             add(*pieces(flat_all[0], target, start))
         if first:
-            out, out_spec = (rows, span, cols), slab
+            pair = pl.BlockSpec((2, 8, cols), lambda i: (0, i, 0))
+            out, out_spec = [(rows, span, cols)] + [(2, span, cols)] * 2, [slab, pair, pair]
         else:
-            out, out_spec = (span * rows, cols), pl.BlockSpec((8 * rows, cols), lambda i: (i, 0))
+            out, out_spec = [(span * rows, cols)], [pl.BlockSpec((8 * rows, cols), lambda i: (i, 0))]
         return pl.pallas_call(
             functools.partial(tangent_kernel, rows, parts, first, last),
             grid=(span // 8,),
             in_specs=specs,
             out_specs=out_spec,
-            out_shape=jax.ShapeDtypeStruct(out, f32),
+            out_shape=[jax.ShapeDtypeStruct(o, f32) for o in out],
             scratch_shapes=[
                 pltpu.VMEM((rows + 4, 8, cols), f32),
                 pltpu.VMEM((rows + 2, 8, cols), f32),
@@ -203,11 +233,16 @@
         )(*inputs)
 
     def advance(sub, target, start, stop):
-        far = first_halo(sub, start, stop)
-        state = tangent(0, sub, start, stop, None, far, far, None)
+        low, high = edges(sub, start, stop)
         last = sub == subs - 1
-        halo = neighbour(state[rows - 2 :], 1, last), neighbour(state[:2], -1, last)
-        return tangent(1, sub, start, stop, state, halo, far, target).reshape(stop - start, rows, cols)
+        far = neighbour(low, 1, last), neighbour(high, -1, last)
+        state, low, high = tangent(0, sub, start, stop, None, far, far, None)
+        near = neighbour(low, 1, last), neighbour(high, -1, last)
+        (moved,) = tangent(1, sub, start, stop, state, near, far, target)
+        moved = moved.reshape(-1, rows, cols)
+        if target is None:
+            moved = increments[0, start:stop] - next_sub(moved)
+        return moved
 
     def spread(value):
         return lax.all_to_all(value, "brick", split_axis=0, concat_axis=0, tiled=True)
@@ -263,17 +298,15 @@
         )(*inputs)
 
     out = None
-    work = []
-    for target in range(subs - 1, 0, -1):
-        cuts = chunk_of(CUTS_LAST if target == subs - 1 else CUTS_FIRST)
-        work.append((target, [(a, b, advance(target - 1, target, a, b)) for a, b in cuts]))
-    ends = [(a, b, advance(subs - 1, None, a, b)) for a, b in chunk_of(CUTS_FIRST)]
-    work.append((0, [(a, b, increments[0, a:b] - next_sub(e)) for a, b, e in ends]))
-    received = [(sub, [(a, b, spread(jump)) for a, b, jump in group]) for sub, group in work]
+    work = {}
+    for name, sub, target, start, stop in jobs_of(subs, levels, bricks):
+        moved = advance(sub, target, start, stop)
+        block = spread(moved)
+        work.setdefault(0 if target is None else target, []).append((name, start, stop, block))
     returned = []
-    for sub, group in received:
+    for sub, group in work.items():
         done, offset, columns = None, 0, []
-        for a, b, block in group:
+        for name, a, b, block in group:
             share = (b - a) // bricks
             done = middle(block, done, offset, levels // bricks)
             offset += share

time: 570 us -> 548 us (0.961)
  local copies, waits for them, and re-layouts: 41.9 us -> 5.19 us
  Pallas kernels: 116 us -> 133 us
  waiting for transfers between devices: 262 us -> 269 us
  starting transfers between devices: 117 us -> 111 us
    ppermute x12, waiting for transfers between devices: 87.5 us -> 120 us  [neighbour(): return lax.ppermute(value, ('sub', 'brick'), pairs)]
    all_to_all x5, waiting for transfers between devices: 174 us -> 148 us  [spread(): lax.all_to_all(value, 'brick', split_axis=0, concat_axis=0, tiled=True)]
    pallas_call x0 -> x3, Pallas kernels: none -> 16.4 us  [edges(): pl.pallas_call(edge_kernel, grid=((stop - start) // size,), in_specs=[blo...]
    slice x9 -> x0, local copies, waits for them, and re-layouts: 14.4 us -> none  [the longest x6 11 us: first_halo(): a[sub, start:stop]]
    unnamed x45 -> x30, local copies, waits for them, and re-layouts: 15.2 us -> 5.02 us
    squeeze x3 -> x0, local copies, waits for them, and re-layouts: 9.96 us -> none  [first_halo(): a[sub, start:stop]]
  transfers between devices with their start and end apart: 18 -> 18, of which waited for: 14 -> 16; matrix products, arithmetic and copies ran while one was open for 7% -> 4% of each run, Pallas kernels for 17% -> 19%
where the time goes in v2:
time: 548 us; the launch traced here: 537 us
  waiting for transfers between devices  269 us (49%)
  Pallas kernels  133 us (24%)
  starting transfers between devices  111 us (20%)
  other arithmetic  19.7 us (4%)
    all_to_all x5, waiting for transfers between devices, spread(): lax.all_to_all(value, 'brick', split_axis=0, concat_axis=0, tiled=True)  148 us
    ppermute x12, waiting for transfers between devices, neighbour(): return lax.ppermute(value, ('sub', 'brick'), pairs)  120 us
    all_to_all x5, starting transfers between devices, spread(): lax.all_to_all(value, 'brick', split_axis=0, concat_axis=0, tiled=True)  78 us
    pallas_call x6, Pallas kernels, tangent(): pl.pallas_call(functools.partial(tangent_kernel, rows, parts, first, last...  66.2 us
    pallas_call x3, Pallas kernels, middle(): pl.pallas_call(kernel, grid=(share,), in_specs=specs, out_specs=pl.BlockS...  37.2 us
    ppermute x12, starting transfers between devices, neighbour(): return lax.ppermute(value, ('sub', 'brick'), pairs)  29.4 us
    pallas_call x3, Pallas kernels, edges(): pl.pallas_call(edge_kernel, grid=((stop - start) // size,), in_specs=[blo...  16.4 us
    pallas_call x2, Pallas kernels, mix(): pl.pallas_call(kernel, grid=(parts,), in_specs=specs, out_specs=pl.BlockS...  12.9 us
  transfers between devices with their start and end apart: 18, of which 16 were waited for; matrix products, arithmetic and copies ran while one was open for 4% of the time, Pallas kernels for 19%

profile of v2, /device:TPU:0, one launch (start us, length us, event | category | flops | bytes accessed | tf_op | source)
XLA Modules:
  0.0 537.4 jit_solution(3317874327794384305)
XLA Ops:
  0.0 4.3 edge.4
  4.3 4.9 collective-permute-start.5
  9.2 1.3 collective-permute-start.6
  10.5 0.6 pad_maximum_fusion.refs_0_
  11.1 20.8 %collective-permute-done.5.refs_13_.refs_12_ = f32[4,64,512]{2,1,0:T(8,128)S(1)} collective-permute-done((f32[4,64,512]{2,1,0:T(8,128)}, f32[4,64,512]{2,1,0:T(8,128)S(1)}, u32[]{:S(2)}, u32[]{:S(2)}) %collective-permute-start.5) | collective-permute-done | bytes 524320 | tf_op jit(solution)/shard_map/ppermute | solution.py:155
  31.9 1.8 collective-permute-done.6.refs_14_.refs_13_
  33.7 0.8 copy-done.3
  34.5 8.4 %tangent.8 = (f32[16,64,512]{2,1,0:T(8,128)}, f32[2,64,512]{2,1,0:T(8,128)}, f32[2,64,512]{2,1,0:T(8,128)}) custom-call(f32[2]{0:T(128)} %pad_maximum_fusion.refs_0_, f32[4096,512]{1,0:T(8,128)} %bitcast.85, f32[4096,512]{1,0:T(8,128)} %bitcast.86, f32[4096,512]{1,0:T(8,128)} %bitcast.87, f32[4096,512]{1,0:T(8,128)} %bitcast.88, f32[4096,512]{1,0:T(8,128)} %bitcast.25, ...), custom_call_target="tpu_custom_call" | custom-call | flops 20971520 | bytes 16777216 | tf_op jit(solution)/shard_map/tangent/pallas_call | solution.py:217
  42.9 3.4 collective-permute-start.7
  46.3 1.3 collective-permute-start.8
  47.6 9.3 %collective-permute-done.7.refs_10_ = f32[2,64,512]{2,1,0:T(8,128)S(1)} collective-permute-done((f32[2,64,512]{2,1,0:T(8,128)}, f32[2,64,512]{2,1,0:T(8,128)S(1)}, u32[]{:S(2)}, u32[]{:S(2)}) %collective-permute-start.7) | collective-permute-done | bytes 262176 | tf_op jit(solution)/shard_map/ppermute | solution.py:155
  57.0 0.6 collective-permute-done.8.refs_11_
  57.6 0.1 copy-done.11
  57.7 0.6 copy-done.13
  58.3 9.0 %tangent.9 = f32[1024,512]{1,0:T(8,128)} custom-call(f32[2]{0:T(128)} %pad_maximum_fusion.refs_0_, f32[16,64,512]{2,1,0:T(8,128)} %get-tuple-element.27.refs_1_, f32[4096,512]{1,0:T(8,128)} %bitcast.29, f32[4096,512]{1,0:T(8,128)} %bitcast.30, f32[4096,512]{1,0:T(8,128)} %bitcast.31, f32[4096,512]{1,0:T(8,128)} %bitcast.32, f32[4096,512]{1,0:T(8,128)} %bitcast.59, ...), custom_call_target="tpu_custom_call" | custom-call | flops 20971520 | bytes 16777216 | tf_op jit(solution)/shard_map/tangent/pallas_call | solution.py:217
  67.3 7.1 %all-to-all-start.2 = ((f32[64,16,512]{2,1,0:T(8,128)}), f32[64,16,512]{2,1,0:T(8,128)S(1)}, u32[]{:S(2)}, u32[]{:S(2)}) async-start(f32[64,16,512]{2,1,0:T(8,128)} %bitcast.109), calls=%async_computation.2 | async-start | bytes 4194304 | tf_op jit(solution)/shard_map/all_to_all | solution.py:248
  74.4 7.8 %edge.3 = (f32[4,128,512]{2,1,0:T(8,128)}, f32[4,128,512]{2,1,0:T(8,128)}) custom-call(f32[256,16,512]{2,1,0:T(8,128)} %bitcast.93, f32[256,16,512]{2,1,0:T(8,128)} %bitcast.33, f32[256,16,512]{2,1,0:T(8,128)} %bitcast.63, f32[256,16,512]{2,1,0:T(8,128)} %bitcast.94, f32[256,16,512]{2,1,0:T(8,128)} %bitcast.34, f32[256,16,512]{2,1,0:T(8,128)} %bitcast.64), custom_call_target="tpu_custom_call" | custom-call | bytes 13107200 | tf_op jit(solution)/shard_map/edge/pallas_call | solution.py:180
  82.2 3.9 collective-permute-start
  86.1 1.3 collective-permute-start.1
  87.4 39.2 %collective-permute-done.refs_13_.refs_12_ = f32[4,128,512]{2,1,0:T(8,128)S(1)} collective-permute-done((f32[4,128,512]{2,1,0:T(8,128)}, f32[4,128,512]{2,1,0:T(8,128)S(1)}, u32[]{:S(2)}, u32[]{:S(2)}) %collective-permute-start) | collective-permute-done | bytes 1048608 | tf_op jit(solution)/shard_map/ppermute | solution.py:155
  126.6 2.7 collective-permute-done.1.refs_14_.refs_13_
  129.3 1.0 copy-done.1
  130.3 15.5 %tangent.6 = (f32[16,128,512]{2,1,0:T(8,128)}, f32[2,128,512]{2,1,0:T(8,128)}, f32[2,128,512]{2,1,0:T(8,128)}) custom-call(f32[2]{0:T(128)} %pad_maximum_fusion.refs_0_, f32[4096,512]{1,0:T(8,128)} %bitcast.95, f32[4096,512]{1,0:T(8,128)} %bitcast.96, f32[4096,512]{1,0:T(8,128)} %bitcast.97, f32[4096,512]{1,0:T(8,128)} %bitcast.98, f32[4096,512]{1,0:T(8,128)} %bitcast.37, ...), custom_call_target="tpu_custom_call" | custom-call | flops 41943040 | bytes 33554432 | tf_op jit(solution)/shard_map/tangent/pallas_call | solution.py:217
  145.8 3.6 collective-permute-start.2
  149.4 1.3 collective-permute-start.3
  150.7 7.4 %collective-permute-done.2.refs_10_ = f32[2,128,512]{2,1,0:T(8,128)S(1)} collective-permute-done((f32[2,128,512]{2,1,0:T(8,128)}, f32[2,128,512]{2,1,0:T(8,128)S(1)}, u32[]{:S(2)}, u32[]{:S(2)}) %collective-permute-start.2) | collective-permute-done | bytes 524320 | tf_op jit(solution)/shard_map/ppermute | solution.py:155
  158.1 9.8 %collective-permute-done.3.refs_11_ = f32[2,128,512]{2,1,0:T(8,128)S(1)} collective-permute-done((f32[2,128,512]{2,1,0:T(8,128)}, f32[2,128,512]{2,1,0:T(8,128)S(1)}, u32[]{:S(2)}, u32[]{:S(2)}) %collective-permute-start.3) | collective-permute-done | bytes 524320 | tf_op jit(solution)/shard_map/ppermute | solution.py:155
  167.9 0.8 copy-done.9
  168.7 15.9 %tangent.7 = f32[2048,512]{1,0:T(8,128)} custom-call(f32[2]{0:T(128)} %pad_maximum_fusion.refs_0_, f32[16,128,512]{2,1,0:T(8,128)} %get-tuple-element.22.refs_1_, f32[4096,512]{1,0:T(8,128)} %bitcast.39, f32[4096,512]{1,0:T(8,128)} %bitcast.40, f32[4096,512]{1,0:T(8,128)} %bitcast.41, f32[4096,512]{1,0:T(8,128)} %bitcast.42, f32[4096,512]{1,0:T(8,128)} %bitcast.69, ...), custom_call_target="tpu_custom_call" | custom-call | flops 41943040 | bytes 33554432 | tf_op jit(solution)/shard_map/tangent/pallas_call | solution.py:217
  184.6 3.4 collective-permute-start.4
  188.0 4.4 edge.5
  192.4 1.6 collective-permute-start.9
  193.9 1.3 collective-permute-start.10
  195.2 18.7 %collective-permute-done.9.refs_13_.refs_12_ = f32[4,64,512]{2,1,0:T(8,128)S(1)} collective-permute-done((f32[4,64,512]{2,1,0:T(8,128)}, f32[4,64,512]{2,1,0:T(8,128)S(1)}, u32[]{:S(2)}, u32[]{:S(2)}) %collective-permute-start.9) | collective-permute-done | bytes 524320 | tf_op jit(solution)/shard_map/ppermute | solution.py:155
  213.9 1.6 collective-permute-done.10.refs_14_.refs_13_
  215.5 0.8 copy-done.5
  216.3 8.4 %tangent.10 = (f32[16,64,512]{2,1,0:T(8,128)}, f32[2,64,512]{2,1,0:T(8,128)}, f32[2,64,512]{2,1,0:T(8,128)}) custom-call(f32[2]{0:T(128)} %pad_maximum_fusion.refs_0_, f32[4096,512]{1,0:T(8,128)} %bitcast.101, f32[4096,512]{1,0:T(8,128)} %bitcast.102, f32[4096,512]{1,0:T(8,128)} %bitcast.103, f32[4096,512]{1,0:T(8,128)} %bitcast.104, f32[4096,512]{1,0:T(8,128)} %bitcast.45, ...), custom_call_target="tpu_custom_call" | custom-call | flops 20971520 | bytes 16777216 | tf_op jit(solution)/shard_map/tangent/pallas_call | solution.py:217
  224.7 4.3 collective-permute-start.11
  229.1 1.3 collective-permute-start.12
  230.4 2.9 collective-permute-done.11.refs_10_
  233.2 5.3 collective-permute-done.12.refs_11_
  238.6 0.7 copy-done.12
  239.3 9.0 %tangent.11 = f32[1024,512]{1,0:T(8,128)} custom-call(f32[2]{0:T(128)} %pad_maximum_fusion.refs_0_, f32[16,64,512]{2,1,0:T(8,128)} %get-tuple-element.32.refs_1_, f32[4096,512]{1,0:T(8,128)} %bitcast.49, f32[4096,512]{1,0:T(8,128)} %bitcast.50, f32[4096,512]{1,0:T(8,128)} %bitcast.51, f32[4096,512]{1,0:T(8,128)} %bitcast.52, f32[4096,512]{1,0:T(8,128)} %bitcast.79, ...), custom_call_target="tpu_custom_call" | custom-call | flops 20971520 | bytes 16777216 | tf_op jit(solution)/shard_map/tangent/pallas_call | solution.py:217
  248.3 23.5 %all-to-all-start.3 = ((f32[64,16,512]{2,1,0:T(8,128)}), f32[64,16,512]{2,1,0:T(8,128)}, u32[]{:S(2)}, u32[]{:S(2)}) async-start(f32[64,16,512]{2,1,0:T(8,128)} %bitcast.110), calls=%async_computation.3 | async-start | bytes 4194304 | tf_op jit(solution)/shard_map/all_to_all | solution.py:248
  271.8 7.0 %bitcast_subtract_fusion = f32[128,16,512]{2,1,0:T(8,128)} fusion(f32[128,16,512]{2,1,0:T(8,128)} %collective-permute-done.4, f32[2,128,16,512]{3,2,1,0:T(8,128)} %param.5), kind=kLoop, calls=%fused_computation | loop fusion | flops 1048576 | bytes 12582912 | tf_op jit(solution)/shard_map/sub | solution.py:244
  278.8 45.4 %all-to-all-done.3 = f32[64,16,512]{2,1,0:T(8,128)} async-done(((f32[64,16,512]{2,1,0:T(8,128)}), f32[64,16,512]{2,1,0:T(8,128)}, u32[]{:S(2)}, u32[]{:S(2)}) %all-to-all-start.3) | async-done | bytes 2097184 | tf_op jit(solution)/shard_map/all_to_all | solution.py:248
  324.2 12.3 %all-to-all-start = ((f32[128,16,512]{2,1,0:T(8,128)}), f32[128,16,512]{2,1,0:T(8,128)}, u32[]{:S(2)}, u32[]{:S(2)}) async-start(f32[128,16,512]{2,1,0:T(8,128)} %bitcast_subtract_fusion), calls=%async_computation | async-start | bytes 8388608 | tf_op jit(solution)/shard_map/all_to_all | solution.py:248
  336.6 2.7 fusion.3
  339.2 8.2 %fusion.1 = (bf16[512,512]{1,0:T(8,128)(2,1)}, bf16[512,512]{1,0:T(8,128)(2,1)}, bf16[512,512]{1,0:T(8,128)(2,1)}, bf16[512,512]{1,0:T(8,128)(2,1)}) fusion(f32[512]{0:T(512)S(1)} %get-tuple-element.51, f32[512]{0:T(512)S(1)} %get-tuple-element.52), kind=kLoop, calls=%fused_computation.6 | loop fusion | flops 3670016 | bytes 2101248 | tf_op jit(solution)/shard_map/convert_element_type | solution.py:27
  347.4 10.0 %middle.4.refs_10_ = f32[16,8,16,512]{3,2,1,0:T(8,128)} custom-call(f32[16,4,16,512]{3,2,1,0:T(8,128)} %bitcast.15.block_ref, f32[256,512]{1,0:T(8,128)} %refs_1_.1, bf16[256,256]{1,0:T(8,128)(2,1)} %get-tuple-element.48.rh.refs_2_, bf16[256,256]{1,0:T(8,128)(2,1)} %get-tuple-element.46.rl.refs_3_, bf16[256,256]{1,0:T(8,128)(2,1)} %get-tuple-element.47.rth.refs_4_, ...), custom_call_target="tpu_custom_call" | custom-call | flops 4831838208 | bytes 4194304 | tf_op jit(solution)/shard_map/middle/pallas_call | solution.py:264
  357.4 10.0 %middle.5 = f32[16,8,16,512]{3,2,1,0:T(8,128)} custom-call(f32[16,4,16,512]{3,2,1,0:T(8,128)} %bitcast.112, f32[256,512]{1,0:T(8,128)} %refs_1_.1, bf16[256,256]{1,0:T(8,128)(2,1)} %get-tuple-element.48.rh.refs_2_, bf16[256,256]{1,0:T(8,128)(2,1)} %get-tuple-element.46.rl.refs_3_, ...), custom_call_target="tpu_custom_call", output_to_operand_aliasing={{}: (10, {})} | custom-call | flops 4831838208 | bytes 4194304 | tf_op jit(solution)/shard_map/middle/pallas_call | solution.py:264
  367.4 41.2 %all-to-all-done = f32[128,16,512]{2,1,0:T(8,128)} async-done(((f32[128,16,512]{2,1,0:T(8,128)}), f32[128,16,512]{2,1,0:T(8,128)}, u32[]{:S(2)}, u32[]{:S(2)}) %all-to-all-start) | async-done | bytes 4194336 | tf_op jit(solution)/shard_map/all_to_all | solution.py:248
  408.6 22.8 %all-to-all-start.4 = ((f32[16,8,16,512]{3,2,1,0:T(8,128)}), f32[16,8,16,512]{3,2,1,0:T(8,128)}, u32[]{:S(2)}, u32[]{:S(2)}) async-start(f32[16,8,16,512]{3,2,1,0:T(8,128)} %middle.5), calls=%async_computation.4 | async-start | bytes 8388608 | tf_op jit(solution)/shard_map/all_to_all | solution.py:248
  431.4 17.2 %middle.3 = f32[16,8,16,512]{3,2,1,0:T(8,128)} custom-call(f32[16,8,16,512]{3,2,1,0:T(8,128)} %bitcast.10.block_ref, f32[256,512]{1,0:T(8,128)} %refs_1_.1, bf16[256,256]{1,0:T(8,128)(2,1)} %get-tuple-element.48.rh.refs_2_, bf16[256,256]{1,0:T(8,128)(2,1)} %get-tuple-element.46.rl.refs_3_, bf16[256,256]{1,0:T(8,128)(2,1)} %get-tuple-element.47.rth.refs_4_, ...), custom_call_target="tpu_custom_call" | custom-call | flops 9663676416 | bytes 8388608 | tf_op jit(solution)/shard_map/middle/pallas_call | solution.py:264
  448.6 26.6 %all-to-all-done.4 = f32[16,8,16,512]{3,2,1,0:T(8,128)} async-done(((f32[16,8,16,512]{3,2,1,0:T(8,128)}), f32[16,8,16,512]{3,2,1,0:T(8,128)}, u32[]{:S(2)}, u32[]{:S(2)}) %all-to-all-start.4) | async-done | bytes 4194336 | tf_op jit(solution)/shard_map/all_to_all | solution.py:248
  475.2 12.3 %all-to-all-start.1 = ((f32[16,8,16,512]{3,2,1,0:T(8,128)}), f32[16,8,16,512]{3,2,1,0:T(8,128)}, u32[]{:S(2)}, u32[]{:S(2)}) async-start(f32[16,8,16,512]{3,2,1,0:T(8,128)} %middle.3), calls=%async_computation.1 | async-start | bytes 8388608 | tf_op jit(solution)/shard_map/all_to_all | solution.py:248
  487.5 0.1 fusion.7
  487.6 0.1 copy.12
  487.8 0.1 copy.10
  487.9 0.6 fusion.4
  488.5 0.6 fusion.5
  489.1 6.5 %mix.2.refs_0_ = f32[4096,512]{1,0:T(8,128)} custom-call(f32[2048,512]{1,0:T(8,128)} %bitcast.16.field_ref, bf16[128,128]{1,0:T(8,128)(2,1)} %get-tuple-element.36.vh_ref, bf16[128,128]{1,0:T(8,128)(2,1)} %get-tuple-element.35.vl_ref), custom_call_target="tpu_custom_call" | custom-call | flops 805306368 | bytes 8388608 | tf_op jit(solution)/shard_map/mix/pallas_call | solution.py:286
  495.6 35.3 %all-to-all-done.1 = f32[16,8,16,512]{3,2,1,0:T(8,128)} async-done(((f32[16,8,16,512]{3,2,1,0:T(8,128)}), f32[16,8,16,512]{3,2,1,0:T(8,128)}, u32[]{:S(2)}, u32[]{:S(2)}) %all-to-all-start.1) | async-done | bytes 4194336 | tf_op jit(solution)/shard_map/all_to_all | solution.py:248
  530.9 6.5 %mix.3 = f32[4096,512]{1,0:T(8,128)} custom-call(f32[2048,512]{1,0:T(8,128)} %bitcast.11.field_ref, bf16[128,128]{1,0:T(8,128)(2,1)} %get-tuple-element.40.vh_ref, bf16[128,128]{1,0:T(8,128)(2,1)} %get-tuple-element.39.vl_ref, f32[4096,512]{1,0:T(8,128)} %mix.2.refs_0_), custom_call_target="tpu_custom_call", output_to_operand_aliasing={{}: (3, {})} | custom-call | flops 805306368 | bytes 8388608 | tf_op jit(solution)/shard_map/mix/pallas_call | solution.py:286
  (27 shorter events, 0.2 us)
Async XLA Ops:
  4.3 27.6 %collective-permute-start.5 = (f32[4,64,512]{2,1,0:T(8,128)}, f32[4,64,512]{2,1,0:T(8,128)S(1)}, u32[]{:S(2)}, u32[]{:S(2)}) collective-permute-start(f32[4,64,512]{2,1,0:T(8,128)} %get-tuple-element.25), channel_id=1, source_target_pairs={{0,1},{1,2},{2,3},{3,4},{4,5},{5,6},{6,7},{7,8},{8,9},{9,10},{10,1... | collective-permute-start | bytes 1572872 | tf_op jit(solution)/shard_map/ppermute | solution.py:155
  9.2 24.5 %collective-permute-start.6 = (f32[4,64,512]{2,1,0:T(8,128)}, f32[4,64,512]{2,1,0:T(8,128)S(1)}, u32[]{:S(2)}, u32[]{:S(2)}) collective-permute-start(f32[4,64,512]{2,1,0:T(8,128)} %get-tuple-element.26), channel_id=1, source_target_pairs={{1,0},{2,1},{3,2},{4,3},{5,4},{6,5},{7,6},{8,7},{9,8},{10,9},{11,1... | collective-permute-start | bytes 1572872 | tf_op jit(solution)/shard_map/ppermute | solution.py:155
  31.9 1.8 copy-start.2
  33.7 0.8 copy-start.3
  42.9 14.1 %collective-permute-start.7 = (f32[2,64,512]{2,1,0:T(8,128)}, f32[2,64,512]{2,1,0:T(8,128)S(1)}, u32[]{:S(2)}, u32[]{:S(2)}) collective-permute-start(f32[2,64,512]{2,1,0:T(8,128)} %get-tuple-element.28), channel_id=1, source_target_pairs={{0,1},{1,2},{2,3},{3,4},{4,5},{5,6},{6,7},{7,8},{8,9},{9,10},{10,1... | collective-permute-start | bytes 786440 | tf_op jit(solution)/shard_map/ppermute | solution.py:155
  46.3 11.3 %collective-permute-start.8 = (f32[2,64,512]{2,1,0:T(8,128)}, f32[2,64,512]{2,1,0:T(8,128)S(1)}, u32[]{:S(2)}, u32[]{:S(2)}) collective-permute-start(f32[2,64,512]{2,1,0:T(8,128)} %get-tuple-element.29), channel_id=1, source_target_pairs={{1,0},{2,1},{3,2},{4,3},{5,4},{6,5},{7,6},{8,7},{9,8},{10,9},{11,1... | collective-permute-start | bytes 786440 | tf_op jit(solution)/shard_map/ppermute | solution.py:155
  57.0 0.7 copy-start.11
  57.6 0.7 copy-start.13
  67.3 181.0 %all-to-all-start.2 = ((f32[64,16,512]{2,1,0:T(8,128)}), f32[64,16,512]{2,1,0:T(8,128)S(1)}, u32[]{:S(2)}, u32[]{:S(2)}) async-start(f32[64,16,512]{2,1,0:T(8,128)} %bitcast.109), calls=%async_computation.2 | async-start | bytes 4194304 | tf_op jit(solution)/shard_map/all_to_all | solution.py:248
  82.2 44.4 %collective-permute-start = (f32[4,128,512]{2,1,0:T(8,128)}, f32[4,128,512]{2,1,0:T(8,128)S(1)}, u32[]{:S(2)}, u32[]{:S(2)}) collective-permute-start(f32[4,128,512]{2,1,0:T(8,128)} %get-tuple-element.20), channel_id=1, source_target_pairs={{0,1},{1,2},{2,3},{3,4},{4,5},{5,6},{6,7},{7,8},{8,9},{9,10},{10,1... | collective-permute-start | bytes 3145736 | tf_op jit(solution)/shard_map/ppermute | solution.py:155
  86.1 43.2 %collective-permute-start.1 = (f32[4,128,512]{2,1,0:T(8,128)}, f32[4,128,512]{2,1,0:T(8,128)S(1)}, u32[]{:S(2)}, u32[]{:S(2)}) collective-permute-start(f32[4,128,512]{2,1,0:T(8,128)} %get-tuple-element.21), channel_id=1, source_target_pairs={{1,0},{2,1},{3,2},{4,3},{5,4},{6,5},{7,6},{8,7},{9,8},{10,9},{11,1... | collective-permute-start | bytes 3145736 | tf_op jit(solution)/shard_map/ppermute | solution.py:155
  126.6 2.7 copy-start
  129.3 1.0 copy-start.1
  145.8 12.3 %collective-permute-start.2 = (f32[2,128,512]{2,1,0:T(8,128)}, f32[2,128,512]{2,1,0:T(8,128)S(1)}, u32[]{:S(2)}, u32[]{:S(2)}) collective-permute-start(f32[2,128,512]{2,1,0:T(8,128)} %get-tuple-element.23), channel_id=1, source_target_pairs={{0,1},{1,2},{2,3},{3,4},{4,5},{5,6},{6,7},{7,8},{8,9},{9,10},{10,1... | collective-permute-start | bytes 1572872 | tf_op jit(solution)/shard_map/ppermute | solution.py:155
  149.4 18.6 %collective-permute-start.3 = (f32[2,128,512]{2,1,0:T(8,128)}, f32[2,128,512]{2,1,0:T(8,128)S(1)}, u32[]{:S(2)}, u32[]{:S(2)}) collective-permute-start(f32[2,128,512]{2,1,0:T(8,128)} %get-tuple-element.24), channel_id=1, source_target_pairs={{1,0},{2,1},{3,2},{4,3},{5,4},{6,5},{7,6},{8,7},{9,8},{10,9},{11,1... | collective-permute-start | bytes 1572872 | tf_op jit(solution)/shard_map/ppermute | solution.py:155
  158.1 9.8 %copy-start.8 = (f32[2,128,512]{2,1,0:T(8,128)}, f32[2,128,512]{2,1,0:T(8,128)S(1)}, u32[]{:S(2)}) copy-start(f32[2,128,512]{2,1,0:T(8,128)S(1)} %collective-permute-done.2.refs_10_) | copy-start | bytes 1572868
  167.9 0.8 copy-start.9
  184.6 87.2 %collective-permute-start.4 = (f32[128,16,512]{2,1,0:T(8,128)}, f32[128,16,512]{2,1,0:T(8,128)}, u32[]{:S(2)}, u32[]{:S(2)}) collective-permute-start(f32[128,16,512]{2,1,0:T(8,128)} %bitcast.111), channel_id=1, source_target_pairs={{0,16},{1,17},{2,18},{3,19},{4,20},{5,21},{6,22},{7,23},{8,24},{9,... | collective-permute-start | bytes 12582920 | tf_op jit(solution)/shard_map/ppermute | solution.py:158
  192.4 21.6 %collective-permute-start.9 = (f32[4,64,512]{2,1,0:T(8,128)}, f32[4,64,512]{2,1,0:T(8,128)S(1)}, u32[]{:S(2)}, u32[]{:S(2)}) collective-permute-start(f32[4,64,512]{2,1,0:T(8,128)} %get-tuple-element.30), channel_id=1, source_target_pairs={{0,1},{1,2},{2,3},{3,4},{4,5},{5,6},{6,7},{7,8},{8,9},{9,10},{10,1... | collective-permute-start | bytes 1572872 | tf_op jit(solution)/shard_map/ppermute | solution.py:155
  193.9 21.6 %collective-permute-start.10 = (f32[4,64,512]{2,1,0:T(8,128)}, f32[4,64,512]{2,1,0:T(8,128)S(1)}, u32[]{:S(2)}, u32[]{:S(2)}) collective-permute-start(f32[4,64,512]{2,1,0:T(8,128)} %get-tuple-element.31), channel_id=1, source_target_pairs={{1,0},{2,1},{3,2},{4,3},{5,4},{6,5},{7,6},{8,7},{9,8},{10,9},{11,1... | collective-permute-start | bytes 1572872 | tf_op jit(solution)/shard_map/ppermute | solution.py:155
  213.9 1.6 copy-start.4
  215.5 0.8 copy-start.5
  224.7 8.5 %collective-permute-start.11 = (f32[2,64,512]{2,1,0:T(8,128)}, f32[2,64,512]{2,1,0:T(8,128)S(1)}, u32[]{:S(2)}, u32[]{:S(2)}) collective-permute-start(f32[2,64,512]{2,1,0:T(8,128)} %get-tuple-element.33), channel_id=1, source_target_pairs={{0,1},{1,2},{2,3},{3,4},{4,5},{5,6},{6,7},{7,8},{8,9},{9,10},{10,1... | collective-permute-start | bytes 786440 | tf_op jit(solution)/shard_map/ppermute | solution.py:155
  229.1 9.5 %collective-permute-start.12 = (f32[2,64,512]{2,1,0:T(8,128)}, f32[2,64,512]{2,1,0:T(8,128)S(1)}, u32[]{:S(2)}, u32[]{:S(2)}) collective-permute-start(f32[2,64,512]{2,1,0:T(8,128)} %get-tuple-element.34), channel_id=1, source_target_pairs={{1,0},{2,1},{3,2},{4,3},{5,4},{6,5},{7,6},{8,7},{9,8},{10,9},{11,1... | collective-permute-start | bytes 786440 | tf_op jit(solution)/shard_map/ppermute | solution.py:155
  233.2 5.4 copy-start.10
  238.6 0.7 copy-start.12
  248.3 30.4 %copy-start.6 = (f32[64,16,512]{2,1,0:T(8,128)}, f32[64,16,512]{2,1,0:T(8,128)S(1)}, u32[]{:S(2)}) copy-start(f32[64,16,512]{2,1,0:T(8,128)S(1)} %all-to-all-done.2) | copy-start | bytes 6291460
  248.3 75.9 %all-to-all-start.3 = ((f32[64,16,512]{2,1,0:T(8,128)}), f32[64,16,512]{2,1,0:T(8,128)}, u32[]{:S(2)}, u32[]{:S(2)}) async-start(f32[64,16,512]{2,1,0:T(8,128)} %bitcast.110), calls=%async_computation.3 | async-start | bytes 4194304 | tf_op jit(solution)/shard_map/all_to_all | solution.py:248
  324.2 84.4 %all-to-all-start = ((f32[128,16,512]{2,1,0:T(8,128)}), f32[128,16,512]{2,1,0:T(8,128)}, u32[]{:S(2)}, u32[]{:S(2)}) async-start(f32[128,16,512]{2,1,0:T(8,128)} %bitcast_subtract_fusion), calls=%async_computation | async-start | bytes 8388608 | tf_op jit(solution)/shard_map/all_to_all | solution.py:248
  408.6 66.6 %all-to-all-start.4 = ((f32[16,8,16,512]{3,2,1,0:T(8,128)}), f32[16,8,16,512]{3,2,1,0:T(8,128)}, u32[]{:S(2)}, u32[]{:S(2)}) async-start(f32[16,8,16,512]{3,2,1,0:T(8,128)} %middle.5), calls=%async_computation.4 | async-start | bytes 8388608 | tf_op jit(solution)/shard_map/all_to_all | solution.py:248
  448.6 38.9 %copy-start.7 = (f32[128,128]{1,0:T(8,128)S(1)}, f32[128,128]{1,0:T(8,128)}, u32[]{:S(2)}) copy-start(f32[128,128]{1,0:T(8,128)} %param.9) | copy-start | bytes 196612
  475.2 55.7 %all-to-all-start.1 = ((f32[16,8,16,512]{3,2,1,0:T(8,128)}), f32[16,8,16,512]{3,2,1,0:T(8,128)}, u32[]{:S(2)}, u32[]{:S(2)}) async-start(f32[16,8,16,512]{3,2,1,0:T(8,128)} %middle.3), calls=%async_computation.1 | async-start | bytes 8388608 | tf_op jit(solution)/shard_map/all_to_all | solution.py:248

commit v3 on v2

--- a/solution.py
+++ b/solution.py
@@ -12,6 +12,7 @@
 DIFFUSION = 0.2
 CUTS_LAST = (4, 8)
 CUTS_FIRST = (8,)
+HOLD = 0
 
 
 def dct_table(count):
@@ -37,23 +38,37 @@
     return dot(left[0], right[0]) + (dot(left[0], right[1]) + dot(left[1], right[0]))
 
 
-def stepped(center, north, south, half_x, half_y):
+def beside(center):
     cols = center.shape[1]
     lane = lax.broadcasted_iota(jnp.int32, center.shape, 1)
     east = jnp.where(lane == cols - 1, 0.0, pltpu.roll(center, cols - 1, 1))
     west = jnp.where(lane == 0, 0.0, pltpu.roll(center, 1, 1))
+    return east, west
+
+
+def stepped(center, north, south, half_x, half_y):
+    east, west = beside(center)
     total = (north + south) + (east + west) + center
     return DIFFUSION * total - half_x * (north - south) - half_y * (east - west)
 
 
+def offered(center, inner, half_x, half_y, sign):
+    east, west = beside(center)
+    return DIFFUSION * (center + (east + west) + inner) + sign * half_x * inner - half_y * (east - west)
+
+
 def edge_kernel(inc_b, cx_b, cy_b, inc_t, cx_t, cy_t, low, high):
-    low[0], low[1] = inc_b[:, 6, :], inc_b[:, 7, :]
-    low[2], low[3] = cx_b[:, 7, :], cy_b[:, 7, :]
-    high[0], high[1] = inc_t[:, 0, :], inc_t[:, 1, :]
-    high[2], high[3] = cx_t[:, 0, :], cy_t[:, 0, :]
-
-
-def tangent_kernel(rows, parts, first, last, *refs):
+    half_x, half_y = 0.5 * cx_b[:, 7, :], 0.5 * cy_b[:, 7, :]
+    low[0] = inc_b[:, 7, :]
+    low[1] = offered(inc_b[:, 7, :], inc_b[:, 6, :], half_x, half_y, 1.0)
+    low[2] = DIFFUSION - half_x
+    half_x, half_y = 0.5 * cx_t[:, 0, :], 0.5 * cy_t[:, 0, :]
+    high[0] = inc_t[:, 0, :]
+    high[1] = offered(inc_t[:, 0, :], inc_t[:, 1, :], half_x, half_y, -1.0)
+    high[2] = DIFFUSION + half_x
+
+
+def tangent_kernel(rows, parts, first, last, hold, *refs):
     refs = list(refs)
 
     def take(count):
@@ -61,11 +76,14 @@
         del refs[:count]
         return taken
 
-    (inside,) = take(1)
+    held = take(1) if hold else None
     state = take(parts) if first else take(1)[0]
     cx, cy = take(parts), take(parts)
     before, after = take(2)
-    far_before, far_after = (before, after) if first else take(2)
+    if first:
+        share_before, share_after = before.at[2], after.at[2]
+    else:
+        share_before, share_after = (r.at[0] for r in take(2))
     target = take(parts) if last == "jump" else None
     (out,) = take(1)
     low, high = (None, None) if last else take(2)
@@ -75,36 +93,41 @@
     def gather(pieces, x):
         return jnp.concatenate([p[pl.ds(x, 8, stride=rows), :] for p in pieces], axis=1)
 
+    if hold:
+
+        @pl.when(pl.program_id(0) == 0)
+        def _():
+            def more(_, carry):
+                mid[0] = mid[0] + 1.0
+                return carry
+
+            lax.fori_loop(0, held[0][0], more, 0)
+
     for x in range(rows):
-        old[x + 2] = gather(state, x) if first else state[x]
-        hx[x + 1] = 0.5 * gather(cx, x)
-        hy[x + 1] = 0.5 * gather(cy, x)
-    for h in range(2):
-        old[h] = before[h]
-        old[rows + 2 + h] = after[h]
-    hx[0], hy[0] = 0.5 * far_before[2], 0.5 * far_before[3]
-    hx[rows + 1], hy[rows + 1] = 0.5 * far_after[2], 0.5 * far_after[3]
-    for x in range(rows + 2):
-        new = stepped(old[x + 1], old[x + 2], old[x], hx[x], hy[x])
-        if x == 0:
-            new = new * inside[0]
-        if x == rows + 1:
-            new = new * inside[1]
-        mid[x] = new
+        old[x + 1] = gather(state, x) if first else state[x]
+        hx[x] = 0.5 * gather(cx, x)
+        hy[x] = 0.5 * gather(cy, x)
+    old[0] = before[0]
+    old[rows + 1] = after[0]
+    mid[0] = before[1] + share_before[...] * old[1]
+    mid[rows + 1] = after[1] + share_after[...] * old[rows]
     for x in range(rows):
-        new = stepped(mid[x + 1], mid[x + 2], mid[x], hx[x + 1], hy[x + 1])
+        mid[x + 1] = stepped(old[x + 1], old[x + 2], old[x], hx[x], hy[x])
+    for x in range(rows):
+        new = stepped(mid[x + 1], mid[x + 2], mid[x], hx[x], hy[x])
         if not last:
             out[x] = new
-            if x < 2:
-                high[x] = new
-            if x >= rows - 2:
-                low[x - rows + 2] = new
         else:
             for i in range(parts):
                 flat[i, pl.ds(x, 8, stride=rows), :] = new[:, at(i)]
     if last:
         for i in range(parts):
             out[:, at(i)] = target[i][...] - flat[i] if target else flat[i]
+    else:
+        low[0] = out[rows - 1]
+        low[1] = offered(out[rows - 1], out[rows - 2], hx[rows - 1], hy[rows - 1], 1.0)
+        high[0] = out[0]
+        high[1] = offered(out[0], out[1], hx[0], hy[0], -1.0)
 
 
 def mid_kernel(block_ref, spectrum_ref, rh, rl, rth, rtl, ch, cl, cth, ctl, out_ref):
@@ -145,7 +168,6 @@
 def on_device(increments, courant_x, courant_y, spectrum, vertical):
     subs, levels, rows, cols = increments.shape
     bricks, groups = lax.axis_size("brick"), lax.axis_size("sub")
-    brick = lax.axis_index("brick")
     f32 = jnp.float32
 
     def neighbour(value, by, part_of_end):
@@ -165,7 +187,7 @@
 
     parts = cols // LANES
     flat_all = [a.reshape(-1, cols) for a in (increments, courant_x, courant_y)]
-    inside = jnp.stack([jnp.where(brick > 0, 1.0, 0.0), jnp.where(brick < bricks - 1, 1.0, 0.0)]).astype(f32)
+    late = (lax.axis_index("sub") % 2 * HOLD).astype(jnp.int32).reshape(1)
 
     def pieces(array, sub, start):
         specs = [
@@ -181,19 +203,19 @@
             edge_kernel,
             grid=((stop - start) // size,),
             in_specs=[block(rows // 8 - 1)] * 3 + [block(0)] * 3,
-            out_specs=[pl.BlockSpec((4, size, cols), lambda i: (0, i, 0))] * 2,
-            out_shape=[jax.ShapeDtypeStruct((4, stop - start, cols), f32)] * 2,
+            out_specs=[pl.BlockSpec((3, size, cols), lambda i: (0, i, 0))] * 2,
+            out_shape=[jax.ShapeDtypeStruct((3, stop - start, cols), f32)] * 2,
             compiler_params=params(),
             cost_estimate=pl.CostEstimate(flops=0, bytes_accessed=200 * (stop - start) * cols, transcendentals=0),
             name="edge",
         )(*arrays, *arrays)
 
-    def tangent(number, sub, start, stop, state, halo, far, target):
+    def tangent(number, sub, start, stop, state, halo, far, target, hold):
         span = stop - start
         first = number == 0
         last = None if first else ("end" if target is None else "jump")
         slab = pl.BlockSpec((rows, 8, cols), lambda i: (0, i, 0))
-        inputs, specs = [inside], [pl.BlockSpec(memory_space=pltpu.SMEM)]
+        inputs, specs = ([late], [pl.BlockSpec(memory_space=pltpu.SMEM)]) if hold else ([], [])
 
         def add(more, with_specs):
             inputs.extend(more)
@@ -205,8 +227,9 @@
             add([state], [slab])
         add(*pieces(flat_all[1], sub, start))
         add(*pieces(flat_all[2], sub, start))
-        for pair in (halo,) if first else (halo, far):
-            add(pair, [pl.BlockSpec((pair[0].shape[0], 8, cols), lambda i: (0, i, 0))] * 2)
+        add(halo, [pl.BlockSpec((halo[0].shape[0], 8, cols), lambda i: (0, i, 0))] * 2)
+        if not first:
+            add(far, [pl.BlockSpec((1, 8, cols), lambda i: (2, i, 0))] * 2)
         if last == "jump":
             add(*pieces(flat_all[0], target, start))
         if first:
@@ -215,16 +238,16 @@
         else:
             out, out_spec = [(span * rows, cols)], [pl.BlockSpec((8 * rows, cols), lambda i: (i, 0))]
         return pl.pallas_call(
-            functools.partial(tangent_kernel, rows, parts, first, last),
+            functools.partial(tangent_kernel, rows, parts, first, last, hold),
             grid=(span // 8,),
             in_specs=specs,
             out_specs=out_spec,
             out_shape=[jax.ShapeDtypeStruct(o, f32) for o in out],
             scratch_shapes=[
-                pltpu.VMEM((rows + 4, 8, cols), f32),
                 pltpu.VMEM((rows + 2, 8, cols), f32),
                 pltpu.VMEM((rows + 2, 8, cols), f32),
-                pltpu.VMEM((rows + 2, 8, cols), f32),
+                pltpu.VMEM((rows, 8, cols), f32),
+                pltpu.VMEM((rows, 8, cols), f32),
                 pltpu.VMEM((parts, 8 * rows, LANES), f32),
             ],
             compiler_params=params(),
@@ -232,13 +255,13 @@
             name="tangent",
         )(*inputs)
 
-    def advance(sub, target, start, stop):
+    def advance(sub, target, start, stop, hold):
         low, high = edges(sub, start, stop)
         last = sub == subs - 1
         far = neighbour(low, 1, last), neighbour(high, -1, last)
-        state, low, high = tangent(0, sub, start, stop, None, far, far, None)
+        state, low, high = tangent(0, sub, start, stop, None, far, far, None, False)
         near = neighbour(low, 1, last), neighbour(high, -1, last)
-        (moved,) = tangent(1, sub, start, stop, state, near, far, target)
+        (moved,) = tangent(1, sub, start, stop, state, near, far, target, HOLD > 0 and hold)
         moved = moved.reshape(-1, rows, cols)
         if target is None:
             moved = increments[0, start:stop] - next_sub(moved)
@@ -300,7 +323,7 @@
     out = None
     work = {}
     for name, sub, target, start, stop in jobs_of(subs, levels, bricks):
-        moved = advance(sub, target, start, stop)
+        moved = advance(sub, target, start, stop, not work)
         block = spread(moved)
         work.setdefault(0 if target is None else target, []).append((name, start, stop, block))
     returned = []

time: 548 us -> 537 us (0.980)
  waiting for transfers between devices: 269 us -> 257 us
    ppermute x12, waiting for transfers between devices: 120 us -> 108 us  [neighbour(): return lax.ppermute(value, ('sub', 'brick'), pairs)]
  transfers between devices with their start and end apart: 18 -> 18, of which waited for: 16 -> 16; matrix products, arithmetic and copies ran while one was open for 4% -> 4% of each run, Pallas kernels for 19% -> 20%
where the time goes in v3:
time: 537 us; the launch traced here: 526 us
  waiting for transfers between devices  257 us (48%)
  Pallas kernels  132 us (25%)
  starting transfers between devices  112 us (21%)
  other arithmetic  19.1 us (4%)
    all_to_all x5, waiting for transfers between devices, spread(): lax.all_to_all(value, 'brick', split_axis=0, concat_axis=0, tiled=True)  148 us
    ppermute x12, waiting for transfers between devices, neighbour(): return lax.ppermute(value, ('sub', 'brick'), pairs)  108 us
    all_to_all x5, starting transfers between devices, spread(): lax.all_to_all(value, 'brick', split_axis=0, concat_axis=0, tiled=True)  81.1 us
    pallas_call x6, Pallas kernels, tangent(): pl.pallas_call(functools.partial(tangent_kernel, rows, parts, first, last...  65.5 us
    pallas_call x3, Pallas kernels, middle(): pl.pallas_call(kernel, grid=(share,), in_specs=specs, out_specs=pl.BlockS...  37.2 us
    ppermute x12, starting transfers between devices, neighbour(): return lax.ppermute(value, ('sub', 'brick'), pairs)  28 us
    pallas_call x3, Pallas kernels, edges(): pl.pallas_call(edge_kernel, grid=((stop - start) // size,), in_specs=[blo...  16.6 us
    pallas_call x2, Pallas kernels, mix(): pl.pallas_call(kernel, grid=(parts,), in_specs=specs, out_specs=pl.BlockS...  12.9 us
  transfers between devices with their start and end apart: 18, of which 16 were waited for; matrix products, arithmetic and copies ran while one was open for 4% of the time, Pallas kernels for 20%

profile of v3, /device:TPU:0, one launch (start us, length us, event | category | flops | bytes accessed | tf_op | source)
XLA Modules:
  0.0 526.0 jit_solution(6204850048588232639)
XLA Ops:
  0.0 4.4 edge.4
  4.4 4.9 collective-permute-start.5
  9.3 1.3 collective-permute-start.6
  10.6 15.8 %collective-permute-done.5.refs_12_.refs_11_ = f32[3,64,512]{2,1,0:T(8,128)S(1)} collective-permute-done((f32[3,64,512]{2,1,0:T(8,128)}, f32[3,64,512]{2,1,0:T(8,128)S(1)}, u32[]{:S(2)}, u32[]{:S(2)}) %collective-permute-start.5) | collective-permute-done | bytes 393248 | tf_op jit(solution)/shard_map/ppermute | solution.py:177
  26.4 1.8 collective-permute-done.6.refs_13_.refs_12_
  28.2 0.7 copy-done.5
  28.9 8.5 %tangent.8 = (f32[16,64,512]{2,1,0:T(8,128)}, f32[2,64,512]{2,1,0:T(8,128)}, f32[2,64,512]{2,1,0:T(8,128)}) custom-call(f32[4096,512]{1,0:T(8,128)} %bitcast.83, f32[4096,512]{1,0:T(8,128)} %bitcast.84, f32[4096,512]{1,0:T(8,128)} %bitcast.85, f32[4096,512]{1,0:T(8,128)} %bitcast.86, f32[4096,512]{1,0:T(8,128)} %bitcast.23, f32[4096,512]{1,0:T(8,128)} %bitcast.24, ...), custom_call_target="tpu_custom_call" | custom-call | flops 20971520 | bytes 16777216 | tf_op jit(solution)/shard_map/tangent/pallas_call | solution.py:240
  37.5 3.4 collective-permute-start.7
  40.9 1.3 collective-permute-start.8
  42.2 9.3 %collective-permute-done.7.refs_9_ = f32[2,64,512]{2,1,0:T(8,128)S(1)} collective-permute-done((f32[2,64,512]{2,1,0:T(8,128)}, f32[2,64,512]{2,1,0:T(8,128)S(1)}, u32[]{:S(2)}, u32[]{:S(2)}) %collective-permute-start.7) | collective-permute-done | bytes 262176 | tf_op jit(solution)/shard_map/ppermute | solution.py:177
  51.5 0.6 collective-permute-done.8.refs_10_
  52.1 0.1 copy-done.10
  52.2 0.6 copy-done.12
  52.8 8.7 %tangent.9 = f32[1024,512]{1,0:T(8,128)} custom-call(f32[16,64,512]{2,1,0:T(8,128)} %get-tuple-element.27.refs_0_, f32[4096,512]{1,0:T(8,128)} %bitcast.27, f32[4096,512]{1,0:T(8,128)} %bitcast.28, f32[4096,512]{1,0:T(8,128)} %bitcast.29, f32[4096,512]{1,0:T(8,128)} %bitcast.30, f32[4096,512]{1,0:T(8,128)} %bitcast.57, f32[4096,512]{1,0:T(8,128)} %bitcast.58, ...), custom_call_target="tpu_custom_call" | custom-call | flops 20971520 | bytes 16777216 | tf_op jit(solution)/shard_map/tangent/pallas_call | solution.py:240
  61.6 7.1 %all-to-all-start.2 = ((f32[64,16,512]{2,1,0:T(8,128)}), f32[64,16,512]{2,1,0:T(8,128)S(1)}, u32[]{:S(2)}, u32[]{:S(2)}) async-start(f32[64,16,512]{2,1,0:T(8,128)} %bitcast.107), calls=%async_computation.2 | async-start | bytes 4194304 | tf_op jit(solution)/shard_map/all_to_all | solution.py:271
  68.7 7.8 %edge.3 = (f32[3,128,512]{2,1,0:T(8,128)}, f32[3,128,512]{2,1,0:T(8,128)}) custom-call(f32[256,16,512]{2,1,0:T(8,128)} %bitcast.91, f32[256,16,512]{2,1,0:T(8,128)} %bitcast.31, f32[256,16,512]{2,1,0:T(8,128)} %bitcast.61, f32[256,16,512]{2,1,0:T(8,128)} %bitcast.92, f32[256,16,512]{2,1,0:T(8,128)} %bitcast.32, f32[256,16,512]{2,1,0:T(8,128)} %bitcast.62), custom_call_target="tpu_custom_call" | custom-call | bytes 13107200 | tf_op jit(solution)/shard_map/edge/pallas_call | solution.py:202
  76.5 3.8 collective-permute-start
  80.4 1.3 collective-permute-start.1
  81.7 33.6 %collective-permute-done.refs_12_.refs_11_ = f32[3,128,512]{2,1,0:T(8,128)S(1)} collective-permute-done((f32[3,128,512]{2,1,0:T(8,128)}, f32[3,128,512]{2,1,0:T(8,128)S(1)}, u32[]{:S(2)}, u32[]{:S(2)}) %collective-permute-start) | collective-permute-done | bytes 786464 | tf_op jit(solution)/shard_map/ppermute | solution.py:177
  115.3 2.7 collective-permute-done.1.refs_13_.refs_12_
  118.0 1.0 copy-done.1
  118.9 15.8 %tangent.6 = (f32[16,128,512]{2,1,0:T(8,128)}, f32[2,128,512]{2,1,0:T(8,128)}, f32[2,128,512]{2,1,0:T(8,128)}) custom-call(f32[4096,512]{1,0:T(8,128)} %bitcast.93, f32[4096,512]{1,0:T(8,128)} %bitcast.94, f32[4096,512]{1,0:T(8,128)} %bitcast.95, f32[4096,512]{1,0:T(8,128)} %bitcast.96, f32[4096,512]{1,0:T(8,128)} %bitcast.35, f32[4096,512]{1,0:T(8,128)} %bitcast.34, ...), custom_call_target="tpu_custom_call" | custom-call | flops 41943040 | bytes 33554432 | tf_op jit(solution)/shard_map/tangent/pallas_call | solution.py:240
  134.7 4.4 collective-permute-start.2
  139.1 1.3 collective-permute-start.3
  140.4 14.9 %collective-permute-done.2.refs_9_ = f32[2,128,512]{2,1,0:T(8,128)S(1)} collective-permute-done((f32[2,128,512]{2,1,0:T(8,128)}, f32[2,128,512]{2,1,0:T(8,128)S(1)}, u32[]{:S(2)}, u32[]{:S(2)}) %collective-permute-start.2) | collective-permute-done | bytes 524320 | tf_op jit(solution)/shard_map/ppermute | solution.py:177
  155.3 2.4 collective-permute-done.3.refs_10_
  157.7 0.8 copy-done.9
  158.5 15.3 %tangent.7 = f32[2048,512]{1,0:T(8,128)} custom-call(f32[16,128,512]{2,1,0:T(8,128)} %get-tuple-element.22.refs_0_, f32[4096,512]{1,0:T(8,128)} %bitcast.37, f32[4096,512]{1,0:T(8,128)} %bitcast.38, f32[4096,512]{1,0:T(8,128)} %bitcast.39, f32[4096,512]{1,0:T(8,128)} %bitcast.40, f32[4096,512]{1,0:T(8,128)} %bitcast.67, f32[4096,512]{1,0:T(8,128)} %bitcast.68, ...), custom_call_target="tpu_custom_call" | custom-call | flops 41943040 | bytes 33554432 | tf_op jit(solution)/shard_map/tangent/pallas_call | solution.py:240
  173.8 3.4 collective-permute-start.4
  177.1 4.4 edge.5
  181.5 2.1 collective-permute-start.9
  183.7 1.3 collective-permute-start.10
  185.0 8.8 %collective-permute-done.9.refs_12_.refs_11_ = f32[3,64,512]{2,1,0:T(8,128)S(1)} collective-permute-done((f32[3,64,512]{2,1,0:T(8,128)}, f32[3,64,512]{2,1,0:T(8,128)S(1)}, u32[]{:S(2)}, u32[]{:S(2)}) %collective-permute-start.9) | collective-permute-done | bytes 393248 | tf_op jit(solution)/shard_map/ppermute | solution.py:177
  193.8 8.7 %collective-permute-done.10.refs_13_.refs_12_ = f32[3,64,512]{2,1,0:T(8,128)S(1)} collective-permute-done((f32[3,64,512]{2,1,0:T(8,128)}, f32[3,64,512]{2,1,0:T(8,128)S(1)}, u32[]{:S(2)}, u32[]{:S(2)}) %collective-permute-start.10) | collective-permute-done | bytes 393248 | tf_op jit(solution)/shard_map/ppermute | solution.py:177
  202.5 0.7 copy-done.6
  203.2 8.5 %tangent.10 = (f32[16,64,512]{2,1,0:T(8,128)}, f32[2,64,512]{2,1,0:T(8,128)}, f32[2,64,512]{2,1,0:T(8,128)}) custom-call(f32[4096,512]{1,0:T(8,128)} %bitcast.99, f32[4096,512]{1,0:T(8,128)} %bitcast.100, f32[4096,512]{1,0:T(8,128)} %bitcast.101, f32[4096,512]{1,0:T(8,128)} %bitcast.102, f32[4096,512]{1,0:T(8,128)} %bitcast.43, f32[4096,512]{1,0:T(8,128)} %bitcast.44, ...), custom_call_target="tpu_custom_call" | custom-call | flops 20971520 | bytes 16777216 | tf_op jit(solution)/shard_map/tangent/pallas_call | solution.py:240
  211.7 1.6 collective-permute-start.11
  213.3 1.3 collective-permute-start.12
  214.6 4.9 collective-permute-done.11.refs_9_
  219.5 4.9 collective-permute-done.12.refs_10_
  224.4 0.7 copy-done.13
  225.1 8.7 %tangent.11 = f32[1024,512]{1,0:T(8,128)} custom-call(f32[16,64,512]{2,1,0:T(8,128)} %get-tuple-element.32.refs_0_, f32[4096,512]{1,0:T(8,128)} %bitcast.47, f32[4096,512]{1,0:T(8,128)} %bitcast.48, f32[4096,512]{1,0:T(8,128)} %bitcast.49, f32[4096,512]{1,0:T(8,128)} %bitcast.50, f32[4096,512]{1,0:T(8,128)} %bitcast.77, f32[4096,512]{1,0:T(8,128)} %bitcast.78, ...), custom_call_target="tpu_custom_call" | custom-call | flops 20971520 | bytes 16777216 | tf_op jit(solution)/shard_map/tangent/pallas_call | solution.py:240
  233.9 26.5 %all-to-all-start.3 = ((f32[64,16,512]{2,1,0:T(8,128)}), f32[64,16,512]{2,1,0:T(8,128)}, u32[]{:S(2)}, u32[]{:S(2)}) async-start(f32[64,16,512]{2,1,0:T(8,128)} %bitcast.108), calls=%async_computation.3 | async-start | bytes 4194304 | tf_op jit(solution)/shard_map/all_to_all | solution.py:271
  260.5 7.0 %bitcast_subtract_fusion = f32[128,16,512]{2,1,0:T(8,128)} fusion(f32[128,16,512]{2,1,0:T(8,128)} %collective-permute-done.4, f32[2,128,16,512]{3,2,1,0:T(8,128)} %param.5), kind=kLoop, calls=%fused_computation | loop fusion | flops 1048576 | bytes 12582912 | tf_op jit(solution)/shard_map/sub | solution.py:267
  267.4 45.4 %all-to-all-done.3 = f32[64,16,512]{2,1,0:T(8,128)} async-done(((f32[64,16,512]{2,1,0:T(8,128)}), f32[64,16,512]{2,1,0:T(8,128)}, u32[]{:S(2)}, u32[]{:S(2)}) %all-to-all-start.3) | async-done | bytes 2097184 | tf_op jit(solution)/shard_map/all_to_all | solution.py:271
  312.9 12.3 %all-to-all-start = ((f32[128,16,512]{2,1,0:T(8,128)}), f32[128,16,512]{2,1,0:T(8,128)}, u32[]{:S(2)}, u32[]{:S(2)}) async-start(f32[128,16,512]{2,1,0:T(8,128)} %bitcast_subtract_fusion), calls=%async_computation | async-start | bytes 8388608 | tf_op jit(solution)/shard_map/all_to_all | solution.py:271
  325.2 2.7 fusion.3
  327.9 8.2 %fusion.1 = (bf16[512,512]{1,0:T(8,128)(2,1)}, bf16[512,512]{1,0:T(8,128)(2,1)}, bf16[512,512]{1,0:T(8,128)(2,1)}, bf16[512,512]{1,0:T(8,128)(2,1)}) fusion(f32[512]{0:T(512)S(1)} %get-tuple-element.51, f32[512]{0:T(512)S(1)} %get-tuple-element.52), kind=kLoop, calls=%fused_computation.6 | loop fusion | flops 3670016 | bytes 2101248 | tf_op jit(solution)/shard_map/convert_element_type | solution.py:28
  336.1 10.0 %middle.4.refs_10_ = f32[16,8,16,512]{3,2,1,0:T(8,128)} custom-call(f32[16,4,16,512]{3,2,1,0:T(8,128)} %bitcast.13.block_ref, f32[256,512]{1,0:T(8,128)} %refs_1_.1, bf16[256,256]{1,0:T(8,128)(2,1)} %get-tuple-element.48.rh.refs_2_, bf16[256,256]{1,0:T(8,128)(2,1)} %get-tuple-element.46.rl.refs_3_, bf16[256,256]{1,0:T(8,128)(2,1)} %get-tuple-element.47.rth.refs_4_, ...), custom_call_target="tpu_custom_call" | custom-call | flops 4831838208 | bytes 4194304 | tf_op jit(solution)/shard_map/middle/pallas_call | solution.py:287
  346.1 10.0 %middle.5 = f32[16,8,16,512]{3,2,1,0:T(8,128)} custom-call(f32[16,4,16,512]{3,2,1,0:T(8,128)} %bitcast.110, f32[256,512]{1,0:T(8,128)} %refs_1_.1, bf16[256,256]{1,0:T(8,128)(2,1)} %get-tuple-element.48.rh.refs_2_, bf16[256,256]{1,0:T(8,128)(2,1)} %get-tuple-element.46.rl.refs_3_, ...), custom_call_target="tpu_custom_call", output_to_operand_aliasing={{}: (10, {})} | custom-call | flops 4831838208 | bytes 4194304 | tf_op jit(solution)/shard_map/middle/pallas_call | solution.py:287
  356.1 41.1 %all-to-all-done = f32[128,16,512]{2,1,0:T(8,128)} async-done(((f32[128,16,512]{2,1,0:T(8,128)}), f32[128,16,512]{2,1,0:T(8,128)}, u32[]{:S(2)}, u32[]{:S(2)}) %all-to-all-start) | async-done | bytes 4194336 | tf_op jit(solution)/shard_map/all_to_all | solution.py:271
  397.2 22.8 %all-to-all-start.4 = ((f32[16,8,16,512]{3,2,1,0:T(8,128)}), f32[16,8,16,512]{3,2,1,0:T(8,128)}, u32[]{:S(2)}, u32[]{:S(2)}) async-start(f32[16,8,16,512]{3,2,1,0:T(8,128)} %middle.5), calls=%async_computation.4 | async-start | bytes 8388608 | tf_op jit(solution)/shard_map/all_to_all | solution.py:271
  420.1 17.2 %middle.3 = f32[16,8,16,512]{3,2,1,0:T(8,128)} custom-call(f32[16,8,16,512]{3,2,1,0:T(8,128)} %bitcast.8.block_ref, f32[256,512]{1,0:T(8,128)} %refs_1_.1, bf16[256,256]{1,0:T(8,128)(2,1)} %get-tuple-element.48.rh.refs_2_, bf16[256,256]{1,0:T(8,128)(2,1)} %get-tuple-element.46.rl.refs_3_, bf16[256,256]{1,0:T(8,128)(2,1)} %get-tuple-element.47.rth.refs_4_, ...), custom_call_target="tpu_custom_call" | custom-call | flops 9663676416 | bytes 8388608 | tf_op jit(solution)/shard_map/middle/pallas_call | solution.py:287
  437.3 26.6 %all-to-all-done.4 = f32[16,8,16,512]{3,2,1,0:T(8,128)} async-done(((f32[16,8,16,512]{3,2,1,0:T(8,128)}), f32[16,8,16,512]{3,2,1,0:T(8,128)}, u32[]{:S(2)}, u32[]{:S(2)}) %all-to-all-start.4) | async-done | bytes 4194336 | tf_op jit(solution)/shard_map/all_to_all | solution.py:271
  463.9 12.3 %all-to-all-start.1 = ((f32[16,8,16,512]{3,2,1,0:T(8,128)}), f32[16,8,16,512]{3,2,1,0:T(8,128)}, u32[]{:S(2)}, u32[]{:S(2)}) async-start(f32[16,8,16,512]{3,2,1,0:T(8,128)} %middle.3), calls=%async_computation.1 | async-start | bytes 8388608 | tf_op jit(solution)/shard_map/all_to_all | solution.py:271
  476.1 0.1 fusion.7
  476.2 0.1 copy.13
  476.3 0.1 copy.12
  476.4 0.1 copy.10
  476.5 0.6 fusion.4
  477.2 0.6 fusion.5
  477.8 6.5 %mix.2.refs_0_ = f32[4096,512]{1,0:T(8,128)} custom-call(f32[2048,512]{1,0:T(8,128)} %bitcast.14.field_ref, bf16[128,128]{1,0:T(8,128)(2,1)} %get-tuple-element.36.vh_ref, bf16[128,128]{1,0:T(8,128)(2,1)} %get-tuple-element.35.vl_ref), custom_call_target="tpu_custom_call" | custom-call | flops 805306368 | bytes 8388608 | tf_op jit(solution)/shard_map/mix/pallas_call | solution.py:309
  484.2 35.3 %all-to-all-done.1 = f32[16,8,16,512]{3,2,1,0:T(8,128)} async-done(((f32[16,8,16,512]{3,2,1,0:T(8,128)}), f32[16,8,16,512]{3,2,1,0:T(8,128)}, u32[]{:S(2)}, u32[]{:S(2)}) %all-to-all-start.1) | async-done | bytes 4194336 | tf_op jit(solution)/shard_map/all_to_all | solution.py:271
  519.5 6.5 %mix.3 = f32[4096,512]{1,0:T(8,128)} custom-call(f32[2048,512]{1,0:T(8,128)} %bitcast.9.field_ref, bf16[128,128]{1,0:T(8,128)(2,1)} %get-tuple-element.40.vh_ref, bf16[128,128]{1,0:T(8,128)(2,1)} %get-tuple-element.39.vl_ref, f32[4096,512]{1,0:T(8,128)} %mix.2.refs_0_), custom_call_target="tpu_custom_call", output_to_operand_aliasing={{}: (3, {})} | custom-call | flops 805306368 | bytes 8388608 | tf_op jit(solution)/shard_map/mix/pallas_call | solution.py:309
  (26 shorter events, 0.1 us)
Async XLA Ops:
  4.4 22.0 %collective-permute-start.5 = (f32[3,64,512]{2,1,0:T(8,128)}, f32[3,64,512]{2,1,0:T(8,128)S(1)}, u32[]{:S(2)}, u32[]{:S(2)}) collective-permute-start(f32[3,64,512]{2,1,0:T(8,128)} %get-tuple-element.25), channel_id=1, source_target_pairs={{0,1},{1,2},{2,3},{3,4},{4,5},{5,6},{6,7},{7,8},{8,9},{9,10},{10,1... | collective-permute-start | bytes 1179656 | tf_op jit(solution)/shard_map/ppermute | solution.py:177
  9.3 18.9 %collective-permute-start.6 = (f32[3,64,512]{2,1,0:T(8,128)}, f32[3,64,512]{2,1,0:T(8,128)S(1)}, u32[]{:S(2)}, u32[]{:S(2)}) collective-permute-start(f32[3,64,512]{2,1,0:T(8,128)} %get-tuple-element.26), channel_id=1, source_target_pairs={{1,0},{2,1},{3,2},{4,3},{5,4},{6,5},{7,6},{8,7},{9,8},{10,9},{11,1... | collective-permute-start | bytes 1179656 | tf_op jit(solution)/shard_map/ppermute | solution.py:177
  26.4 1.8 copy-start.3
  28.2 0.7 copy-start.5
  37.5 14.1 %collective-permute-start.7 = (f32[2,64,512]{2,1,0:T(8,128)}, f32[2,64,512]{2,1,0:T(8,128)S(1)}, u32[]{:S(2)}, u32[]{:S(2)}) collective-permute-start(f32[2,64,512]{2,1,0:T(8,128)} %get-tuple-element.28), channel_id=1, source_target_pairs={{0,1},{1,2},{2,3},{3,4},{4,5},{5,6},{6,7},{7,8},{8,9},{9,10},{10,1... | collective-permute-start | bytes 786440 | tf_op jit(solution)/shard_map/ppermute | solution.py:177
  40.9 11.3 %collective-permute-start.8 = (f32[2,64,512]{2,1,0:T(8,128)}, f32[2,64,512]{2,1,0:T(8,128)S(1)}, u32[]{:S(2)}, u32[]{:S(2)}) collective-permute-start(f32[2,64,512]{2,1,0:T(8,128)} %get-tuple-element.29), channel_id=1, source_target_pairs={{1,0},{2,1},{3,2},{4,3},{5,4},{6,5},{7,6},{8,7},{9,8},{10,9},{11,1... | collective-permute-start | bytes 786440 | tf_op jit(solution)/shard_map/ppermute | solution.py:177
  51.5 0.7 copy-start.10
  52.1 0.7 copy-start.12
  61.6 172.3 %all-to-all-start.2 = ((f32[64,16,512]{2,1,0:T(8,128)}), f32[64,16,512]{2,1,0:T(8,128)S(1)}, u32[]{:S(2)}, u32[]{:S(2)}) async-start(f32[64,16,512]{2,1,0:T(8,128)} %bitcast.107), calls=%async_computation.2 | async-start | bytes 4194304 | tf_op jit(solution)/shard_map/all_to_all | solution.py:271
  76.5 38.7 %collective-permute-start = (f32[3,128,512]{2,1,0:T(8,128)}, f32[3,128,512]{2,1,0:T(8,128)S(1)}, u32[]{:S(2)}, u32[]{:S(2)}) collective-permute-start(f32[3,128,512]{2,1,0:T(8,128)} %get-tuple-element.20), channel_id=1, source_target_pairs={{0,1},{1,2},{2,3},{3,4},{4,5},{5,6},{6,7},{7,8},{8,9},{9,10},{10,1... | collective-permute-start | bytes 2359304 | tf_op jit(solution)/shard_map/ppermute | solution.py:177
  80.4 37.6 %collective-permute-start.1 = (f32[3,128,512]{2,1,0:T(8,128)}, f32[3,128,512]{2,1,0:T(8,128)S(1)}, u32[]{:S(2)}, u32[]{:S(2)}) collective-permute-start(f32[3,128,512]{2,1,0:T(8,128)} %get-tuple-element.21), channel_id=1, source_target_pairs={{1,0},{2,1},{3,2},{4,3},{5,4},{6,5},{7,6},{8,7},{9,8},{10,9},{11,1... | collective-permute-start | bytes 2359304 | tf_op jit(solution)/shard_map/ppermute | solution.py:177
  115.3 2.7 copy-start
  118.0 1.0 copy-start.1
  134.7 20.6 %collective-permute-start.2 = (f32[2,128,512]{2,1,0:T(8,128)}, f32[2,128,512]{2,1,0:T(8,128)S(1)}, u32[]{:S(2)}, u32[]{:S(2)}) collective-permute-start(f32[2,128,512]{2,1,0:T(8,128)} %get-tuple-element.23), channel_id=1, source_target_pairs={{0,1},{1,2},{2,3},{3,4},{4,5},{5,6},{6,7},{7,8},{8,9},{9,10},{10,1... | collective-permute-start | bytes 1572872 | tf_op jit(solution)/shard_map/ppermute | solution.py:177
  139.1 18.6 %collective-permute-start.3 = (f32[2,128,512]{2,1,0:T(8,128)}, f32[2,128,512]{2,1,0:T(8,128)S(1)}, u32[]{:S(2)}, u32[]{:S(2)}) collective-permute-start(f32[2,128,512]{2,1,0:T(8,128)} %get-tuple-element.24), channel_id=1, source_target_pairs={{1,0},{2,1},{3,2},{4,3},{5,4},{6,5},{7,6},{8,7},{9,8},{10,9},{11,1... | collective-permute-start | bytes 1572872 | tf_op jit(solution)/shard_map/ppermute | solution.py:177
  155.3 2.4 copy-start.8
  157.7 0.8 copy-start.9
  173.8 86.7 %collective-permute-start.4 = (f32[128,16,512]{2,1,0:T(8,128)}, f32[128,16,512]{2,1,0:T(8,128)}, u32[]{:S(2)}, u32[]{:S(2)}) collective-permute-start(f32[128,16,512]{2,1,0:T(8,128)} %bitcast.109), channel_id=1, source_target_pairs={{0,16},{1,17},{2,18},{3,19},{4,20},{5,21},{6,22},{7,23},{8,24},{9,... | collective-permute-start | bytes 12582920 | tf_op jit(solution)/shard_map/ppermute | solution.py:180
  181.5 12.3 %collective-permute-start.9 = (f32[3,64,512]{2,1,0:T(8,128)}, f32[3,64,512]{2,1,0:T(8,128)S(1)}, u32[]{:S(2)}, u32[]{:S(2)}) collective-permute-start(f32[3,64,512]{2,1,0:T(8,128)} %get-tuple-element.30), channel_id=1, source_target_pairs={{0,1},{1,2},{2,3},{3,4},{4,5},{5,6},{6,7},{7,8},{8,9},{9,10},{10,1... | collective-permute-start | bytes 1179656 | tf_op jit(solution)/shard_map/ppermute | solution.py:177
  183.7 18.8 %collective-permute-start.10 = (f32[3,64,512]{2,1,0:T(8,128)}, f32[3,64,512]{2,1,0:T(8,128)S(1)}, u32[]{:S(2)}, u32[]{:S(2)}) collective-permute-start(f32[3,64,512]{2,1,0:T(8,128)} %get-tuple-element.31), channel_id=1, source_target_pairs={{1,0},{2,1},{3,2},{4,3},{5,4},{6,5},{7,6},{8,7},{9,8},{10,9},{11,1... | collective-permute-start | bytes 1179656 | tf_op jit(solution)/shard_map/ppermute | solution.py:177
  193.8 8.7 %copy-start.4 = (f32[3,64,512]{2,1,0:T(8,128)}, f32[3,64,512]{2,1,0:T(8,128)S(1)}, u32[]{:S(2)}) copy-start(f32[3,64,512]{2,1,0:T(8,128)S(1)} %collective-permute-done.9.refs_12_.refs_11_) | copy-start | bytes 1179652
  202.5 0.7 copy-start.6
  211.7 7.8 %collective-permute-start.11 = (f32[2,64,512]{2,1,0:T(8,128)}, f32[2,64,512]{2,1,0:T(8,128)S(1)}, u32[]{:S(2)}, u32[]{:S(2)}) collective-permute-start(f32[2,64,512]{2,1,0:T(8,128)} %get-tuple-element.33), channel_id=1, source_target_pairs={{0,1},{1,2},{2,3},{3,4},{4,5},{5,6},{6,7},{7,8},{8,9},{9,10},{10,1... | collective-permute-start | bytes 786440 | tf_op jit(solution)/shard_map/ppermute | solution.py:177
  213.3 11.1 %collective-permute-start.12 = (f32[2,64,512]{2,1,0:T(8,128)}, f32[2,64,512]{2,1,0:T(8,128)S(1)}, u32[]{:S(2)}, u32[]{:S(2)}) collective-permute-start(f32[2,64,512]{2,1,0:T(8,128)} %get-tuple-element.34), channel_id=1, source_target_pairs={{1,0},{2,1},{3,2},{4,3},{5,4},{6,5},{7,6},{8,7},{9,8},{10,9},{11,1... | collective-permute-start | bytes 786440 | tf_op jit(solution)/shard_map/ppermute | solution.py:177
  219.5 4.9 copy-start.11
  224.4 0.7 copy-start.13
  233.9 33.5 %copy-start.2 = (f32[64,16,512]{2,1,0:T(8,128)}, f32[64,16,512]{2,1,0:T(8,128)S(1)}, u32[]{:S(2)}) copy-start(f32[64,16,512]{2,1,0:T(8,128)S(1)} %all-to-all-done.2) | copy-start | bytes 6291460
  233.9 78.9 %all-to-all-start.3 = ((f32[64,16,512]{2,1,0:T(8,128)}), f32[64,16,512]{2,1,0:T(8,128)}, u32[]{:S(2)}, u32[]{:S(2)}) async-start(f32[64,16,512]{2,1,0:T(8,128)} %bitcast.108), calls=%async_computation.3 | async-start | bytes 4194304 | tf_op jit(solution)/shard_map/all_to_all | solution.py:271
  312.9 84.4 %all-to-all-start = ((f32[128,16,512]{2,1,0:T(8,128)}), f32[128,16,512]{2,1,0:T(8,128)}, u32[]{:S(2)}, u32[]{:S(2)}) async-start(f32[128,16,512]{2,1,0:T(8,128)} %bitcast_subtract_fusion), calls=%async_computation | async-start | bytes 8388608 | tf_op jit(solution)/shard_map/all_to_all | solution.py:271
  397.2 66.6 %all-to-all-start.4 = ((f32[16,8,16,512]{3,2,1,0:T(8,128)}), f32[16,8,16,512]{3,2,1,0:T(8,128)}, u32[]{:S(2)}, u32[]{:S(2)}) async-start(f32[16,8,16,512]{3,2,1,0:T(8,128)} %middle.5), calls=%async_computation.4 | async-start | bytes 8388608 | tf_op jit(solution)/shard_map/all_to_all | solution.py:271
  437.3 38.9 %copy-start.7 = (f32[128,128]{1,0:T(8,128)S(1)}, f32[128,128]{1,0:T(8,128)}, u32[]{:S(2)}) copy-start(f32[128,128]{1,0:T(8,128)} %param.9) | copy-start | bytes 196612
  463.9 55.7 %all-to-all-start.1 = ((f32[16,8,16,512]{3,2,1,0:T(8,128)}), f32[16,8,16,512]{3,2,1,0:T(8,128)}, u32[]{:S(2)}, u32[]{:S(2)}) async-start(f32[16,8,16,512]{3,2,1,0:T(8,128)} %middle.3), calls=%async_computation.1 | async-start | bytes 8388608 | tf_op jit(solution)/shard_map/all_to_all | solution.py:271

commit v4 on v3

--- a/solution.py
+++ b/solution.py
@@ -12,7 +12,7 @@
 DIFFUSION = 0.2
 CUTS_LAST = (4, 8)
 CUTS_FIRST = (8,)
-HOLD = 0
+STACK = 4
 
 
 def dct_table(count):
@@ -68,7 +68,7 @@
     high[2] = DIFFUSION + half_x
 
 
-def tangent_kernel(rows, parts, first, last, hold, *refs):
+def tangent_kernel(rows, parts, first, last, *refs):
     refs = list(refs)
 
     def take(count):
@@ -76,7 +76,6 @@
         del refs[:count]
         return taken
 
-    held = take(1) if hold else None
     state = take(parts) if first else take(1)[0]
     cx, cy = take(parts), take(parts)
     before, after = take(2)
@@ -89,45 +88,42 @@
     low, high = (None, None) if last else take(2)
     old, mid, hx, hy, flat = refs
     at = lambda i: slice(i * LANES, (i + 1) * LANES)
-
-    def gather(pieces, x):
-        return jnp.concatenate([p[pl.ds(x, 8, stride=rows), :] for p in pieces], axis=1)
-
-    if hold:
-
-        @pl.when(pl.program_id(0) == 0)
-        def _():
-            def more(_, carry):
-                mid[0] = mid[0] + 1.0
-                return carry
-
-            lax.fori_loop(0, held[0][0], more, 0)
-
-    for x in range(rows):
-        old[x + 1] = gather(state, x) if first else state[x]
-        hx[x] = 0.5 * gather(cx, x)
-        hy[x] = 0.5 * gather(cy, x)
-    old[0] = before[0]
-    old[rows + 1] = after[0]
-    mid[0] = before[1] + share_before[...] * old[1]
-    mid[rows + 1] = after[1] + share_after[...] * old[rows]
-    for x in range(rows):
-        mid[x + 1] = stepped(old[x + 1], old[x + 2], old[x], hx[x], hy[x])
-    for x in range(rows):
-        new = stepped(mid[x + 1], mid[x + 2], mid[x], hx[x], hy[x])
-        if not last:
-            out[x] = new
+    stack = out.shape[0] // (8 * rows) if last else out.shape[1] // 8
+
+    for g in range(stack):
+        group = pl.ds(8 * g, 8)
+        every = lambda x: pl.ds(8 * g * rows + x, 8, stride=rows)
+
+        def gather(pieces, x):
+            return jnp.concatenate([p[every(x), :] for p in pieces], axis=1)
+
+        for x in range(rows):
+            old[x + 1] = gather(state, x) if first else state[x, group]
+            hx[x] = 0.5 * gather(cx, x)
+            hy[x] = 0.5 * gather(cy, x)
+        old[0] = before[0, group]
+        old[rows + 1] = after[0, group]
+        mid[0] = before[1, group] + share_before[group] * old[1]
+        mid[rows + 1] = after[1, group] + share_after[group] * old[rows]
+        for x in range(rows):
+            mid[x + 1] = stepped(old[x + 1], old[x + 2], old[x], hx[x], hy[x])
+        for x in range(rows):
+            new = stepped(mid[x + 1], mid[x + 2], mid[x], hx[x], hy[x])
+            if not last:
+                out[x, group] = new
+            else:
+                for i in range(parts):
+                    flat[i, pl.ds(x, 8, stride=rows), :] = new[:, at(i)]
+        if last:
+            block = pl.ds(8 * g * rows, 8 * rows)
+            for i in range(parts):
+                out[block, at(i)] = target[i][block, :] - flat[i] if target else flat[i]
         else:
-            for i in range(parts):
-                flat[i, pl.ds(x, 8, stride=rows), :] = new[:, at(i)]
-    if last:
-        for i in range(parts):
-            out[:, at(i)] = target[i][...] - flat[i] if target else flat[i]
-    else:
-        low[0] = out[rows - 1]
-        low[1] = offered(out[rows - 1], out[rows - 2], hx[rows - 1], hy[rows - 1], 1.0)
-        high[0] = out[0]
-        high[1] = offered(out[0], out[1], hx[0], hy[0], -1.0)
+            final, first_row = out[rows - 1, group], out[0, group]
+            low[0, group] = final
+            low[1, group] = offered(final, out[rows - 2, group], hx[rows - 1], hy[rows - 1], 1.0)
+            high[0, group] = first_row
+            high[1, group] = offered(first_row, out[1, group], hx[0], hy[0], -1.0)
 
 
 def mid_kernel(block_ref, spectrum_ref, rh, rl, rth, rtl, ch, cl, cth, ctl, out_ref):
@@ -187,11 +183,11 @@
 
     parts = cols // LANES
     flat_all = [a.reshape(-1, cols) for a in (increments, courant_x, courant_y)]
-    late = (lax.axis_index("sub") % 2 * HOLD).astype(jnp.int32).reshape(1)
 
     def pieces(array, sub, start):
         specs = [
-            pl.BlockSpec((8 * rows, LANES), lambda i, j=j: ((sub * levels + start) // 8 + i, j)) for j in range(parts)
+            pl.BlockSpec((8 * STACK * rows, LANES), lambda i, j=j: ((sub * levels + start) // (8 * STACK) + i, j))
+            for j in range(parts)
         ]
         return [array] * parts, specs
 
@@ -210,12 +206,12 @@
             name="edge",
         )(*arrays, *arrays)
 
-    def tangent(number, sub, start, stop, state, halo, far, target, hold):
+    def tangent(number, sub, start, stop, state, halo, far, target):
         span = stop - start
         first = number == 0
         last = None if first else ("end" if target is None else "jump")
-        slab = pl.BlockSpec((rows, 8, cols), lambda i: (0, i, 0))
-        inputs, specs = ([late], [pl.BlockSpec(memory_space=pltpu.SMEM)]) if hold else ([], [])
+        slab = pl.BlockSpec((rows, 8 * STACK, cols), lambda i: (0, i, 0))
+        inputs, specs = [], []
 
         def add(more, with_specs):
             inputs.extend(more)
@@ -227,19 +223,19 @@
             add([state], [slab])
         add(*pieces(flat_all[1], sub, start))
         add(*pieces(flat_all[2], sub, start))
-        add(halo, [pl.BlockSpec((halo[0].shape[0], 8, cols), lambda i: (0, i, 0))] * 2)
+        add(halo, [pl.BlockSpec((halo[0].shape[0], 8 * STACK, cols), lambda i: (0, i, 0))] * 2)
         if not first:
-            add(far, [pl.BlockSpec((1, 8, cols), lambda i: (2, i, 0))] * 2)
+            add(far, [pl.BlockSpec((1, 8 * STACK, cols), lambda i: (2, i, 0))] * 2)
         if last == "jump":
             add(*pieces(flat_all[0], target, start))
         if first:
-            pair = pl.BlockSpec((2, 8, cols), lambda i: (0, i, 0))
+            pair = pl.BlockSpec((2, 8 * STACK, cols), lambda i: (0, i, 0))
             out, out_spec = [(rows, span, cols)] + [(2, span, cols)] * 2, [slab, pair, pair]
         else:
-            out, out_spec = [(span * rows, cols)], [pl.BlockSpec((8 * rows, cols), lambda i: (i, 0))]
+            out, out_spec = [(span * rows, cols)], [pl.BlockSpec((8 * STACK * rows, cols), lambda i: (i, 0))]
         return pl.pallas_call(
-            functools.partial(tangent_kernel, rows, parts, first, last, hold),
-            grid=(span // 8,),
+            functools.partial(tangent_kernel, rows, parts, first, last),
+            grid=(span // (8 * STACK),),
             in_specs=specs,
             out_specs=out_spec,
             out_shape=[jax.ShapeDtypeStruct(o, f32) for o in out],
@@ -255,13 +251,13 @@
             name="tangent",
         )(*inputs)
 
-    def advance(sub, target, start, stop, hold):
+    def advance(sub, target, start, stop):
         low, high = edges(sub, start, stop)
         last = sub == subs - 1
         far = neighbour(low, 1, last), neighbour(high, -1, last)
-        state, low, high = tangent(0, sub, start, stop, None, far, far, None, False)
+        state, low, high = tangent(0, sub, start, stop, None, far, far, None)
         near = neighbour(low, 1, last), neighbour(high, -1, last)
-        (moved,) = tangent(1, sub, start, stop, state, near, far, target, HOLD > 0 and hold)
+        (moved,) = tangent(1, sub, start, stop, state, near, far, target)
         moved = moved.reshape(-1, rows, cols)
         if target is None:
             moved = increments[0, start:stop] - next_sub(moved)
@@ -323,7 +319,7 @@
     out = None
     work = {}
     for name, sub, target, start, stop in jobs_of(subs, levels, bricks):
-        moved = advance(sub, target, start, stop, not work)
+        moved = advance(sub, target, start, stop)
         block = spread(moved)
         work.setdefault(0 if target is None else target, []).append((name, start, stop, block))
     returned = []

time: 537 us -> 535 us (level)
  waiting for transfers between devices: 257 us -> 278 us
  Pallas kernels: 132 us -> 117 us
    all_to_all x5, waiting for transfers between devices: 148 us -> 171 us  [spread(): lax.all_to_all(value, 'brick', split_axis=0, concat_axis=0, tiled=True)]
    pallas_call x6, Pallas kernels: 65.5 us -> 50.5 us  [tangent(): pl.pallas_call(functools.partial(tangent_kernel, rows, parts, first, last...]
    all_to_all x5, starting transfers between devices: 81.1 us -> 70.7 us  [spread(): lax.all_to_all(value, 'brick', split_axis=0, concat_axis=0, tiled=True)]
    ppermute x12, starting transfers between devices: 28 us -> 33.5 us  [neighbour(): return lax.ppermute(value, ('sub', 'brick'), pairs)]
  transfers between devices with their start and end apart: 18 -> 18, of which waited for: 16 -> 16; matrix products, arithmetic and copies ran while one was open for 4% -> 4% of each run, Pallas kernels for 20% -> 18%
where the time goes in v4:
time: 535 us; the launch traced here: 527 us
  waiting for transfers between devices  278 us (52%)
  Pallas kernels  117 us (22%)
  starting transfers between devices  108 us (20%)
  other arithmetic  19.1 us (4%)
    all_to_all x5, waiting for transfers between devices, spread(): lax.all_to_all(value, 'brick', split_axis=0, concat_axis=0, tiled=True)  171 us
    ppermute x12, waiting for transfers between devices, neighbour(): return lax.ppermute(value, ('sub', 'brick'), pairs)  107 us
    all_to_all x5, starting transfers between devices, spread(): lax.all_to_all(value, 'brick', split_axis=0, concat_axis=0, tiled=True)  70.7 us
    pallas_call x6, Pallas kernels, tangent(): pl.pallas_call(functools.partial(tangent_kernel, rows, parts, first, last...  50.5 us
    pallas_call x3, Pallas kernels, middle(): pl.pallas_call(kernel, grid=(share,), in_specs=specs, out_specs=pl.BlockS...  37.2 us
    ppermute x12, starting transfers between devices, neighbour(): return lax.ppermute(value, ('sub', 'brick'), pairs)  33.5 us
    pallas_call x3, Pallas kernels, edges(): pl.pallas_call(edge_kernel, grid=((stop - start) // size,), in_specs=[blo...  16.7 us
    pallas_call x2, Pallas kernels, mix(): pl.pallas_call(kernel, grid=(parts,), in_specs=specs, out_specs=pl.BlockS...  12.9 us
  transfers between devices with their start and end apart: 18, of which 16 were waited for; matrix products, arithmetic and copies ran while one was open for 4% of the time, Pallas kernels for 18%

profile of v4, /device:TPU:0, one launch (start us, length us, event | category | flops | bytes accessed | tf_op | source)
XLA Modules:
  0.0 527.1 jit_solution(3229801793992851420)
XLA Ops:
  0.0 4.4 edge.4
  4.4 4.9 collective-permute-start.5
  9.3 1.3 collective-permute-start.6
  10.6 15.8 %collective-permute-done.5.refs_12_.refs_11_ = f32[3,64,512]{2,1,0:T(8,128)S(1)} collective-permute-done((f32[3,64,512]{2,1,0:T(8,128)}, f32[3,64,512]{2,1,0:T(8,128)S(1)}, u32[]{:S(2)}, u32[]{:S(2)}) %collective-permute-start.5) | collective-permute-done | bytes 393248 | tf_op jit(solution)/shard_map/ppermute | solution.py:173
  26.4 1.8 collective-permute-done.6.refs_13_.refs_12_
  28.2 0.7 copy-done.5
  28.9 6.9 %tangent.8 = (f32[16,64,512]{2,1,0:T(8,128)}, f32[2,64,512]{2,1,0:T(8,128)}, f32[2,64,512]{2,1,0:T(8,128)}) custom-call(f32[4096,512]{1,0:T(8,128)} %bitcast.83, f32[4096,512]{1,0:T(8,128)} %bitcast.84, f32[4096,512]{1,0:T(8,128)} %bitcast.85, f32[4096,512]{1,0:T(8,128)} %bitcast.86, f32[4096,512]{1,0:T(8,128)} %bitcast.23, f32[4096,512]{1,0:T(8,128)} %bitcast.24, ...), custom_call_target="tpu_custom_call" | custom-call | flops 20971520 | bytes 16777216 | tf_op jit(solution)/shard_map/tangent/pallas_call | solution.py:236
  35.8 3.4 collective-permute-start.7
  39.2 1.3 collective-permute-start.8
  40.5 9.3 %collective-permute-done.7.refs_9_ = f32[2,64,512]{2,1,0:T(8,128)S(1)} collective-permute-done((f32[2,64,512]{2,1,0:T(8,128)}, f32[2,64,512]{2,1,0:T(8,128)S(1)}, u32[]{:S(2)}, u32[]{:S(2)}) %collective-permute-start.7) | collective-permute-done | bytes 262176 | tf_op jit(solution)/shard_map/ppermute | solution.py:173
  49.9 0.6 collective-permute-done.8.refs_10_
  50.5 0.1 copy-done.10
  50.6 0.6 copy-done.12
  51.2 7.2 %tangent.9 = f32[1024,512]{1,0:T(8,128)} custom-call(f32[16,64,512]{2,1,0:T(8,128)} %get-tuple-element.27.refs_0_, f32[4096,512]{1,0:T(8,128)} %bitcast.27, f32[4096,512]{1,0:T(8,128)} %bitcast.28, f32[4096,512]{1,0:T(8,128)} %bitcast.29, f32[4096,512]{1,0:T(8,128)} %bitcast.30, f32[4096,512]{1,0:T(8,128)} %bitcast.57, f32[4096,512]{1,0:T(8,128)} %bitcast.58, ...), custom_call_target="tpu_custom_call" | custom-call | flops 20971520 | bytes 16777216 | tf_op jit(solution)/shard_map/tangent/pallas_call | solution.py:236
  58.4 7.1 %all-to-all-start.2 = ((f32[64,16,512]{2,1,0:T(8,128)}), f32[64,16,512]{2,1,0:T(8,128)S(1)}, u32[]{:S(2)}, u32[]{:S(2)}) async-start(f32[64,16,512]{2,1,0:T(8,128)} %bitcast.107), calls=%async_computation.2 | async-start | bytes 4194304 | tf_op jit(solution)/shard_map/all_to_all | solution.py:267
  65.5 7.8 %edge.3 = (f32[3,128,512]{2,1,0:T(8,128)}, f32[3,128,512]{2,1,0:T(8,128)}) custom-call(f32[256,16,512]{2,1,0:T(8,128)} %bitcast.91, f32[256,16,512]{2,1,0:T(8,128)} %bitcast.31, f32[256,16,512]{2,1,0:T(8,128)} %bitcast.61, f32[256,16,512]{2,1,0:T(8,128)} %bitcast.92, f32[256,16,512]{2,1,0:T(8,128)} %bitcast.32, f32[256,16,512]{2,1,0:T(8,128)} %bitcast.62), custom_call_target="tpu_custom_call" | custom-call | bytes 13107200 | tf_op jit(solution)/shard_map/edge/pallas_call | solution.py:198
  73.3 3.8 collective-permute-start
  77.2 1.3 collective-permute-start.1
  78.5 34.8 %collective-permute-done.refs_12_.refs_11_ = f32[3,128,512]{2,1,0:T(8,128)S(1)} collective-permute-done((f32[3,128,512]{2,1,0:T(8,128)}, f32[3,128,512]{2,1,0:T(8,128)S(1)}, u32[]{:S(2)}, u32[]{:S(2)}) %collective-permute-start) | collective-permute-done | bytes 786464 | tf_op jit(solution)/shard_map/ppermute | solution.py:173
  113.3 3.6 collective-permute-done.1.refs_13_.refs_12_
  117.0 1.0 copy-done.1
  117.9 11.4 %tangent.6 = (f32[16,128,512]{2,1,0:T(8,128)}, f32[2,128,512]{2,1,0:T(8,128)}, f32[2,128,512]{2,1,0:T(8,128)}) custom-call(f32[4096,512]{1,0:T(8,128)} %bitcast.93, f32[4096,512]{1,0:T(8,128)} %bitcast.94, f32[4096,512]{1,0:T(8,128)} %bitcast.95, f32[4096,512]{1,0:T(8,128)} %bitcast.96, f32[4096,512]{1,0:T(8,128)} %bitcast.35, f32[4096,512]{1,0:T(8,128)} %bitcast.34, ...), custom_call_target="tpu_custom_call" | custom-call | flops 41943040 | bytes 33554432 | tf_op jit(solution)/shard_map/tangent/pallas_call | solution.py:236
  129.3 5.5 %collective-permute-start.2 = (f32[2,128,512]{2,1,0:T(8,128)}, f32[2,128,512]{2,1,0:T(8,128)S(1)}, u32[]{:S(2)}, u32[]{:S(2)}) collective-permute-start(f32[2,128,512]{2,1,0:T(8,128)} %get-tuple-element.23), channel_id=1, source_target_pairs={{0,1},{1,2},{2,3},{3,4},{4,5},{5,6},{6,7},{7,8},{8,9},{9,10},{10,1... | collective-permute-start | bytes 1572872 | tf_op jit(solution)/shard_map/ppermute | solution.py:173
  134.8 1.3 collective-permute-start.3
  136.1 16.2 %collective-permute-done.2.refs_9_ = f32[2,128,512]{2,1,0:T(8,128)S(1)} collective-permute-done((f32[2,128,512]{2,1,0:T(8,128)}, f32[2,128,512]{2,1,0:T(8,128)S(1)}, u32[]{:S(2)}, u32[]{:S(2)}) %collective-permute-start.2) | collective-permute-done | bytes 524320 | tf_op jit(solution)/shard_map/ppermute | solution.py:173
  152.3 0.6 collective-permute-done.3.refs_10_
  153.0 0.2 copy-done.8
  153.2 0.6 copy-done.9
  153.8 11.0 %tangent.7 = f32[2048,512]{1,0:T(8,128)} custom-call(f32[16,128,512]{2,1,0:T(8,128)} %get-tuple-element.22.refs_0_, f32[4096,512]{1,0:T(8,128)} %bitcast.37, f32[4096,512]{1,0:T(8,128)} %bitcast.38, f32[4096,512]{1,0:T(8,128)} %bitcast.39, f32[4096,512]{1,0:T(8,128)} %bitcast.40, f32[4096,512]{1,0:T(8,128)} %bitcast.67, f32[4096,512]{1,0:T(8,128)} %bitcast.68, ...), custom_call_target="tpu_custom_call" | custom-call | flops 41943040 | bytes 33554432 | tf_op jit(solution)/shard_map/tangent/pallas_call | solution.py:236
  164.7 3.4 collective-permute-start.4
  168.1 4.4 edge.5
  172.6 3.9 collective-permute-start.9
  176.4 1.5 collective-permute-start.10
  177.9 15.0 %collective-permute-done.9.refs_12_.refs_11_ = f32[3,64,512]{2,1,0:T(8,128)S(1)} collective-permute-done((f32[3,64,512]{2,1,0:T(8,128)}, f32[3,64,512]{2,1,0:T(8,128)S(1)}, u32[]{:S(2)}, u32[]{:S(2)}) %collective-permute-start.9) | collective-permute-done | bytes 393248 | tf_op jit(solution)/shard_map/ppermute | solution.py:173
  193.0 1.0 collective-permute-done.10.refs_13_.refs_12_
  194.0 0.7 copy-done.6
  194.7 6.9 %tangent.10 = (f32[16,64,512]{2,1,0:T(8,128)}, f32[2,64,512]{2,1,0:T(8,128)}, f32[2,64,512]{2,1,0:T(8,128)}) custom-call(f32[4096,512]{1,0:T(8,128)} %bitcast.99, f32[4096,512]{1,0:T(8,128)} %bitcast.100, f32[4096,512]{1,0:T(8,128)} %bitcast.101, f32[4096,512]{1,0:T(8,128)} %bitcast.102, f32[4096,512]{1,0:T(8,128)} %bitcast.43, f32[4096,512]{1,0:T(8,128)} %bitcast.44, ...), custom_call_target="tpu_custom_call" | custom-call | flops 20971520 | bytes 16777216 | tf_op jit(solution)/shard_map/tangent/pallas_call | solution.py:236
  201.6 4.1 collective-permute-start.11
  205.6 1.3 collective-permute-start.12
  206.9 2.9 collective-permute-done.11.refs_9_
  209.8 5.2 collective-permute-done.12.refs_10_
  215.1 0.7 copy-done.13
  215.8 7.2 %tangent.11 = f32[1024,512]{1,0:T(8,128)} custom-call(f32[16,64,512]{2,1,0:T(8,128)} %get-tuple-element.32.refs_0_, f32[4096,512]{1,0:T(8,128)} %bitcast.47, f32[4096,512]{1,0:T(8,128)} %bitcast.48, f32[4096,512]{1,0:T(8,128)} %bitcast.49, f32[4096,512]{1,0:T(8,128)} %bitcast.50, f32[4096,512]{1,0:T(8,128)} %bitcast.77, f32[4096,512]{1,0:T(8,128)} %bitcast.78, ...), custom_call_target="tpu_custom_call" | custom-call | flops 20971520 | bytes 16777216 | tf_op jit(solution)/shard_map/tangent/pallas_call | solution.py:236
  223.0 14.5 %all-to-all-start.3 = ((f32[64,16,512]{2,1,0:T(8,128)}), f32[64,16,512]{2,1,0:T(8,128)}, u32[]{:S(2)}, u32[]{:S(2)}) async-start(f32[64,16,512]{2,1,0:T(8,128)} %bitcast.108), calls=%async_computation.3 | async-start | bytes 4194304 | tf_op jit(solution)/shard_map/all_to_all | solution.py:267
  237.5 7.0 %bitcast_subtract_fusion = f32[128,16,512]{2,1,0:T(8,128)} fusion(f32[128,16,512]{2,1,0:T(8,128)} %collective-permute-done.4, f32[2,128,16,512]{3,2,1,0:T(8,128)} %param.5), kind=kLoop, calls=%fused_computation | loop fusion | flops 1048576 | bytes 12582912 | tf_op jit(solution)/shard_map/sub | solution.py:263
  244.5 25.4 %all-to-all-done.3 = f32[64,16,512]{2,1,0:T(8,128)} async-done(((f32[64,16,512]{2,1,0:T(8,128)}), f32[64,16,512]{2,1,0:T(8,128)}, u32[]{:S(2)}, u32[]{:S(2)}) %all-to-all-start.3) | async-done | bytes 2097184 | tf_op jit(solution)/shard_map/all_to_all | solution.py:267
  269.9 9.4 %all-to-all-start = ((f32[128,16,512]{2,1,0:T(8,128)}), f32[128,16,512]{2,1,0:T(8,128)}, u32[]{:S(2)}, u32[]{:S(2)}) async-start(f32[128,16,512]{2,1,0:T(8,128)} %bitcast_subtract_fusion), calls=%async_computation | async-start | bytes 8388608 | tf_op jit(solution)/shard_map/all_to_all | solution.py:267
  279.4 2.7 fusion.3
  282.0 8.2 %fusion.1 = (bf16[512,512]{1,0:T(8,128)(2,1)}, bf16[512,512]{1,0:T(8,128)(2,1)}, bf16[512,512]{1,0:T(8,128)(2,1)}, bf16[512,512]{1,0:T(8,128)(2,1)}) fusion(f32[512]{0:T(512)S(1)} %get-tuple-element.51, f32[512]{0:T(512)S(1)} %get-tuple-element.52), kind=kLoop, calls=%fused_computation.6 | loop fusion | flops 3670016 | bytes 2101248 | tf_op jit(solution)/shard_map/convert_element_type | solution.py:28
  290.2 10.0 %middle.4.refs_10_ = f32[16,8,16,512]{3,2,1,0:T(8,128)} custom-call(f32[16,4,16,512]{3,2,1,0:T(8,128)} %bitcast.13.block_ref, f32[256,512]{1,0:T(8,128)} %refs_1_.1, bf16[256,256]{1,0:T(8,128)(2,1)} %get-tuple-element.48.rh.refs_2_, bf16[256,256]{1,0:T(8,128)(2,1)} %get-tuple-element.46.rl.refs_3_, bf16[256,256]{1,0:T(8,128)(2,1)} %get-tuple-element.47.rth.refs_4_, ...), custom_call_target="tpu_custom_call" | custom-call | flops 4831838208 | bytes 4194304 | tf_op jit(solution)/shard_map/middle/pallas_call | solution.py:283
  300.2 10.0 %middle.5 = f32[16,8,16,512]{3,2,1,0:T(8,128)} custom-call(f32[16,4,16,512]{3,2,1,0:T(8,128)} %bitcast.110, f32[256,512]{1,0:T(8,128)} %refs_1_.1, bf16[256,256]{1,0:T(8,128)(2,1)} %get-tuple-element.48.rh.refs_2_, bf16[256,256]{1,0:T(8,128)(2,1)} %get-tuple-element.46.rl.refs_3_, ...), custom_call_target="tpu_custom_call", output_to_operand_aliasing={{}: (10, {})} | custom-call | flops 4831838208 | bytes 4194304 | tf_op jit(solution)/shard_map/middle/pallas_call | solution.py:283
  310.2 48.9 %all-to-all-done = f32[128,16,512]{2,1,0:T(8,128)} async-done(((f32[128,16,512]{2,1,0:T(8,128)}), f32[128,16,512]{2,1,0:T(8,128)}, u32[]{:S(2)}, u32[]{:S(2)}) %all-to-all-start) | async-done | bytes 4194336 | tf_op jit(solution)/shard_map/all_to_all | solution.py:267
  359.1 20.2 %all-to-all-start.4 = ((f32[16,8,16,512]{3,2,1,0:T(8,128)}), f32[16,8,16,512]{3,2,1,0:T(8,128)}, u32[]{:S(2)}, u32[]{:S(2)}) async-start(f32[16,8,16,512]{3,2,1,0:T(8,128)} %middle.5), calls=%async_computation.4 | async-start | bytes 8388608 | tf_op jit(solution)/shard_map/all_to_all | solution.py:267
  379.3 17.2 %middle.3 = f32[16,8,16,512]{3,2,1,0:T(8,128)} custom-call(f32[16,8,16,512]{3,2,1,0:T(8,128)} %bitcast.8.block_ref, f32[256,512]{1,0:T(8,128)} %refs_1_.1, bf16[256,256]{1,0:T(8,128)(2,1)} %get-tuple-element.48.rh.refs_2_, bf16[256,256]{1,0:T(8,128)(2,1)} %get-tuple-element.46.rl.refs_3_, bf16[256,256]{1,0:T(8,128)(2,1)} %get-tuple-element.47.rth.refs_4_, ...), custom_call_target="tpu_custom_call" | custom-call | flops 9663676416 | bytes 8388608 | tf_op jit(solution)/shard_map/middle/pallas_call | solution.py:283
  396.5 61.2 %all-to-all-done.4 = f32[16,8,16,512]{3,2,1,0:T(8,128)} async-done(((f32[16,8,16,512]{3,2,1,0:T(8,128)}), f32[16,8,16,512]{3,2,1,0:T(8,128)}, u32[]{:S(2)}, u32[]{:S(2)}) %all-to-all-start.4) | async-done | bytes 4194336 | tf_op jit(solution)/shard_map/all_to_all | solution.py:267
  457.8 19.5 %all-to-all-start.1 = ((f32[16,8,16,512]{3,2,1,0:T(8,128)}), f32[16,8,16,512]{3,2,1,0:T(8,128)}, u32[]{:S(2)}, u32[]{:S(2)}) async-start(f32[16,8,16,512]{3,2,1,0:T(8,128)} %middle.3), calls=%async_computation.1 | async-start | bytes 8388608 | tf_op jit(solution)/shard_map/all_to_all | solution.py:267
  477.3 0.1 fusion.7
  477.4 0.1 copy.12
  477.5 0.1 copy.10
  477.6 0.6 fusion.4
  478.3 0.6 fusion.5
  478.9 6.5 %mix.2.refs_0_ = f32[4096,512]{1,0:T(8,128)} custom-call(f32[2048,512]{1,0:T(8,128)} %bitcast.14.field_ref, bf16[128,128]{1,0:T(8,128)(2,1)} %get-tuple-element.36.vh_ref, bf16[128,128]{1,0:T(8,128)(2,1)} %get-tuple-element.35.vl_ref), custom_call_target="tpu_custom_call" | custom-call | flops 805306368 | bytes 8388608 | tf_op jit(solution)/shard_map/mix/pallas_call | solution.py:305
  485.4 35.3 %all-to-all-done.1 = f32[16,8,16,512]{3,2,1,0:T(8,128)} async-done(((f32[16,8,16,512]{3,2,1,0:T(8,128)}), f32[16,8,16,512]{3,2,1,0:T(8,128)}, u32[]{:S(2)}, u32[]{:S(2)}) %all-to-all-start.1) | async-done | bytes 4194336 | tf_op jit(solution)/shard_map/all_to_all | solution.py:267
  520.7 6.5 %mix.3 = f32[4096,512]{1,0:T(8,128)} custom-call(f32[2048,512]{1,0:T(8,128)} %bitcast.9.field_ref, bf16[128,128]{1,0:T(8,128)(2,1)} %get-tuple-element.40.vh_ref, bf16[128,128]{1,0:T(8,128)(2,1)} %get-tuple-element.39.vl_ref, f32[4096,512]{1,0:T(8,128)} %mix.2.refs_0_), custom_call_target="tpu_custom_call", output_to_operand_aliasing={{}: (3, {})} | custom-call | flops 805306368 | bytes 8388608 | tf_op jit(solution)/shard_map/mix/pallas_call | solution.py:305
  (26 shorter events, 0.2 us)
Async XLA Ops:
  4.4 22.0 %collective-permute-start.5 = (f32[3,64,512]{2,1,0:T(8,128)}, f32[3,64,512]{2,1,0:T(8,128)S(1)}, u32[]{:S(2)}, u32[]{:S(2)}) collective-permute-start(f32[3,64,512]{2,1,0:T(8,128)} %get-tuple-element.25), channel_id=1, source_target_pairs={{0,1},{1,2},{2,3},{3,4},{4,5},{5,6},{6,7},{7,8},{8,9},{9,10},{10,1... | collective-permute-start | bytes 1179656 | tf_op jit(solution)/shard_map/ppermute | solution.py:173
  9.3 18.9 %collective-permute-start.6 = (f32[3,64,512]{2,1,0:T(8,128)}, f32[3,64,512]{2,1,0:T(8,128)S(1)}, u32[]{:S(2)}, u32[]{:S(2)}) collective-permute-start(f32[3,64,512]{2,1,0:T(8,128)} %get-tuple-element.26), channel_id=1, source_target_pairs={{1,0},{2,1},{3,2},{4,3},{5,4},{6,5},{7,6},{8,7},{9,8},{10,9},{11,1... | collective-permute-start | bytes 1179656 | tf_op jit(solution)/shard_map/ppermute | solution.py:173
  26.4 1.8 copy-start.3
  28.2 0.7 copy-start.5
  35.8 14.1 %collective-permute-start.7 = (f32[2,64,512]{2,1,0:T(8,128)}, f32[2,64,512]{2,1,0:T(8,128)S(1)}, u32[]{:S(2)}, u32[]{:S(2)}) collective-permute-start(f32[2,64,512]{2,1,0:T(8,128)} %get-tuple-element.28), channel_id=1, source_target_pairs={{0,1},{1,2},{2,3},{3,4},{4,5},{5,6},{6,7},{7,8},{8,9},{9,10},{10,1... | collective-permute-start | bytes 786440 | tf_op jit(solution)/shard_map/ppermute | solution.py:173
  39.2 11.3 %collective-permute-start.8 = (f32[2,64,512]{2,1,0:T(8,128)}, f32[2,64,512]{2,1,0:T(8,128)S(1)}, u32[]{:S(2)}, u32[]{:S(2)}) collective-permute-start(f32[2,64,512]{2,1,0:T(8,128)} %get-tuple-element.29), channel_id=1, source_target_pairs={{1,0},{2,1},{3,2},{4,3},{5,4},{6,5},{7,6},{8,7},{9,8},{10,9},{11,1... | collective-permute-start | bytes 786440 | tf_op jit(solution)/shard_map/ppermute | solution.py:173
  49.9 0.7 copy-start.10
  50.5 0.7 copy-start.12
  58.4 164.6 %all-to-all-start.2 = ((f32[64,16,512]{2,1,0:T(8,128)}), f32[64,16,512]{2,1,0:T(8,128)S(1)}, u32[]{:S(2)}, u32[]{:S(2)}) async-start(f32[64,16,512]{2,1,0:T(8,128)} %bitcast.107), calls=%async_computation.2 | async-start | bytes 4194304 | tf_op jit(solution)/shard_map/all_to_all | solution.py:267
  73.3 40.0 %collective-permute-start = (f32[3,128,512]{2,1,0:T(8,128)}, f32[3,128,512]{2,1,0:T(8,128)S(1)}, u32[]{:S(2)}, u32[]{:S(2)}) collective-permute-start(f32[3,128,512]{2,1,0:T(8,128)} %get-tuple-element.20), channel_id=1, source_target_pairs={{0,1},{1,2},{2,3},{3,4},{4,5},{5,6},{6,7},{7,8},{8,9},{9,10},{10,1... | collective-permute-start | bytes 2359304 | tf_op jit(solution)/shard_map/ppermute | solution.py:173
  77.2 39.8 %collective-permute-start.1 = (f32[3,128,512]{2,1,0:T(8,128)}, f32[3,128,512]{2,1,0:T(8,128)S(1)}, u32[]{:S(2)}, u32[]{:S(2)}) collective-permute-start(f32[3,128,512]{2,1,0:T(8,128)} %get-tuple-element.21), channel_id=1, source_target_pairs={{1,0},{2,1},{3,2},{4,3},{5,4},{6,5},{7,6},{8,7},{9,8},{10,9},{11,1... | collective-permute-start | bytes 2359304 | tf_op jit(solution)/shard_map/ppermute | solution.py:173
  113.3 3.6 copy-start
  117.0 1.0 copy-start.1
  129.3 23.0 %collective-permute-start.2 = (f32[2,128,512]{2,1,0:T(8,128)}, f32[2,128,512]{2,1,0:T(8,128)S(1)}, u32[]{:S(2)}, u32[]{:S(2)}) collective-permute-start(f32[2,128,512]{2,1,0:T(8,128)} %get-tuple-element.23), channel_id=1, source_target_pairs={{0,1},{1,2},{2,3},{3,4},{4,5},{5,6},{6,7},{7,8},{8,9},{9,10},{10,1... | collective-permute-start | bytes 1572872 | tf_op jit(solution)/shard_map/ppermute | solution.py:173
  134.8 18.2 %collective-permute-start.3 = (f32[2,128,512]{2,1,0:T(8,128)}, f32[2,128,512]{2,1,0:T(8,128)S(1)}, u32[]{:S(2)}, u32[]{:S(2)}) collective-permute-start(f32[2,128,512]{2,1,0:T(8,128)} %get-tuple-element.24), channel_id=1, source_target_pairs={{1,0},{2,1},{3,2},{4,3},{5,4},{6,5},{7,6},{8,7},{9,8},{10,9},{11,1... | collective-permute-start | bytes 1572872 | tf_op jit(solution)/shard_map/ppermute | solution.py:173
  152.3 0.8 copy-start.8
  153.0 0.8 copy-start.9
  164.7 72.7 %collective-permute-start.4 = (f32[128,16,512]{2,1,0:T(8,128)}, f32[128,16,512]{2,1,0:T(8,128)}, u32[]{:S(2)}, u32[]{:S(2)}) collective-permute-start(f32[128,16,512]{2,1,0:T(8,128)} %bitcast.109), channel_id=1, source_target_pairs={{0,16},{1,17},{2,18},{3,19},{4,20},{5,21},{6,22},{7,23},{8,24},{9,... | collective-permute-start | bytes 12582920 | tf_op jit(solution)/shard_map/ppermute | solution.py:176
  172.6 20.4 %collective-permute-start.9 = (f32[3,64,512]{2,1,0:T(8,128)}, f32[3,64,512]{2,1,0:T(8,128)S(1)}, u32[]{:S(2)}, u32[]{:S(2)}) collective-permute-start(f32[3,64,512]{2,1,0:T(8,128)} %get-tuple-element.30), channel_id=1, source_target_pairs={{0,1},{1,2},{2,3},{3,4},{4,5},{5,6},{6,7},{7,8},{8,9},{9,10},{10,1... | collective-permute-start | bytes 1179656 | tf_op jit(solution)/shard_map/ppermute | solution.py:173
  176.4 17.5 %collective-permute-start.10 = (f32[3,64,512]{2,1,0:T(8,128)}, f32[3,64,512]{2,1,0:T(8,128)S(1)}, u32[]{:S(2)}, u32[]{:S(2)}) collective-permute-start(f32[3,64,512]{2,1,0:T(8,128)} %get-tuple-element.31), channel_id=1, source_target_pairs={{1,0},{2,1},{3,2},{4,3},{5,4},{6,5},{7,6},{8,7},{9,8},{10,9},{11,1... | collective-permute-start | bytes 1179656 | tf_op jit(solution)/shard_map/ppermute | solution.py:173
  193.0 1.0 copy-start.4
  194.0 0.7 copy-start.6
  201.6 8.2 %collective-permute-start.11 = (f32[2,64,512]{2,1,0:T(8,128)}, f32[2,64,512]{2,1,0:T(8,128)S(1)}, u32[]{:S(2)}, u32[]{:S(2)}) collective-permute-start(f32[2,64,512]{2,1,0:T(8,128)} %get-tuple-element.33), channel_id=1, source_target_pairs={{0,1},{1,2},{2,3},{3,4},{4,5},{5,6},{6,7},{7,8},{8,9},{9,10},{10,1... | collective-permute-start | bytes 786440 | tf_op jit(solution)/shard_map/ppermute | solution.py:173
  205.6 9.4 %collective-permute-start.12 = (f32[2,64,512]{2,1,0:T(8,128)}, f32[2,64,512]{2,1,0:T(8,128)S(1)}, u32[]{:S(2)}, u32[]{:S(2)}) collective-permute-start(f32[2,64,512]{2,1,0:T(8,128)} %get-tuple-element.34), channel_id=1, source_target_pairs={{1,0},{2,1},{3,2},{4,3},{5,4},{6,5},{7,6},{8,7},{9,8},{10,9},{11,1... | collective-permute-start | bytes 786440 | tf_op jit(solution)/shard_map/ppermute | solution.py:173
  209.8 5.2 copy-start.11
  215.1 0.7 copy-start.13
  223.0 21.5 %copy-start.2 = (f32[64,16,512]{2,1,0:T(8,128)}, f32[64,16,512]{2,1,0:T(8,128)S(1)}, u32[]{:S(2)}) copy-start(f32[64,16,512]{2,1,0:T(8,128)S(1)} %all-to-all-done.2) | copy-start | bytes 6291460
  223.0 46.9 %all-to-all-start.3 = ((f32[64,16,512]{2,1,0:T(8,128)}), f32[64,16,512]{2,1,0:T(8,128)}, u32[]{:S(2)}, u32[]{:S(2)}) async-start(f32[64,16,512]{2,1,0:T(8,128)} %bitcast.108), calls=%async_computation.3 | async-start | bytes 4194304 | tf_op jit(solution)/shard_map/all_to_all | solution.py:267
  269.9 89.2 %all-to-all-start = ((f32[128,16,512]{2,1,0:T(8,128)}), f32[128,16,512]{2,1,0:T(8,128)}, u32[]{:S(2)}, u32[]{:S(2)}) async-start(f32[128,16,512]{2,1,0:T(8,128)} %bitcast_subtract_fusion), calls=%async_computation | async-start | bytes 8388608 | tf_op jit(solution)/shard_map/all_to_all | solution.py:267
  359.1 98.6 %all-to-all-start.4 = ((f32[16,8,16,512]{3,2,1,0:T(8,128)}), f32[16,8,16,512]{3,2,1,0:T(8,128)}, u32[]{:S(2)}, u32[]{:S(2)}) async-start(f32[16,8,16,512]{3,2,1,0:T(8,128)} %middle.5), calls=%async_computation.4 | async-start | bytes 8388608 | tf_op jit(solution)/shard_map/all_to_all | solution.py:267
  396.5 80.7 %copy-start.7 = (f32[128,128]{1,0:T(8,128)S(1)}, f32[128,128]{1,0:T(8,128)}, u32[]{:S(2)}) copy-start(f32[128,128]{1,0:T(8,128)} %param.9) | copy-start | bytes 196612
  457.8 62.9 %all-to-all-start.1 = ((f32[16,8,16,512]{3,2,1,0:T(8,128)}), f32[16,8,16,512]{3,2,1,0:T(8,128)}, u32[]{:S(2)}, u32[]{:S(2)}) async-start(f32[16,8,16,512]{3,2,1,0:T(8,128)} %middle.3), calls=%async_computation.1 | async-start | bytes 8388608 | tf_op jit(solution)/shard_map/all_to_all | solution.py:267

commit v5 on v4

--- a/solution.py
+++ b/solution.py
@@ -135,13 +135,13 @@
     out_ref[...] = dot3(split(back), (ch[...], cl[...])).reshape(count, 1, rows, cols)
 
 
-def mix_kernel(rows, field_ref, vh_ref, vl_ref, *refs):
-    out_ref = refs[-1]
-    levels = vh_ref.shape[1]
+def mix_kernel(field_ref, vh_ref, vl_ref, *refs):
+    levels, height, lanes = field_ref.shape
+    field, out = (r.reshape(levels * height, lanes) for r in (field_ref, refs[-1]))
     factor = (vh_ref[...], vl_ref[...])
-    for x in range(rows):
-        field = field_ref[pl.ds(x, levels, stride=rows), :]
-        out_ref[pl.ds(x, levels, stride=rows), :] = dot3(factor, split(field))
+    for x in range(height):
+        own = pl.ds(x, levels, stride=height)
+        out[own, :] = dot3(factor, split(field[own, :]))
 
 
 def params(**more):
@@ -192,7 +192,7 @@
         return [array] * parts, specs
 
     def edges(sub, start, stop):
-        size = 16
+        size = 32
         block = lambda at: pl.BlockSpec((size, 8, cols), lambda i: ((sub * levels + start) // size + i, at, 0))
         arrays = [a.reshape(-1, rows, cols) for a in (increments, courant_x, courant_y)]
         return pl.pallas_call(
@@ -293,21 +293,21 @@
         )(*inputs)
 
     def mix(field, sub, factor, old):
-        field = field.reshape(levels * rows, cols)
+        field = field.reshape(levels, rows, cols)
         inputs = [field, *factor]
-        whole = pl.BlockSpec((levels, levels), lambda i: (0, 0))
-        specs = [pl.BlockSpec((levels * rows, LANES), lambda i: (0, i)), whole, whole]
-        kernel, alias = functools.partial(mix_kernel, rows), {}
+        whole = pl.BlockSpec((levels, levels), lambda i, j: (0, 0))
+        specs = [pl.BlockSpec((levels, 8, LANES), lambda i, j: (0, j, i)), whole, whole]
+        kernel, alias = mix_kernel, {}
         if old is not None:
             inputs.append(old)
             specs.append(pl.BlockSpec(memory_space=pl.ANY))
             alias = {3: 0}
         return pl.pallas_call(
             kernel,
-            grid=(parts,),
+            grid=(parts, rows // 8),
             in_specs=specs,
-            out_specs=pl.BlockSpec((levels * rows, LANES), lambda i: (sub, i)),
-            out_shape=jax.ShapeDtypeStruct((subs * levels * rows, cols), f32),
+            out_specs=pl.BlockSpec((levels, 8, LANES), lambda i, j: (sub, j, i)),
+            out_shape=jax.ShapeDtypeStruct((subs * levels, rows, cols), f32),
             input_output_aliases=alias,
             compiler_params=params(),
             cost_estimate=pl.CostEstimate(

time: 535 us -> 535 us (level)
    ppermute x12, waiting for transfers between devices: 107 us -> 113 us  [neighbour(): return lax.ppermute(value, ('sub', 'brick'), pairs)]
  transfers between devices with their start and end apart: 18 -> 18, of which waited for: 16 -> 16; matrix products, arithmetic and copies ran while one was open for 4% -> 4% of each run, Pallas kernels for 18% -> 17%
where the time goes in v5:
time: 535 us; the launch traced here: 527 us
  waiting for transfers between devices  281 us (53%)
  Pallas kernels  117 us (22%)
  starting transfers between devices  105 us (20%)
  other arithmetic  19.1 us (4%)
    all_to_all x5, waiting for transfers between devices, spread(): lax.all_to_all(value, 'brick', split_axis=0, concat_axis=0, tiled=True)  168 us
    ppermute x12, waiting for transfers between devices, neighbour(): return lax.ppermute(value, ('sub', 'brick'), pairs)  113 us
    all_to_all x5, starting transfers between devices, spread(): lax.all_to_all(value, 'brick', split_axis=0, concat_axis=0, tiled=True)  71.6 us
    pallas_call x6, Pallas kernels, tangent(): pl.pallas_call(functools.partial(tangent_kernel, rows, parts, first, last...  50.5 us
    pallas_call x3, Pallas kernels, middle(): pl.pallas_call(kernel, grid=(share,), in_specs=specs, out_specs=pl.BlockS...  37.2 us
    ppermute x12, starting transfers between devices, neighbour(): return lax.ppermute(value, ('sub', 'brick'), pairs)  30 us
    pallas_call x2, Pallas kernels, mix(): pl.pallas_call(kernel, grid=(parts, rows // 8), in_specs=specs, out_specs...  15.5 us
    pallas_call x3, Pallas kernels, edges(): pl.pallas_call(edge_kernel, grid=((stop - start) // size,), in_specs=[blo...  13.8 us
  transfers between devices with their start and end apart: 18, of which 16 were waited for; matrix products, arithmetic and copies ran while one was open for 4% of the time, Pallas kernels for 17%

profile of v5, /device:TPU:0, one launch (start us, length us, event | category | flops | bytes accessed | tf_op | source)
XLA Modules:
  0.0 527.3 jit_solution(6266621848618413985)
XLA Ops:
  0.0 3.8 edge.4
  3.8 4.9 collective-permute-start.5
  8.7 1.3 collective-permute-start.6
  10.0 15.8 %collective-permute-done.5.refs_12_.refs_11_ = f32[3,64,512]{2,1,0:T(8,128)S(1)} collective-permute-done((f32[3,64,512]{2,1,0:T(8,128)}, f32[3,64,512]{2,1,0:T(8,128)S(1)}, u32[]{:S(2)}, u32[]{:S(2)}) %collective-permute-start.5) | collective-permute-done | bytes 393248 | tf_op jit(solution)/shard_map/ppermute | solution.py:173
  25.7 1.8 collective-permute-done.6.refs_13_.refs_12_
  27.6 0.7 copy-done.5
  28.3 6.9 %tangent.8 = (f32[16,64,512]{2,1,0:T(8,128)}, f32[2,64,512]{2,1,0:T(8,128)}, f32[2,64,512]{2,1,0:T(8,128)}) custom-call(f32[4096,512]{1,0:T(8,128)} %bitcast.83, f32[4096,512]{1,0:T(8,128)} %bitcast.84, f32[4096,512]{1,0:T(8,128)} %bitcast.85, f32[4096,512]{1,0:T(8,128)} %bitcast.86, f32[4096,512]{1,0:T(8,128)} %bitcast.23, f32[4096,512]{1,0:T(8,128)} %bitcast.24, ...), custom_call_target="tpu_custom_call" | custom-call | flops 20971520 | bytes 16777216 | tf_op jit(solution)/shard_map/tangent/pallas_call | solution.py:236
  35.2 3.4 collective-permute-start.7
  38.6 1.3 collective-permute-start.8
  39.9 9.3 %collective-permute-done.7.refs_9_ = f32[2,64,512]{2,1,0:T(8,128)S(1)} collective-permute-done((f32[2,64,512]{2,1,0:T(8,128)}, f32[2,64,512]{2,1,0:T(8,128)S(1)}, u32[]{:S(2)}, u32[]{:S(2)}) %collective-permute-start.7) | collective-permute-done | bytes 262176 | tf_op jit(solution)/shard_map/ppermute | solution.py:173
  49.3 0.6 collective-permute-done.8.refs_10_
  49.9 0.1 copy-done.10
  50.0 0.6 copy-done.12
  50.6 7.2 %tangent.9 = f32[1024,512]{1,0:T(8,128)} custom-call(f32[16,64,512]{2,1,0:T(8,128)} %get-tuple-element.27.refs_0_, f32[4096,512]{1,0:T(8,128)} %bitcast.27, f32[4096,512]{1,0:T(8,128)} %bitcast.28, f32[4096,512]{1,0:T(8,128)} %bitcast.29, f32[4096,512]{1,0:T(8,128)} %bitcast.30, f32[4096,512]{1,0:T(8,128)} %bitcast.57, f32[4096,512]{1,0:T(8,128)} %bitcast.58, ...), custom_call_target="tpu_custom_call" | custom-call | flops 20971520 | bytes 16777216 | tf_op jit(solution)/shard_map/tangent/pallas_call | solution.py:236
  57.8 7.1 %all-to-all-start.2 = ((f32[64,16,512]{2,1,0:T(8,128)}), f32[64,16,512]{2,1,0:T(8,128)S(1)}, u32[]{:S(2)}, u32[]{:S(2)}) async-start(f32[64,16,512]{2,1,0:T(8,128)} %bitcast.107), calls=%async_computation.2 | async-start | bytes 4194304 | tf_op jit(solution)/shard_map/all_to_all | solution.py:267
  64.9 6.3 %edge.3 = (f32[3,128,512]{2,1,0:T(8,128)}, f32[3,128,512]{2,1,0:T(8,128)}) custom-call(f32[256,16,512]{2,1,0:T(8,128)} %bitcast.91, f32[256,16,512]{2,1,0:T(8,128)} %bitcast.31, f32[256,16,512]{2,1,0:T(8,128)} %bitcast.61, f32[256,16,512]{2,1,0:T(8,128)} %bitcast.92, f32[256,16,512]{2,1,0:T(8,128)} %bitcast.32, f32[256,16,512]{2,1,0:T(8,128)} %bitcast.62), custom_call_target="tpu_custom_call" | custom-call | bytes 13107200 | tf_op jit(solution)/shard_map/edge/pallas_call | solution.py:198
  71.2 3.8 collective-permute-start
  75.0 1.3 collective-permute-start.1
  76.3 35.3 %collective-permute-done.refs_12_.refs_11_ = f32[3,128,512]{2,1,0:T(8,128)S(1)} collective-permute-done((f32[3,128,512]{2,1,0:T(8,128)}, f32[3,128,512]{2,1,0:T(8,128)S(1)}, u32[]{:S(2)}, u32[]{:S(2)}) %collective-permute-start) | collective-permute-done | bytes 786464 | tf_op jit(solution)/shard_map/ppermute | solution.py:173
  111.7 5.0 collective-permute-done.1.refs_13_.refs_12_
  116.7 1.0 copy-done.1
  117.6 11.4 %tangent.6 = (f32[16,128,512]{2,1,0:T(8,128)}, f32[2,128,512]{2,1,0:T(8,128)}, f32[2,128,512]{2,1,0:T(8,128)}) custom-call(f32[4096,512]{1,0:T(8,128)} %bitcast.93, f32[4096,512]{1,0:T(8,128)} %bitcast.94, f32[4096,512]{1,0:T(8,128)} %bitcast.95, f32[4096,512]{1,0:T(8,128)} %bitcast.96, f32[4096,512]{1,0:T(8,128)} %bitcast.35, f32[4096,512]{1,0:T(8,128)} %bitcast.34, ...), custom_call_target="tpu_custom_call" | custom-call | flops 41943040 | bytes 33554432 | tf_op jit(solution)/shard_map/tangent/pallas_call | solution.py:236
  129.0 4.5 collective-permute-start.2
  133.5 1.3 collective-permute-start.3
  134.8 15.9 %collective-permute-done.2.refs_9_ = f32[2,128,512]{2,1,0:T(8,128)S(1)} collective-permute-done((f32[2,128,512]{2,1,0:T(8,128)}, f32[2,128,512]{2,1,0:T(8,128)S(1)}, u32[]{:S(2)}, u32[]{:S(2)}) %collective-permute-start.2) | collective-permute-done | bytes 524320 | tf_op jit(solution)/shard_map/ppermute | solution.py:173
  150.7 0.6 collective-permute-done.3.refs_10_
  151.3 0.2 copy-done.8
  151.5 0.6 copy-done.9
  152.1 11.0 %tangent.7 = f32[2048,512]{1,0:T(8,128)} custom-call(f32[16,128,512]{2,1,0:T(8,128)} %get-tuple-element.22.refs_0_, f32[4096,512]{1,0:T(8,128)} %bitcast.37, f32[4096,512]{1,0:T(8,128)} %bitcast.38, f32[4096,512]{1,0:T(8,128)} %bitcast.39, f32[4096,512]{1,0:T(8,128)} %bitcast.40, f32[4096,512]{1,0:T(8,128)} %bitcast.67, f32[4096,512]{1,0:T(8,128)} %bitcast.68, ...), custom_call_target="tpu_custom_call" | custom-call | flops 41943040 | bytes 33554432 | tf_op jit(solution)/shard_map/tangent/pallas_call | solution.py:236
  163.1 3.4 collective-permute-start.4
  166.4 3.8 edge.5
  170.2 3.9 collective-permute-start.9
  174.1 1.5 collective-permute-start.10
  175.6 9.0 %collective-permute-done.9.refs_12_.refs_11_ = f32[3,64,512]{2,1,0:T(8,128)S(1)} collective-permute-done((f32[3,64,512]{2,1,0:T(8,128)}, f32[3,64,512]{2,1,0:T(8,128)S(1)}, u32[]{:S(2)}, u32[]{:S(2)}) %collective-permute-start.9) | collective-permute-done | bytes 393248 | tf_op jit(solution)/shard_map/ppermute | solution.py:173
  184.6 8.5 %collective-permute-done.10.refs_13_.refs_12_ = f32[3,64,512]{2,1,0:T(8,128)S(1)} collective-permute-done((f32[3,64,512]{2,1,0:T(8,128)}, f32[3,64,512]{2,1,0:T(8,128)S(1)}, u32[]{:S(2)}, u32[]{:S(2)}) %collective-permute-start.10) | collective-permute-done | bytes 393248 | tf_op jit(solution)/shard_map/ppermute | solution.py:173
  193.1 0.7 copy-done.6
  193.8 6.9 %tangent.10 = (f32[16,64,512]{2,1,0:T(8,128)}, f32[2,64,512]{2,1,0:T(8,128)}, f32[2,64,512]{2,1,0:T(8,128)}) custom-call(f32[4096,512]{1,0:T(8,128)} %bitcast.99, f32[4096,512]{1,0:T(8,128)} %bitcast.100, f32[4096,512]{1,0:T(8,128)} %bitcast.101, f32[4096,512]{1,0:T(8,128)} %bitcast.102, f32[4096,512]{1,0:T(8,128)} %bitcast.43, f32[4096,512]{1,0:T(8,128)} %bitcast.44, ...), custom_call_target="tpu_custom_call" | custom-call | flops 20971520 | bytes 16777216 | tf_op jit(solution)/shard_map/tangent/pallas_call | solution.py:236
  200.7 1.6 collective-permute-start.11
  202.2 1.3 collective-permute-start.12
  203.5 5.7 %collective-permute-done.11.refs_9_ = f32[2,64,512]{2,1,0:T(8,128)S(1)} collective-permute-done((f32[2,64,512]{2,1,0:T(8,128)}, f32[2,64,512]{2,1,0:T(8,128)S(1)}, u32[]{:S(2)}, u32[]{:S(2)}) %collective-permute-start.11) | collective-permute-done | bytes 262176 | tf_op jit(solution)/shard_map/ppermute | solution.py:173
  209.2 5.6 %collective-permute-done.12.refs_10_ = f32[2,64,512]{2,1,0:T(8,128)S(1)} collective-permute-done((f32[2,64,512]{2,1,0:T(8,128)}, f32[2,64,512]{2,1,0:T(8,128)S(1)}, u32[]{:S(2)}, u32[]{:S(2)}) %collective-permute-start.12) | collective-permute-done | bytes 262176 | tf_op jit(solution)/shard_map/ppermute | solution.py:173
  214.8 0.7 copy-done.13
  215.5 7.2 %tangent.11 = f32[1024,512]{1,0:T(8,128)} custom-call(f32[16,64,512]{2,1,0:T(8,128)} %get-tuple-element.32.refs_0_, f32[4096,512]{1,0:T(8,128)} %bitcast.47, f32[4096,512]{1,0:T(8,128)} %bitcast.48, f32[4096,512]{1,0:T(8,128)} %bitcast.49, f32[4096,512]{1,0:T(8,128)} %bitcast.50, f32[4096,512]{1,0:T(8,128)} %bitcast.77, f32[4096,512]{1,0:T(8,128)} %bitcast.78, ...), custom_call_target="tpu_custom_call" | custom-call | flops 20971520 | bytes 16777216 | tf_op jit(solution)/shard_map/tangent/pallas_call | solution.py:236
  222.7 15.8 %all-to-all-start.3 = ((f32[64,16,512]{2,1,0:T(8,128)}), f32[64,16,512]{2,1,0:T(8,128)}, u32[]{:S(2)}, u32[]{:S(2)}) async-start(f32[64,16,512]{2,1,0:T(8,128)} %bitcast.108), calls=%async_computation.3 | async-start | bytes 4194304 | tf_op jit(solution)/shard_map/all_to_all | solution.py:267
  238.6 7.0 %bitcast_subtract_fusion = f32[128,16,512]{2,1,0:T(8,128)} fusion(f32[128,16,512]{2,1,0:T(8,128)} %collective-permute-done.4, f32[2,128,16,512]{3,2,1,0:T(8,128)} %param.5), kind=kLoop, calls=%fused_computation | loop fusion | flops 1048576 | bytes 12582912 | tf_op jit(solution)/shard_map/sub | solution.py:263
  245.5 24.8 %all-to-all-done.3 = f32[64,16,512]{2,1,0:T(8,128)} async-done(((f32[64,16,512]{2,1,0:T(8,128)}), f32[64,16,512]{2,1,0:T(8,128)}, u32[]{:S(2)}, u32[]{:S(2)}) %all-to-all-start.3) | async-done | bytes 2097184 | tf_op jit(solution)/shard_map/all_to_all | solution.py:267
  270.3 9.6 %all-to-all-start = ((f32[128,16,512]{2,1,0:T(8,128)}), f32[128,16,512]{2,1,0:T(8,128)}, u32[]{:S(2)}, u32[]{:S(2)}) async-start(f32[128,16,512]{2,1,0:T(8,128)} %bitcast_subtract_fusion), calls=%async_computation | async-start | bytes 8388608 | tf_op jit(solution)/shard_map/all_to_all | solution.py:267
  280.0 2.7 fusion.3
  282.6 8.2 %fusion.1 = (bf16[512,512]{1,0:T(8,128)(2,1)}, bf16[512,512]{1,0:T(8,128)(2,1)}, bf16[512,512]{1,0:T(8,128)(2,1)}, bf16[512,512]{1,0:T(8,128)(2,1)}) fusion(f32[512]{0:T(512)S(1)} %get-tuple-element.51, f32[512]{0:T(512)S(1)} %get-tuple-element.52), kind=kLoop, calls=%fused_computation.6 | loop fusion | flops 3670016 | bytes 2101248 | tf_op jit(solution)/shard_map/convert_element_type | solution.py:28
  290.8 10.0 %middle.4.refs_10_ = f32[16,8,16,512]{3,2,1,0:T(8,128)} custom-call(f32[16,4,16,512]{3,2,1,0:T(8,128)} %bitcast.13.block_ref, f32[256,512]{1,0:T(8,128)} %refs_1_.1, bf16[256,256]{1,0:T(8,128)(2,1)} %get-tuple-element.48.rh.refs_2_, bf16[256,256]{1,0:T(8,128)(2,1)} %get-tuple-element.46.rl.refs_3_, bf16[256,256]{1,0:T(8,128)(2,1)} %get-tuple-element.47.rth.refs_4_, ...), custom_call_target="tpu_custom_call" | custom-call | flops 4831838208 | bytes 4194304 | tf_op jit(solution)/shard_map/middle/pallas_call | solution.py:283
  300.8 10.0 %middle.5 = f32[16,8,16,512]{3,2,1,0:T(8,128)} custom-call(f32[16,4,16,512]{3,2,1,0:T(8,128)} %bitcast.110, f32[256,512]{1,0:T(8,128)} %refs_1_.1, bf16[256,256]{1,0:T(8,128)(2,1)} %get-tuple-element.48.rh.refs_2_, bf16[256,256]{1,0:T(8,128)(2,1)} %get-tuple-element.46.rl.refs_3_, ...), custom_call_target="tpu_custom_call", output_to_operand_aliasing={{}: (10, {})} | custom-call | flops 4831838208 | bytes 4194304 | tf_op jit(solution)/shard_map/middle/pallas_call | solution.py:283
  310.8 47.7 %all-to-all-done = f32[128,16,512]{2,1,0:T(8,128)} async-done(((f32[128,16,512]{2,1,0:T(8,128)}), f32[128,16,512]{2,1,0:T(8,128)}, u32[]{:S(2)}, u32[]{:S(2)}) %all-to-all-start) | async-done | bytes 4194336 | tf_op jit(solution)/shard_map/all_to_all | solution.py:267
  358.6 19.7 %all-to-all-start.4 = ((f32[16,8,16,512]{3,2,1,0:T(8,128)}), f32[16,8,16,512]{3,2,1,0:T(8,128)}, u32[]{:S(2)}, u32[]{:S(2)}) async-start(f32[16,8,16,512]{3,2,1,0:T(8,128)} %middle.5), calls=%async_computation.4 | async-start | bytes 8388608 | tf_op jit(solution)/shard_map/all_to_all | solution.py:267
  378.2 17.2 %middle.3 = f32[16,8,16,512]{3,2,1,0:T(8,128)} custom-call(f32[16,8,16,512]{3,2,1,0:T(8,128)} %bitcast.8.block_ref, f32[256,512]{1,0:T(8,128)} %refs_1_.1, bf16[256,256]{1,0:T(8,128)(2,1)} %get-tuple-element.48.rh.refs_2_, bf16[256,256]{1,0:T(8,128)(2,1)} %get-tuple-element.46.rl.refs_3_, bf16[256,256]{1,0:T(8,128)(2,1)} %get-tuple-element.47.rth.refs_4_, ...), custom_call_target="tpu_custom_call" | custom-call | flops 9663676416 | bytes 8388608 | tf_op jit(solution)/shard_map/middle/pallas_call | solution.py:283
  395.5 61.2 %all-to-all-done.4 = f32[16,8,16,512]{3,2,1,0:T(8,128)} async-done(((f32[16,8,16,512]{3,2,1,0:T(8,128)}), f32[16,8,16,512]{3,2,1,0:T(8,128)}, u32[]{:S(2)}, u32[]{:S(2)}) %all-to-all-start.4) | async-done | bytes 4194336 | tf_op jit(solution)/shard_map/all_to_all | solution.py:267
  456.7 19.5 %all-to-all-start.1 = ((f32[16,8,16,512]{3,2,1,0:T(8,128)}), f32[16,8,16,512]{3,2,1,0:T(8,128)}, u32[]{:S(2)}, u32[]{:S(2)}) async-start(f32[16,8,16,512]{3,2,1,0:T(8,128)} %middle.3), calls=%async_computation.1 | async-start | bytes 8388608 | tf_op jit(solution)/shard_map/all_to_all | solution.py:267
  476.2 0.1 fusion.7
  476.3 0.1 copy.12
  476.5 0.1 copy.10
  476.6 0.6 fusion.4
  477.2 0.6 fusion.5
  477.8 7.7 %mix.2.refs_0_ = f32[256,16,512]{2,1,0:T(8,128)} custom-call(f32[128,16,512]{2,1,0:T(8,128)} %bitcast.14.field_ref, bf16[128,128]{1,0:T(8,128)(2,1)} %get-tuple-element.36.vh_ref, bf16[128,128]{1,0:T(8,128)(2,1)} %get-tuple-element.35.vl_ref), custom_call_target="tpu_custom_call" | custom-call | flops 805306368 | bytes 8388608 | tf_op jit(solution)/shard_map/mix/pallas_call | solution.py:305
  485.6 34.0 %all-to-all-done.1 = f32[16,8,16,512]{3,2,1,0:T(8,128)} async-done(((f32[16,8,16,512]{3,2,1,0:T(8,128)}), f32[16,8,16,512]{3,2,1,0:T(8,128)}, u32[]{:S(2)}, u32[]{:S(2)}) %all-to-all-start.1) | async-done | bytes 4194336 | tf_op jit(solution)/shard_map/all_to_all | solution.py:267
  519.6 7.7 %mix.3 = f32[256,16,512]{2,1,0:T(8,128)} custom-call(f32[128,16,512]{2,1,0:T(8,128)} %bitcast.9.field_ref, bf16[128,128]{1,0:T(8,128)(2,1)} %get-tuple-element.40.vh_ref, bf16[128,128]{1,0:T(8,128)(2,1)} %get-tuple-element.39.vl_ref, f32[256,16,512]{2,1,0:T(8,128)} %mix.2.refs_0_), custom_call_target="tpu_custom_call", output_to_operand_aliasing={{}: (3, {})} | custom-call | flops 805306368 | bytes 8388608 | tf_op jit(solution)/shard_map/mix/pallas_call | solution.py:305
  (26 shorter events, 0.2 us)
Async XLA Ops:
  3.8 22.0 %collective-permute-start.5 = (f32[3,64,512]{2,1,0:T(8,128)}, f32[3,64,512]{2,1,0:T(8,128)S(1)}, u32[]{:S(2)}, u32[]{:S(2)}) collective-permute-start(f32[3,64,512]{2,1,0:T(8,128)} %get-tuple-element.25), channel_id=1, source_target_pairs={{0,1},{1,2},{2,3},{3,4},{4,5},{5,6},{6,7},{7,8},{8,9},{9,10},{10,1... | collective-permute-start | bytes 1179656 | tf_op jit(solution)/shard_map/ppermute | solution.py:173
  8.7 18.9 %collective-permute-start.6 = (f32[3,64,512]{2,1,0:T(8,128)}, f32[3,64,512]{2,1,0:T(8,128)S(1)}, u32[]{:S(2)}, u32[]{:S(2)}) collective-permute-start(f32[3,64,512]{2,1,0:T(8,128)} %get-tuple-element.26), channel_id=1, source_target_pairs={{1,0},{2,1},{3,2},{4,3},{5,4},{6,5},{7,6},{8,7},{9,8},{10,9},{11,1... | collective-permute-start | bytes 1179656 | tf_op jit(solution)/shard_map/ppermute | solution.py:173
  25.7 1.8 copy-start.3
  27.6 0.7 copy-start.5
  35.2 14.1 %collective-permute-start.7 = (f32[2,64,512]{2,1,0:T(8,128)}, f32[2,64,512]{2,1,0:T(8,128)S(1)}, u32[]{:S(2)}, u32[]{:S(2)}) collective-permute-start(f32[2,64,512]{2,1,0:T(8,128)} %get-tuple-element.28), channel_id=1, source_target_pairs={{0,1},{1,2},{2,3},{3,4},{4,5},{5,6},{6,7},{7,8},{8,9},{9,10},{10,1... | collective-permute-start | bytes 786440 | tf_op jit(solution)/shard_map/ppermute | solution.py:173
  38.6 11.3 %collective-permute-start.8 = (f32[2,64,512]{2,1,0:T(8,128)}, f32[2,64,512]{2,1,0:T(8,128)S(1)}, u32[]{:S(2)}, u32[]{:S(2)}) collective-permute-start(f32[2,64,512]{2,1,0:T(8,128)} %get-tuple-element.29), channel_id=1, source_target_pairs={{1,0},{2,1},{3,2},{4,3},{5,4},{6,5},{7,6},{8,7},{9,8},{10,9},{11,1... | collective-permute-start | bytes 786440 | tf_op jit(solution)/shard_map/ppermute | solution.py:173
  49.3 0.7 copy-start.10
  49.9 0.7 copy-start.12
  57.8 165.0 %all-to-all-start.2 = ((f32[64,16,512]{2,1,0:T(8,128)}), f32[64,16,512]{2,1,0:T(8,128)S(1)}, u32[]{:S(2)}, u32[]{:S(2)}) async-start(f32[64,16,512]{2,1,0:T(8,128)} %bitcast.107), calls=%async_computation.2 | async-start | bytes 4194304 | tf_op jit(solution)/shard_map/all_to_all | solution.py:267
  71.2 40.5 %collective-permute-start = (f32[3,128,512]{2,1,0:T(8,128)}, f32[3,128,512]{2,1,0:T(8,128)S(1)}, u32[]{:S(2)}, u32[]{:S(2)}) collective-permute-start(f32[3,128,512]{2,1,0:T(8,128)} %get-tuple-element.20), channel_id=1, source_target_pairs={{0,1},{1,2},{2,3},{3,4},{4,5},{5,6},{6,7},{7,8},{8,9},{9,10},{10,1... | collective-permute-start | bytes 2359304 | tf_op jit(solution)/shard_map/ppermute | solution.py:173
  75.0 41.6 %collective-permute-start.1 = (f32[3,128,512]{2,1,0:T(8,128)}, f32[3,128,512]{2,1,0:T(8,128)S(1)}, u32[]{:S(2)}, u32[]{:S(2)}) collective-permute-start(f32[3,128,512]{2,1,0:T(8,128)} %get-tuple-element.21), channel_id=1, source_target_pairs={{1,0},{2,1},{3,2},{4,3},{5,4},{6,5},{7,6},{8,7},{9,8},{10,9},{11,1... | collective-permute-start | bytes 2359304 | tf_op jit(solution)/shard_map/ppermute | solution.py:173
  111.7 5.0 copy-start
  116.7 1.0 copy-start.1
  129.0 21.7 %collective-permute-start.2 = (f32[2,128,512]{2,1,0:T(8,128)}, f32[2,128,512]{2,1,0:T(8,128)S(1)}, u32[]{:S(2)}, u32[]{:S(2)}) collective-permute-start(f32[2,128,512]{2,1,0:T(8,128)} %get-tuple-element.23), channel_id=1, source_target_pairs={{0,1},{1,2},{2,3},{3,4},{4,5},{5,6},{6,7},{7,8},{8,9},{9,10},{10,1... | collective-permute-start | bytes 1572872 | tf_op jit(solution)/shard_map/ppermute | solution.py:173
  133.5 17.8 %collective-permute-start.3 = (f32[2,128,512]{2,1,0:T(8,128)}, f32[2,128,512]{2,1,0:T(8,128)S(1)}, u32[]{:S(2)}, u32[]{:S(2)}) collective-permute-start(f32[2,128,512]{2,1,0:T(8,128)} %get-tuple-element.24), channel_id=1, source_target_pairs={{1,0},{2,1},{3,2},{4,3},{5,4},{6,5},{7,6},{8,7},{9,8},{10,9},{11,1... | collective-permute-start | bytes 1572872 | tf_op jit(solution)/shard_map/ppermute | solution.py:173
  150.6 0.8 copy-start.8
  151.3 0.8 copy-start.9
  163.1 75.5 %collective-permute-start.4 = (f32[128,16,512]{2,1,0:T(8,128)}, f32[128,16,512]{2,1,0:T(8,128)}, u32[]{:S(2)}, u32[]{:S(2)}) collective-permute-start(f32[128,16,512]{2,1,0:T(8,128)} %bitcast.109), channel_id=1, source_target_pairs={{0,16},{1,17},{2,18},{3,19},{4,20},{5,21},{6,22},{7,23},{8,24},{9,... | collective-permute-start | bytes 12582920 | tf_op jit(solution)/shard_map/ppermute | solution.py:176
  170.2 14.4 %collective-permute-start.9 = (f32[3,64,512]{2,1,0:T(8,128)}, f32[3,64,512]{2,1,0:T(8,128)S(1)}, u32[]{:S(2)}, u32[]{:S(2)}) collective-permute-start(f32[3,64,512]{2,1,0:T(8,128)} %get-tuple-element.30), channel_id=1, source_target_pairs={{0,1},{1,2},{2,3},{3,4},{4,5},{5,6},{6,7},{7,8},{8,9},{9,10},{10,1... | collective-permute-start | bytes 1179656 | tf_op jit(solution)/shard_map/ppermute | solution.py:173
  174.1 19.0 %collective-permute-start.10 = (f32[3,64,512]{2,1,0:T(8,128)}, f32[3,64,512]{2,1,0:T(8,128)S(1)}, u32[]{:S(2)}, u32[]{:S(2)}) collective-permute-start(f32[3,64,512]{2,1,0:T(8,128)} %get-tuple-element.31), channel_id=1, source_target_pairs={{1,0},{2,1},{3,2},{4,3},{5,4},{6,5},{7,6},{8,7},{9,8},{10,9},{11,1... | collective-permute-start | bytes 1179656 | tf_op jit(solution)/shard_map/ppermute | solution.py:173
  184.6 8.5 %copy-start.4 = (f32[3,64,512]{2,1,0:T(8,128)}, f32[3,64,512]{2,1,0:T(8,128)S(1)}, u32[]{:S(2)}) copy-start(f32[3,64,512]{2,1,0:T(8,128)S(1)} %collective-permute-done.9.refs_12_.refs_11_) | copy-start | bytes 1179652
  193.1 0.7 copy-start.6
  200.7 8.6 %collective-permute-start.11 = (f32[2,64,512]{2,1,0:T(8,128)}, f32[2,64,512]{2,1,0:T(8,128)S(1)}, u32[]{:S(2)}, u32[]{:S(2)}) collective-permute-start(f32[2,64,512]{2,1,0:T(8,128)} %get-tuple-element.33), channel_id=1, source_target_pairs={{0,1},{1,2},{2,3},{3,4},{4,5},{5,6},{6,7},{7,8},{8,9},{9,10},{10,1... | collective-permute-start | bytes 786440 | tf_op jit(solution)/shard_map/ppermute | solution.py:173
  202.2 12.6 %collective-permute-start.12 = (f32[2,64,512]{2,1,0:T(8,128)}, f32[2,64,512]{2,1,0:T(8,128)S(1)}, u32[]{:S(2)}, u32[]{:S(2)}) collective-permute-start(f32[2,64,512]{2,1,0:T(8,128)} %get-tuple-element.34), channel_id=1, source_target_pairs={{1,0},{2,1},{3,2},{4,3},{5,4},{6,5},{7,6},{8,7},{9,8},{10,9},{11,1... | collective-permute-start | bytes 786440 | tf_op jit(solution)/shard_map/ppermute | solution.py:173
  209.2 5.6 %copy-start.11 = (f32[2,64,512]{2,1,0:T(8,128)}, f32[2,64,512]{2,1,0:T(8,128)S(1)}, u32[]{:S(2)}) copy-start(f32[2,64,512]{2,1,0:T(8,128)S(1)} %collective-permute-done.11.refs_9_) | copy-start | bytes 786436
  214.8 0.7 copy-start.13
  222.7 22.8 %copy-start.2 = (f32[64,16,512]{2,1,0:T(8,128)}, f32[64,16,512]{2,1,0:T(8,128)S(1)}, u32[]{:S(2)}) copy-start(f32[64,16,512]{2,1,0:T(8,128)S(1)} %all-to-all-done.2) | copy-start | bytes 6291460
  222.7 47.6 %all-to-all-start.3 = ((f32[64,16,512]{2,1,0:T(8,128)}), f32[64,16,512]{2,1,0:T(8,128)}, u32[]{:S(2)}, u32[]{:S(2)}) async-start(f32[64,16,512]{2,1,0:T(8,128)} %bitcast.108), calls=%async_computation.3 | async-start | bytes 4194304 | tf_op jit(solution)/shard_map/all_to_all | solution.py:267
  270.3 88.2 %all-to-all-start = ((f32[128,16,512]{2,1,0:T(8,128)}), f32[128,16,512]{2,1,0:T(8,128)}, u32[]{:S(2)}, u32[]{:S(2)}) async-start(f32[128,16,512]{2,1,0:T(8,128)} %bitcast_subtract_fusion), calls=%async_computation | async-start | bytes 8388608 | tf_op jit(solution)/shard_map/all_to_all | solution.py:267
  358.6 98.1 %all-to-all-start.4 = ((f32[16,8,16,512]{3,2,1,0:T(8,128)}), f32[16,8,16,512]{3,2,1,0:T(8,128)}, u32[]{:S(2)}, u32[]{:S(2)}) async-start(f32[16,8,16,512]{3,2,1,0:T(8,128)} %middle.5), calls=%async_computation.4 | async-start | bytes 8388608 | tf_op jit(solution)/shard_map/all_to_all | solution.py:267
  395.5 80.7 %copy-start.7 = (f32[128,128]{1,0:T(8,128)S(1)}, f32[128,128]{1,0:T(8,128)}, u32[]{:S(2)}) copy-start(f32[128,128]{1,0:T(8,128)} %param.9) | copy-start | bytes 196612
  456.7 62.9 %all-to-all-start.1 = ((f32[16,8,16,512]{3,2,1,0:T(8,128)}), f32[16,8,16,512]{3,2,1,0:T(8,128)}, u32[]{:S(2)}, u32[]{:S(2)}) async-start(f32[16,8,16,512]{3,2,1,0:T(8,128)} %middle.3), calls=%async_computation.1 | async-start | bytes 8388608 | tf_op jit(solution)/shard_map/all_to_all | solution.py:267
